TPU v7x, 32 devices: a whole 2x2x4 slice. The times are simulated.
32 devices in a mesh: fsdp: 8 (over y, x, core), seq: 4 (over z).
Axes of the slice: x: 2, y: 2, z: 4, core: 2. Of those that a mesh axis runs over, the one named last changes fastest.
Arguments:
- inputs: bfloat16 [24, 320, 1024], P('fsdp', 'seq'), may hold values from -6 to 6
- lengths: int32 [24], P('fsdp'), may hold values from 256 to 320, as said below
- cotangent: bfloat16 [24, 320, 1024], P('fsdp', 'seq'), may hold values from -6 to 6
- attn_gain: bfloat16 [1024], P('fsdp'), may hold values from 0.25 to 1.75
- attn_shift: bfloat16 [1024], P('fsdp'), may hold values from -1 to 1
- qkv_weight: bfloat16 [1024, 3072], P('fsdp'), may hold values from -0.1875 to 0.1875
- qv_bias: bfloat16 [2048], P('fsdp'), may hold values from -0.5 to 0.5
- proj_weight: bfloat16 [1024, 1024], P('fsdp'), may hold values from -1.5 to 1.5
- proj_bias: bfloat16 [1024], P('fsdp'), may hold values from -1 to 1
- mlp_gain: bfloat16 [1024], P('fsdp'), may hold values from 0.25 to 1.75
- mlp_shift: bfloat16 [1024], P('fsdp'), may hold values from -1 to 1
- up_weight: bfloat16 [1024, 4096], P('fsdp'), may hold values from -0.1875 to 0.1875
- up_bias: bfloat16 [4096], P('fsdp'), may hold values from -1 to 1
- down_weight: bfloat16 [4096, 1024], P('fsdp'), may hold values from -0.09375 to 0.09375
- down_bias: bfloat16 [1024], P('fsdp'), may hold values from -1 to 1
Outputs:
- output: bfloat16 [24, 320, 1024], P('fsdp', 'seq')
- input_grad: bfloat16 [24, 320, 1024], P('fsdp', 'seq')
- attn_gain_grad: float32 [1024], P('fsdp')
- attn_shift_grad: float32 [1024], P('fsdp')
- query_key_value_weight_gradient: float32 [1024, 3072], P('fsdp')
- qv_bias_grad: float32 [2048], P('fsdp')
- proj_weight_grad: float32 [1024, 1024], P('fsdp')
- proj_bias_grad: float32 [1024], P('fsdp')
- mlp_gain_grad: float32 [1024], P('fsdp')
- mlp_shift_grad: float32 [1024], P('fsdp')
- up_weight_grad: float32 [1024, 4096], P('fsdp')
- up_bias_grad: float32 [4096], P('fsdp')
- down_weight_grad: float32 [4096, 1024], P('fsdp')
- down_bias_grad: float32 [1024], P('fsdp')
Inputs may be any that keep to these rules, and one draw needn't show every extreme that they name: `lengths`: valid slots of each sequence; slots at or past it are padding; some sequence is full and some has the fewest.
All inputs are finite; a program needn't handle non-finite values.
Results may differ from a plain program's by a relative error of at most 0.015.
Values may be sent and summed in bfloat16 or wider, within the bound.
No kernel may reach another device: no remote copies, remote signals or barrier semaphores. Data moves between devices by JAX's collectives and lax.ppermute only.
A program may use at most 192 MiB of HBM per device.

v0:
```python
import functools
import math

import jax
import jax.numpy as jnp
from jax import lax
from jax.experimental import pallas as pl
from jax.experimental.pallas import tpu as pltpu
from jax.sharding import PartitionSpec as P

HEAD = 64
EPSILON = 1e-06
MASKED = -1e30
TEAM = 8
ZS = 4
F32 = jnp.float32
BF16 = jnp.bfloat16
VMEM_BYTES = 56 * 1024 * 1024
SCALE = 1024


def params():
    return pltpu.CompilerParams(vmem_limit_bytes=VMEM_BYTES)


def cost(flops, nbytes, trans=0):
    return pl.CostEstimate(flops=int(flops) // SCALE, bytes_accessed=int(nbytes) // SCALE, transcendentals=int(trans) // SCALE)


def shape_of(dims, dtype):
    return jax.ShapeDtypeStruct(dims, dtype)


def mm(left, right):
    return lax.dot_general(left, right, (((1,), (0,)), ((), ())), preferred_element_type=F32)


def mm_rt(left, right):
    return lax.dot_general(left, right, (((1,), (1,)), ((), ())), preferred_element_type=F32)


def mm_lt(left, right):
    return lax.dot_general(left, right, (((0,), (0,)), ((), ())), preferred_element_type=F32)


def normalize(rows):
    center = rows - jnp.mean(rows, axis=-1, keepdims=True)
    inverse = lax.rsqrt(jnp.mean(center * center, axis=-1, keepdims=True) + EPSILON)
    return center * inverse, inverse


def norm_back(upstream, unit, inverse, gain):
    scaled = upstream * gain
    return inverse * (
        scaled
        - jnp.mean(scaled, axis=-1, keepdims=True)
        - unit * jnp.mean(scaled * unit, axis=-1, keepdims=True)
    )


def swap(value, mask):
    size = lax.axis_size("fsdp")
    return lax.ppermute(value, "fsdp", [(i, i ^ mask) for i in range(size)])


def cross(value, mask):
    return lax.ppermute(value, "seq", [(i, i ^ mask) for i in range(ZS)])


def joined(first, second):
    return (first.astype(F32) + second.astype(F32)).astype(BF16)


def after(value, *others):
    return lax.optimization_barrier((value,) + others)[0]


def pick(stack, index, axis=0):
    starts = [jnp.uint32(0)] * stack.ndim
    starts[axis] = index.astype(jnp.uint32)
    sizes = list(stack.shape)
    sizes[axis] = 1
    return lax.dynamic_slice(stack, starts, sizes).reshape(stack.shape[:axis] + stack.shape[axis + 1 :])


def outer_groups(size):
    outer = size // TEAM
    return [[o * TEAM + t for o in range(outer)] for t in range(TEAM)]


def rows_over_outer(value, size):
    if size == TEAM:
        return value
    return lax.psum_scatter(
        value, "fsdp", scatter_dimension=0, axis_index_groups=outer_groups(size), tiled=True
    )


def gather_over_outer(value, size):
    if size == TEAM:
        return value
    return lax.all_gather(value, "fsdp", axis=0, axis_index_groups=outer_groups(size), tiled=True)


def block(*dims):
    return pl.BlockSpec(dims, lambda *i: (0,) * len(dims))


def chosen(values, index):
    out = values[-1]
    for i in range(len(values) - 1):
        out = jnp.where(index == i, values[i], out)
    return out


def head_probs(queries, keys, valid):
    scores = mm_rt(queries, keys) * HEAD ** (-0.5)
    scores = jnp.where(valid, scores, MASKED)
    exponent = jnp.exp(scores - jnp.max(scores, axis=-1, keepdims=True))
    return exponent * (1.0 / jnp.sum(exponent, axis=-1, keepdims=True))


def attend_kernel(meta, rows_ref, wq, wk, wv, vecs, bias, qkv_ref, normed_ref, c0, c1, c2, c3):
    local = rows_ref.shape[2]
    slots = ZS * local
    model = rows_ref.shape[3]
    width = wq.shape[2]
    length = meta[pl.program_id(0)]
    z = meta[meta.shape[0] - 1]
    unit, _ = normalize(rows_ref[:, 0].reshape(slots, model).astype(F32))
    normed = (unit * vecs[0:1] + vecs[1:2]).astype(BF16)
    normed_ref[0] = normed
    parts = []
    for i, w in enumerate((wq, wk, wv)):
        part = (mm(normed, w[...].reshape(model, width)) + bias[:, i * width : (i + 1) * width]).astype(BF16)
        qkv_ref[0, :, i * width : (i + 1) * width] = part
        parts.append(part)
    valid = lax.broadcasted_iota(jnp.int32, (1, slots), 1) < length
    first = lax.broadcasted_iota(jnp.int32, (1, 2 * HEAD), 1) < HEAD
    for pair in range(width // (2 * HEAD)):
        lanes = slice(pair * 2 * HEAD, (pair + 1) * 2 * HEAD)
        queries, keys, values = (part[:, lanes] for part in parts)
        outs = []
        for mine in (first, ~first):
            probs = head_probs(jnp.where(mine, queries, jnp.zeros_like(queries)), keys, valid)
            outs.append(mm(probs.astype(BF16), values))
        context = jnp.where(first, outs[0], outs[1])
        pieces = [context[k * local : (k + 1) * local] for k in range(ZS)]
        for k, out in enumerate((c0, c1, c2, c3)):
            out[:, lanes] = chosen(pieces, z ^ k).astype(BF16)


def weight_specs(weights, own_rows, width):
    return [
        pl.BlockSpec((weights.shape[0], own_rows, width), functools.partial(lambda i, s, m: (0, 0, i), i))
        for i in range(3)
    ]


def attend(meta, rows, weights, vecs, bias):
    _, count, local, model = rows.shape
    slots, width = ZS * local, model // ZS
    flops = count * (2 * slots * model * 3 * width + 8 * slots * slots * width)
    per_sequence = lambda *dims: pl.BlockSpec((1,) + dims, lambda s, m: (s, 0, 0))
    return pl.pallas_call(
        attend_kernel,
        name="attend",
        grid_spec=pltpu.PrefetchScalarGridSpec(
            num_scalar_prefetch=1,
            grid=(count,),
            in_specs=[pl.BlockSpec((ZS, 1, local, model), lambda s, m: (0, s, 0, 0))]
            + weight_specs(weights, model // weights.shape[0], width)
            + [block(*vecs.shape), block(1, 3 * width)],
            out_specs=[per_sequence(slots, 3 * width), per_sequence(slots, model)]
            + [pl.BlockSpec((local, width), lambda s, m: (s, 0))] * ZS,
        ),
        out_shape=[shape_of((count, slots, 3 * width), BF16), shape_of((count, slots, model), BF16)]
        + [shape_of((count * local, width), BF16)] * ZS,
        compiler_params=params(),
        cost_estimate=cost(flops, 2 * count * slots * (2 * model + 4 * width) + 6 * model * width),
    )(meta, rows, weights, weights, weights, vecs, bias)


def attend_back_kernel(meta, rows_ref, d0, d1, d2, d3, qkv_ref, wq, wk, wv, *refs):
    dqkv_ref, keep_ref, give_ref, sums_ref = refs
    local = rows_ref.shape[2]
    slots = ZS * local
    model = rows_ref.shape[3]
    width = wq.shape[2]
    length = meta[pl.program_id(0)]
    z = meta[meta.shape[0] - 1]
    given = [d[...] for d in (d0, d1, d2, d3)]
    upstream = jnp.concatenate([chosen(given, z ^ k) for k in range(ZS)], axis=0)
    valid = lax.broadcasted_iota(jnp.int32, (1, slots), 1) < length
    first = lax.broadcasted_iota(jnp.int32, (1, 2 * HEAD), 1) < HEAD
    for pair in range(width // (2 * HEAD)):
        spans = [slice(i * width + pair * 2 * HEAD, i * width + (pair + 1) * 2 * HEAD) for i in range(3)]
        queries, keys, values = (qkv_ref[0, :, span] for span in spans)
        above = upstream[:, spans[0]]
        grads = []
        for mine in (first, ~first):
            probs = head_probs(jnp.where(mine, queries, jnp.zeros_like(queries)), keys, valid)
            probs_grad = mm_rt(jnp.where(mine, above, jnp.zeros_like(above)), values)
            inner = jnp.sum(probs * probs_grad, axis=-1, keepdims=True)
            scores_grad = (probs * (probs_grad - inner) * HEAD ** (-0.5)).astype(BF16)
            grads.append(
                (mm(scores_grad, keys), mm_lt(scores_grad, queries), mm_lt(probs.astype(BF16), above))
            )
        for span, low, high in zip(spans, *grads):
            dqkv_ref[0, :, span] = jnp.where(first, low, high).astype(BF16)
    grad = dqkv_ref[0]
    total = mm_rt(grad[:, :width], wq[...].reshape(model, width))
    total = total + mm_rt(grad[:, width : 2 * width], wk[...].reshape(model, width))
    total = total + mm_rt(grad[:, 2 * width :], wv[...].reshape(model, width))
    pieces = [total[k * local : (k + 1) * local] for k in range(ZS)]
    for k in range(ZS):
        (keep_ref, give_ref)[k % 2][k // 2] = chosen(pieces, z ^ k).astype(BF16)
    unit, _ = normalize(rows_ref[:, 0].reshape(slots, model).astype(F32))

    @pl.when(pl.program_id(0) == 0)
    def _():
        sums_ref[...] = jnp.zeros_like(sums_ref)

    sums_ref[0:1, :] += jnp.sum(total * unit, axis=0, keepdims=True)
    sums_ref[1:2, :] += jnp.sum(total, axis=0, keepdims=True)
    sums_ref[2:3, : 3 * width] += jnp.sum(grad.astype(F32), axis=0, keepdims=True)


def attend_back(meta, rows, upstream, qkv, weights):
    _, count, local, model = rows.shape
    slots, width = ZS * local, model // ZS
    packed = pl.BlockSpec((1, slots, 3 * width), lambda s, m: (s, 0, 0))
    split = pl.BlockSpec((2, local, model), lambda s, m: (0, s, 0))
    flops = count * (2 * slots * model * 3 * width + 20 * slots * slots * width)
    return pl.pallas_call(
        attend_back_kernel,
        name="attend_back",
        grid_spec=pltpu.PrefetchScalarGridSpec(
            num_scalar_prefetch=1,
            grid=(count,),
            in_specs=[pl.BlockSpec((ZS, 1, local, model), lambda s, m: (0, s, 0, 0))]
            + [pl.BlockSpec((local, width), lambda s, m: (s, 0))] * ZS
            + [packed]
            + weight_specs(weights, model // weights.shape[0], width),
            out_specs=[packed, split, split, block(8, model)],
        ),
        out_shape=[shape_of((count, slots, 3 * width), BF16)]
        + [shape_of((2, count * local, model), BF16)] * 2
        + [shape_of((8, model), F32)],
        compiler_params=params(),
        cost_estimate=cost(flops, 2 * count * slots * (2 * model + 7 * width) + 6 * model * width),
    )(meta, rows, *upstream, qkv, weights, weights, weights)


def project_kernel(meta, c0, c1, c2, c3, x, weights, vecs, hidden_ref, normed_ref):
    width = c0.shape[1]
    z = meta[meta.shape[0] - 1]
    hidden = x[...].astype(F32) + vecs[2:3]
    for k, part in enumerate((c0, c1, c2, c3)):
        start = pl.multiple_of((z ^ k) * width, width)
        hidden = hidden + mm(part[...], weights[pl.ds(start, width), :])
    hidden_ref[...] = hidden
    unit, _ = normalize(hidden)
    normed_ref[...] = (unit * vecs[3:4] + vecs[4:5]).astype(BF16)


def project(meta, parts, x, weights, vecs):
    rows, model = x.shape
    return pl.pallas_call(
        project_kernel,
        name="project",
        grid_spec=pltpu.PrefetchScalarGridSpec(
            num_scalar_prefetch=1,
            grid=(1,),
            in_specs=[block(*part.shape) for part in parts]
            + [block(rows, model), block(model, model), block(*vecs.shape)],
            out_specs=[block(rows, model)] * 2,
        ),
        out_shape=[shape_of((rows, model), F32), shape_of((rows, model), BF16)],
        compiler_params=params(),
        cost_estimate=cost(2 * rows * model * model, rows * model * 10 + 2 * model * model),
    )(meta, *parts, x, weights, vecs)


def feed_kernel(normed, above, up, bias, act_ref, grad_ref, back_ref):
    value = mm(normed[0], up[...]) + bias[...]
    square = value * value
    root = math.sqrt(2.0 / math.pi)
    bend = jnp.tanh(root * value * (1.0 + 0.044715 * square))
    act_ref[0] = (0.5 * value * (1.0 + bend)).astype(BF16)
    slope = 0.5 * (1.0 + bend) + 0.5 * value * (1.0 - bend * bend) * root * (1.0 + 3 * 0.044715 * square)
    grad = (above[0] * slope).astype(BF16)
    grad_ref[0] = grad
    back_ref[0] = mm_rt(grad, up[...]).astype(BF16)


def feed(normed, above, up, bias):
    count, rows, model = normed.shape
    width = up.shape[1]
    wide = pl.BlockSpec((1, rows, model), lambda i: (i, 0, 0))
    thin = pl.BlockSpec((1, rows, width), lambda i: (i, 0, 0))
    return pl.pallas_call(
        feed_kernel,
        name="feed",
        grid=(count,),
        in_specs=[wide, thin, block(model, width), block(1, width)],
        out_specs=[thin, thin, wide],
        out_shape=[shape_of((count, rows, width), BF16)] * 2 + [shape_of((count, rows, model), BF16)],
        compiler_params=params(),
        cost_estimate=cost(
            count * rows * 4 * model * width,
            count * rows * (4 * model + 8 * width) + 2 * model * width,
            count * rows * width,
        ),
    )(normed, above, up, bias)


def feed_grads_kernel(
    act_e, act_o, grad_e, grad_o, normed_e, normed_o, cot_e, cot_o, down, out_e, out_o, down_ref, up_ref, down_sum, up_sum, bias_sum
):
    rows = act_e.shape[1]
    width = down.shape[0]
    act = jnp.concatenate([act_e[0], act_o[0]], axis=0)
    grad = jnp.concatenate([grad_e[0], grad_o[0]], axis=0)
    out = mm(act, down[...]).astype(BF16)
    out_e[0] = out[:rows]
    out_o[0] = out[rows:]

    @pl.when(pl.program_id(0) == 0)
    def _():
        down_sum[...] = jnp.zeros_like(down_sum)
        up_sum[...] = jnp.zeros_like(up_sum)
        bias_sum[...] = jnp.zeros_like(bias_sum)

    down_sum[...] += mm_lt(act, jnp.concatenate([cot_e[0], cot_o[0]], axis=0))
    up_sum[...] += mm_lt(jnp.concatenate([normed_e[0], normed_o[0]], axis=0), grad)
    bias_sum[0:1, :width] += jnp.sum(grad.astype(F32), axis=0, keepdims=True)

    @pl.when(pl.program_id(0) == pl.num_programs(0) - 1)
    def _():
        down_ref[:width] = down_sum[...].astype(BF16)
        down_ref[width:] = bias_sum[...].astype(BF16)
        up_ref[...] = up_sum[...].astype(BF16)


def feed_grads(act, grad, normed, cot, down):
    _, rows, width = act[0].shape
    model = down.shape[1]
    thin = pl.BlockSpec((1, rows, width), lambda i: (i, 0, 0))
    wide = pl.BlockSpec((1, rows, model), lambda i: (i, 0, 0))
    total = 8 * rows
    return pl.pallas_call(
        feed_grads_kernel,
        name="feed_grads",
        grid=(4,),
        in_specs=[thin] * 4 + [wide] * 4 + [block(width, model)],
        out_specs=[wide, wide, block(width + 16, model), block(model, width)],
        scratch_shapes=[
            pltpu.VMEM((width, model), F32),
            pltpu.VMEM((model, width), F32),
            pltpu.VMEM((16, model), F32),
        ],
        out_shape=[
            shape_of((4, rows, model), BF16),
            shape_of((4, rows, model), BF16),
            shape_of((width + 16, model), BF16),
            shape_of((model, width), BF16),
        ],
        compiler_params=params(),
        cost_estimate=cost(6 * total * model * width, 2 * total * (3 * model + 2 * width) + 6 * model * width),
    )(*act, *grad, *normed, *cot, down)


def middle_kernel(meta, g0, g1, gx, gy, gd, hidden, cot, weights, vecs, hidden_grad_ref, grad_ref, sums_ref, d0, d1, d2, d3):
    width = d0.shape[1]
    z = meta[meta.shape[0] - 1]
    normed_grad = (g0[0].astype(F32) + g1[0].astype(F32)) + (gx[...].astype(F32) + gy[...].astype(F32))
    normed_grad = normed_grad + gd[...].astype(F32)
    unit, inverse = normalize(hidden[...])
    upstream = cot[...].astype(F32)
    hidden_grad = upstream + norm_back(normed_grad, unit, inverse, vecs[3:4])
    hidden_grad_ref[...] = hidden_grad
    grad = hidden_grad.astype(BF16)
    grad_ref[...] = grad
    for k, out in enumerate((d0, d1, d2, d3)):
        start = pl.multiple_of((z ^ k) * width, width)
        out[...] = mm_rt(grad, weights[pl.ds(start, width), :]).astype(BF16)
    sums_ref[0:1, :] = jnp.sum(normed_grad * unit, axis=0, keepdims=True)
    sums_ref[1:2, :] = jnp.sum(normed_grad, axis=0, keepdims=True)
    sums_ref[2:3, :] = jnp.sum(grad.astype(F32), axis=0, keepdims=True)
    sums_ref[3:4, :] = jnp.sum(upstream, axis=0, keepdims=True)


def middle(meta, stacks, moved, hidden, cot, weights, vecs):
    rows, model = hidden.shape
    width = model // ZS
    return pl.pallas_call(
        middle_kernel,
        name="middle",
        grid_spec=pltpu.PrefetchScalarGridSpec(
            num_scalar_prefetch=1,
            grid=(1,),
            in_specs=[block(1, rows, model)] * 2
            + [block(rows, model)] * 5
            + [block(model, model), block(*vecs.shape)],
            out_specs=[block(rows, model)] * 2 + [block(4, model)] + [block(rows, width)] * ZS,
        ),
        out_shape=[shape_of((rows, model), F32), shape_of((rows, model), BF16), shape_of((4, model), F32)]
        + [shape_of((rows, width), BF16)] * ZS,
        compiler_params=params(),
        cost_estimate=cost(2 * rows * model * model, rows * model * 26 + 2 * model * model),
    )(meta, *stacks, *moved, hidden, cot, weights, vecs)


def finish_kernel(x, mine, near, far, hidden_grad, vecs, out):
    unit, inverse = normalize(x[...].astype(F32))
    upstream = mine[0].astype(F32) + near[...].astype(F32) + far[...].astype(F32)
    out[...] = (hidden_grad[...] + norm_back(upstream, unit, inverse, vecs[0:1])).astype(BF16)


def finish(x, mine, near, far, hidden_grad, vecs):
    rows, model = x.shape
    steps = 3 if rows % 48 == 0 else 1
    part = pl.BlockSpec((rows // steps, model), lambda i: (i, 0))
    stack = pl.BlockSpec((1, rows // steps, model), lambda i: (0, i, 0))
    return pl.pallas_call(
        finish_kernel,
        name="finish",
        grid=(steps,),
        in_specs=[part, stack, part, part, part, block(*vecs.shape)],
        out_specs=part,
        out_shape=shape_of((rows, model), BF16),
        compiler_params=params(),
        cost_estimate=cost(20 * rows * model, rows * model * 12),
    )(x, mine, near, far, hidden_grad, vecs)


def per_device(
    inputs,
    lengths,
    cotangent,
    attn_gain,
    attn_shift,
    qkv_weight,
    qv_bias,
    proj_weight,
    proj_bias,
    mlp_gain,
    mlp_shift,
    up_weight,
    up_bias,
    down_weight,
    down_bias,
):
    count, local, model = inputs.shape
    size = lax.axis_size("fsdp")
    outer = size // TEAM
    place = lax.axis_index("fsdp").astype(jnp.uint32)
    seat = lax.axis_index("seq").astype(jnp.uint32)
    z = seat.astype(jnp.int32)
    team = place & (TEAM - 1)
    core = team & 1
    chip = team >> 1
    tokens = count * local
    width = model // ZS
    own_rows = qkv_weight.shape[0]
    hidden_units = up_weight.shape[1]
    feed_width = hidden_units // TEAM
    meta = jnp.concatenate([lengths.astype(jnp.int32), z.reshape(1)])

    rows = lax.all_gather(inputs, "seq", axis=0, tiled=False)

    def over_team(own):
        quad = jnp.stack([own] + [swap(own, 2 * m) for m in (1, 2, 3)])
        return jnp.concatenate([quad, swap(quad, 1)], axis=0)

    columns = [
        lax.dynamic_slice(qkv_weight, (jnp.uint32(0), seat * width + i * model), (own_rows, width)) for i in range(3)
    ]
    vectors = (attn_gain, attn_shift, proj_bias, mlp_gain, mlp_shift, down_bias)
    lanes, spot, packed = 3 * width, 0, []
    for vector in vectors:
        packed.append(jnp.pad(vector, (spot, lanes - spot - vector.shape[0])))
        spot += vector.shape[0]
    row_one = functools.reduce(jnp.add, packed).reshape(1, lanes)
    row_two = jnp.pad(qv_bias, (0, lanes - qv_bias.shape[0])).reshape(1, lanes)
    small_rows = jnp.pad(row_one, ((0, 7), (0, 0))) + jnp.pad(row_two, ((1, 6), (0, 0)))
    piece = jnp.concatenate([jnp.concatenate(columns, axis=1), small_rows], axis=0)
    pieces = over_team(piece)
    weights = jnp.stack([pick(pieces, ((j ^ team) & 1) * 4 + ((j ^ team) >> 1)) for j in range(TEAM)])
    weights = gather_over_outer(weights, size)
    vecs = weights[:, own_rows, : 6 * own_rows].reshape(size, 6, own_rows).transpose(1, 0, 2)
    vecs = vecs.reshape(6, model).astype(F32)
    bias_qv = weights[:, own_rows + 1, : qv_bias.shape[0]].reshape(1, 2 * model).astype(F32)
    bias_quarter = jnp.concatenate(
        [
            lax.dynamic_slice(bias_qv, (jnp.uint32(0), seat * width), (1, width)),
            jnp.zeros((1, width), F32),
            lax.dynamic_slice(bias_qv, (jnp.uint32(0), model + seat * width), (1, width)),
        ],
        axis=1,
    )
    proj = lax.all_gather(proj_weight, "fsdp", axis=0, tiled=True)

    up_blocks = up_weight.reshape(own_rows, outer, TEAM, feed_width // outer).transpose(2, 0, 1, 3)
    up_blocks = up_blocks.reshape(TEAM, own_rows, feed_width)
    groups = [[o * TEAM + t for t in range(TEAM)] for o in range(outer)]
    up = lax.all_to_all(
        up_blocks, "fsdp", split_axis=0, concat_axis=0, axis_index_groups=groups, tiled=True
    ).reshape(TEAM * own_rows, feed_width)
    up = gather_over_outer(up, size)
    down = gather_over_outer(down_weight, size)
    bias_up = gather_over_outer(up_bias, size).astype(F32).reshape(1, feed_width)

    half = model // 2

    def over_chips(own):
        by_x, by_y = swap(own, 2), swap(own, 4)
        diagonal = jnp.concatenate([swap(by_x[:, :half], 4), swap(by_y[:, half:], 2)], axis=1)
        return jnp.stack([own, by_x, by_y, diagonal])

    positions = z * local + jnp.arange(local, dtype=jnp.int32)
    row_valid = (positions[None, :] < lengths[:, None])[:, :, None]
    cot = jnp.where(row_valid, cotangent, jnp.zeros_like(cotangent)).reshape(tokens, model)
    cot_even = over_chips(cot)
    cot_odd = swap(cot_even, 1)

    def down_back(stack):
        out = lax.dot_general(stack, down, (((2,), (1,)), ((), ())), preferred_element_type=F32)
        return out

    above_even, above_odd = down_back(cot_even), down_back(cot_odd)

    qkv, normed_attn, *context = attend(meta, after(rows, above_even, above_odd, up), weights, vecs, bias_quarter)
    context = [context[0]] + [cross(context[k], k) for k in range(1, ZS)]
    own = inputs.reshape(tokens, model)
    hidden, normed = project(meta, context, own, proj, vecs)

    normed_even = over_chips(normed)
    normed_odd = swap(normed_even, 1)
    act_even, grad_even, back_even = feed(normed_even, above_even, up, bias_up)
    act_odd, grad_odd, back_odd = feed(normed_odd, above_odd, up, bias_up)
    back_core = swap(back_odd, 1)
    sums = [joined(back_even[m], back_core[m]) for m in (1, 2, 3)]
    moved = [swap(part, 2 * m) for m, part in zip((1, 2, 3), sums)]
    act_even = after(act_even, *sums)
    out_even, out_odd, down_part, up_part = feed_grads(
        (act_even, act_odd), (grad_even, grad_odd), (normed_even, normed_odd), (cot_even, cot_odd), down
    )
    if outer > 1:
        bias_part = rows_over_outer(down_part[feed_width, :feed_width].astype(F32), size)
        bias_part = jnp.pad(bias_part.reshape(1, -1), ((0, 15), (0, model - bias_part.shape[0])))
        down_part = rows_over_outer(down_part[:feed_width], size)
        down_part = jnp.concatenate([down_part, bias_part.astype(BF16)], axis=0)
    down_rows = down_weight.shape[0]
    up_part = rows_over_outer(up_part, size)
    down_total = lax.psum(down_part, "seq")
    side = seat & 1
    half_width = feed_width // 2
    up_keep, up_give = (
        lax.dynamic_slice(up_part, (jnp.uint32(0), part * half_width), (up_part.shape[0], half_width))
        for part in (side, 1 - side)
    )

    hidden_grad, attn_grad, mid_sums, *context_grad = middle(
        meta, (back_even, back_core), moved, after(hidden, out_even), cot, proj, vecs
    )

    def over_core(part, *others):
        keep, give = pick(part, core, 1), pick(part, 1 - core, 1)
        return joined(after(keep, *others), swap(give, 1))

    def over_team_chips(both, at, *others):
        total = after(pick(both, at(0)), *others).astype(F32)
        for m in (1, 2, 3):
            total = total + swap(pick(both, at(m)), 2 * m).astype(F32)
        return total.astype(BF16)

    proj_part = mm_lt(jnp.concatenate(context, axis=1), attn_grad)
    if outer == 1:
        proj_part = proj_part.astype(BF16).reshape(ZS, 2, own_rows, model)
        mid_rows = mid_sums.reshape(4, TEAM, own_rows).transpose(1, 0, 2).reshape(4, 2, 1, 4 * own_rows)
        mid_rows = jnp.pad(mid_rows, ((0, 0), (0, 0), (0, 7), (0, model - 4 * own_rows))).astype(BF16)
        mid_rows = jnp.stack([pick(mid_rows, seat ^ k) for k in range(ZS)])
        proj_part = jnp.concatenate([proj_part, mid_rows], axis=2)
        chip_at = lambda m: chip ^ m ^ seat
    else:
        proj_part = proj_part.reshape(ZS, width, model)
        proj_part = jnp.stack([pick(proj_part, seat ^ j) for j in range(ZS)]).reshape(model, model)
        proj_part = rows_over_outer(proj_part, size).astype(BF16).reshape(4, 2, own_rows, model)
        chip_at = lambda m: chip ^ m

    context_grad = [context_grad[0]] + [cross(context_grad[k], k) for k in range(1, ZS)]
    up_half = joined(after(up_keep, *context_grad), cross(up_give, 1))
    up_across = cross(up_half, 2)
    qkv_grad, mine, give, attn_sums = attend_back(meta, rows, context_grad, after(qkv, up_half), weights)

    qkv_part = mm_lt(normed_attn.reshape(-1, model), qkv_grad.reshape(-1, 3 * width)).astype(BF16)

    if outer == 1:
        qkv_part = qkv_part.reshape(4, 2, own_rows, 3 * width)
        gains = attn_sums[:2].reshape(2, TEAM, own_rows).transpose(1, 0, 2).reshape(4, 2, 1, 2 * own_rows)
        biases = jnp.concatenate([attn_sums[2, :width], attn_sums[2, 2 * width : 3 * width]])
        biases = jnp.broadcast_to(biases, (4, 2, 1, 2 * width))
        packed = jnp.concatenate([gains, biases], axis=3)
        packed = jnp.pad(packed, ((0, 0), (0, 0), (0, 7), (0, 3 * width - packed.shape[3]))).astype(BF16)
        qkv_part = jnp.concatenate([qkv_part, packed], axis=2)
    else:
        qkv_part = rows_over_outer(qkv_part, size).reshape(4, 2, own_rows, 3 * width)

    near = [cross(give[k], 1) for k in range(2)]
    qkv_both = over_core(qkv_part)
    proj_both = over_core(proj_part, qkv_both)
    middle_sum = joined(after(mine[1], proj_both), near[1])
    far = cross(middle_sum, 2)
    up_sum = lax.optimization_barrier(joined(after(up_half, middle_sum), up_across))
    up_sum = up_sum.reshape(4, 2, own_rows, half_width)
    qkv_mine = lax.optimization_barrier(over_team_chips(qkv_both, lambda m: chip ^ m, up_sum))
    pair = jnp.stack([after(pick(up_sum, core, 1), qkv_mine), swap(pick(up_sum, 1 - core, 1), 1)], axis=1)
    proj_mine = over_team_chips(proj_both, chip_at, pair)
    lanes = qkv_mine.shape[1]
    packed = jnp.concatenate([qkv_mine, proj_mine], axis=1)
    packed_two = cross(packed, 2)
    up_rel = [after(pick(pair, chip), packed)] + [swap(pick(pair, chip ^ m), 2 * m) for m in (1, 2, 3)]
    up_rel = lax.optimization_barrier(jnp.stack(up_rel).reshape(TEAM, own_rows, half_width))
    up_other = cross(up_rel, 1)
    out_core = swap(after(out_odd, give), 1)
    out_sums = [joined(after(out_even[m], up_rel), out_core[m]) for m in (1, 2, 3)]
    out_moved = [swap(part, 2 * m) for m, part in zip((1, 2, 3), out_sums)]
    down_grad = after(down_total, qkv_both)[:down_rows].astype(F32)
    input_grad = finish(own, mine, near[0], far, after(hidden_grad, *out_sums), vecs)
    qkv_two = after(packed_two, input_grad)[:, :lanes]
    proj_two = lax.optimization_barrier(joined(proj_mine, packed_two[:, lanes:]))
    packed_one = cross(jnp.concatenate([qkv_mine, qkv_two, proj_two], axis=1), 1)
    qkv_near = [packed_one[:, :lanes], packed_one[:, lanes : 2 * lanes]]
    proj_total = joined(proj_two, packed_one[:, 2 * lanes :]).astype(F32)
    input_grad = input_grad.reshape(inputs.shape)

    output = after(hidden, qkv_two) + vecs[5:6] + out_even[0].astype(F32) + out_core[0].astype(F32)
    for part in out_moved:
        output = output + part.astype(F32)
    output = jnp.where(row_valid, output.reshape(inputs.shape), 0.0).astype(BF16)

    up_bias_grad = down_total[down_rows, : up_bias.shape[0]].astype(F32)
    up_first = jnp.where(side == 0, up_rel, up_other)
    up_second = jnp.where(side == 0, up_other, up_rel)
    up_rel = jnp.concatenate([up_first, up_second], axis=2)
    up_grad = jnp.stack([pick(up_rel, j ^ team) for j in range(TEAM)], axis=1).astype(F32)
    up_grad = up_grad.reshape(own_rows, TEAM, outer, feed_width // outer).transpose(0, 2, 1, 3)
    up_grad = up_grad.reshape(own_rows, hidden_units)
    proj_grad = proj_total[:own_rows]
    qkv_parts = jnp.stack([qkv_mine, qkv_near[0], qkv_two, qkv_near[1]])
    ordered = [pick(qkv_parts, seat ^ j).astype(F32) for j in range(ZS)]
    qkv_weight_grad = jnp.concatenate(
        [part[:own_rows, i * width : (i + 1) * width] for i in range(3) for part in ordered], axis=1
    )

    if outer == 1:
        mid = proj_total[own_rows, : 4 * own_rows].reshape(4, own_rows)
        packed = jnp.stack([part[own_rows] for part in ordered])
        gains = packed[:, : 2 * own_rows]
        gains = (gains[0] + gains[1]) + (gains[2] + gains[3])
        attn_gain_grad, attn_shift_grad = gains[:own_rows], gains[own_rows:]
        mine = pick(packed, place & (ZS - 1))
        start = 2 * own_rows + (place >> 2) * width
        qv_bias_grad = lax.dynamic_slice(mine, (start,), (width,))
        mlp_gain_grad, mlp_shift_grad, proj_bias_grad, down_bias_grad = mid
    else:
        biases = jnp.zeros((2, ZS, width), F32)
        biases = lax.dynamic_update_slice(
            biases, jnp.stack([attn_sums[2, :width], attn_sums[2, 2 * width : 3 * width]])[:, None], (0, z, 0)
        )
        packed = jnp.concatenate([attn_sums[0], attn_sums[1], mid_sums.reshape(-1)]).reshape(6, size, own_rows)
        packed = jnp.concatenate([packed.transpose(1, 0, 2).reshape(size, -1), biases.reshape(size, -1)], axis=1)
        packed = lax.psum_scatter(packed, "fsdp", scatter_dimension=0, tiled=False)
        packed = lax.psum(packed, "seq")
        vectors = packed[: 6 * own_rows].reshape(6, own_rows)
        attn_gain_grad, attn_shift_grad, mlp_gain_grad, mlp_shift_grad, proj_bias_grad, down_bias_grad = vectors
        qv_bias_grad = packed[6 * own_rows :]

    return (
        output,
        input_grad,
        attn_gain_grad,
        attn_shift_grad,
        qkv_weight_grad,
        qv_bias_grad,
        proj_grad,
        proj_bias_grad,
        mlp_gain_grad,
        mlp_shift_grad,
        up_grad,
        up_bias_grad,
        down_grad,
        down_bias_grad,
    )


def solution(mesh):
    split = P("fsdp")
    tokens = P("fsdp", "seq", None)
    matrix = P("fsdp", None)
    in_specs = (tokens, split, tokens, split, split, matrix, split, matrix) + (split,) * 3 + (matrix, split, matrix, split)
    out_specs = (tokens, tokens, split, split, matrix, split, matrix) + (split,) * 3 + (matrix, split, matrix, split)
    return jax.shard_map(per_device, mesh=mesh, in_specs=in_specs, out_specs=out_specs, check_vma=False)
```

profile of v0, /device:TPU:0, one launch (start us, length us, event | category | flops | bytes accessed | tf_op | source)
XLA Modules:
  0.0 356.9 jit_solution(6938339142051444618)
XLA Ops:
  9.8 3.0 collective-permute-start.1
  18.1 2.9 collective-permute-start.7
  22.6 3.6 all-to-all-start
  31.5 4.0 %collective-permute-done.7 = bf16[136,768]{1,0:T(8,128)(2,1)S(1)} collective-permute-done((bf16[136,768]{1,0:T(8,128)(2,1)}, bf16[136,768]{1,0:T(8,128)(2,1)S(1)}, u32[]{:S(2)}, u32[]{:S(2)}) %collective-permute-start.7) | collective-permute-done | bytes 208928 | tf_op jit(solution)/shard_map/ppermute | solution.py:63
  39.4 11.7 %collective-permute-done.3 = bf16[240,512]{1,0:T(8,128)(2,1)S(1)} collective-permute-done((bf16[240,512]{1,0:T(8,128)(2,1)S(1)}, bf16[240,512]{1,0:T(8,128)(2,1)S(1)}, u32[]{:S(2)}, u32[]{:S(2)}) %collective-permute-start.3) | collective-permute-done | bytes 245792 | tf_op jit(solution)/shard_map/ppermute | solution.py:63
  52.4 2.5 fusion.8.above
  57.9 2.6 fusion.6.above
  60.6 11.7 %attend.1 = (bf16[3,320,768]{2,1,0:T(8,128)(2,1)}, bf16[3,320,1024]{2,1,0:T(8,128)(2,1)}, bf16[240,256]{1,0:T(8,128)(2,1)}, bf16[240,256]{1,0:T(8,128)(2,1)}, bf...) custom-call(s32[4]{0:T(128)} %pad_add_fusion.2.meta, bf16[4,3,80,1024]{3,2,1,0:T(8,128)(2,1)} %bitcast.215, ...), custom_call_target="tpu_custom_call" | custom-call | flops 2088960 | bytes 7296 | tf_op jit(solution)/shard_map/attend/pallas_call | solution.py:165
  73.9 2.6 collective-permute-start.10
  78.7 7.4 %collective-permute-done.10.c2 = bf16[240,256]{1,0:T(8,128)(2,1)S(1)} collective-permute-done((bf16[240,256]{1,0:T(8,128)(2,1)}, bf16[240,256]{1,0:T(8,128)(2,1)S(1)}, u32[]{:S(2)}, u32[]{:S(2)}) %collective-permute-start.10) | collective-permute-done | bytes 122912 | tf_op jit(solution)/shard_map/ppermute | solution.py:67
  86.8 4.3 %project.1 = (f32[240,1024]{1,0:T(8,128)}, bf16[240,1024]{1,0:T(8,128)(2,1)}) custom-call(s32[4]{0:T(128)} %pad_add_fusion.2.meta, bf16[240,256]{1,0:T(8,128)(2,1)} %get-tuple-element.64.c0, bf16[240,256]{1,0:T(8,128)(2,1)} %copy-done.30, bf16[240,256]{1,0:T(8,128)(2,1)} %copy-done.32, bf16[240,256]{1,0:T(8,128)(2,1)} %copy-done.34, ...), custom_call_target="tpu_custom_call" | custom-call | flops 491520 | bytes 4448 | tf_op jit(solution)/shard_map/project/pallas_call | solution.py:269
  93.1 9.3 %collective-permute-done.13 = bf16[240,1024]{1,0:T(8,128)(2,1)S(1)} collective-permute-done((bf16[240,1024]{1,0:T(8,128)(2,1)}, bf16[240,1024]{1,0:T(8,128)(2,1)S(1)}, u32[]{:S(2)}, u32[]{:S(2)}) %collective-permute-start.13) | collective-permute-done | bytes 491552 | tf_op jit(solution)/shard_map/ppermute | solution.py:63
  104.9 3.9 %collective-permute-done.15 = bf16[240,512]{1,0:T(8,128)(2,1)S(1)} collective-permute-done((bf16[240,512]{1,0:T(8,128)(2,1)S(1)}, bf16[240,512]{1,0:T(8,128)(2,1)S(1)}, u32[]{:S(2)}, u32[]{:S(2)}) %collective-permute-start.15) | collective-permute-done | bytes 245792 | tf_op jit(solution)/shard_map/ppermute | solution.py:63
  112.7 2.8 collective-permute-done.16.normed.normed_o
  116.8 6.9 %feed.3 = (bf16[4,240,512]{2,1,0:T(8,128)(2,1)}, bf16[4,240,512]{2,1,0:T(8,128)(2,1)}, bf16[4,240,1024]{2,1,0:T(8,128)(2,1)}) custom-call(bf16[4,240,1024]{2,1,0:T(8,128)(2,1)} %copy-done.4, f32[4,240,512]{2,1,0:T(8,128)} %fusion.6.above, bf16[1024,512]{1,0:T(8,128)(2,1)} %bitcast.212, f32[1,512]{1,0:T(1,128)} %bitcast.254), custom_call_target="tpu_custom_call" | custom-call | flops 1966080 | bytes 8704 | tf_op jit(solution)/shard_map/feed/pallas_call | solution.py:302
  123.9 7.0 %feed.2 = (bf16[4,240,512]{2,1,0:T(8,128)(2,1)}, bf16[4,240,512]{2,1,0:T(8,128)(2,1)}, bf16[4,240,1024]{2,1,0:T(8,128)(2,1)}) custom-call(bf16[4,240,1024]{2,1,0:T(8,128)(2,1)} %copy-done.1, f32[4,240,512]{2,1,0:T(8,128)} %fusion.8.above, bf16[1024,512]{1,0:T(8,128)(2,1)} %bitcast.213, f32[1,512]{1,0:T(1,128)} %bitcast.255), custom_call_target="tpu_custom_call" | custom-call | flops 1966080 | bytes 8704 | tf_op jit(solution)/shard_map/feed/pallas_call | solution.py:302
  130.9 3.5 fusion.18
  137.9 13.0 %feed_grads.1 = (bf16[4,240,1024]{2,1,0:T(8,128)(2,1)}, bf16[4,240,1024]{2,1,0:T(8,128)(2,1)}, bf16[528,1024]{1,0:T(8,128)(2,1)}, bf16[1024,512]{1,0:T(8,128)(2,1)}) custom-call(bf16[4,240,512]{2,1,0:T(8,128)(2,1)} %get-tuple-element.74.act_e, bf16[4,240,512]{2,1,0:T(8,128)(2,1)} %get-tuple-element.75.act_o, bf16[4,240,512]{2,1,0:T(8,128)(2,1)} %get-tuple-element.76.grad_e, ...), custom_call_target="tpu_custom_call" | custom-call | flops 5898240 | bytes 18432 | tf_op jit(solution)/shard_map/feed_grads/pallas_call | solution.py:352
  153.8 5.7 %collective-permute-done.19.gy = bf16[240,1024]{1,0:T(8,128)(2,1)S(1)} collective-permute-done((bf16[240,1024]{1,0:T(8,128)(2,1)}, bf16[240,1024]{1,0:T(8,128)(2,1)S(1)}, u32[]{:S(2)}, u32[]{:S(2)}) %collective-permute-start.19) | collective-permute-done | bytes 491552 | tf_op jit(solution)/shard_map/ppermute | solution.py:63
  160.3 5.9 %middle.1 = (f32[240,1024]{1,0:T(8,128)}, bf16[240,1024]{1,0:T(8,128)(2,1)}, f32[4,1024]{1,0:T(4,128)}, bf16[240,256]{1,0:T(8,128)(2,1)}, bf16[240,256]{1,0:T(8,...) custom-call(s32[4]{0:T(128)} %pad_add_fusion.2.meta, bf16[4,240,1024]{2,1,0:T(8,128)(2,1)} %get-tuple-element.71.g0, ...), custom_call_target="tpu_custom_call" | custom-call | flops 491520 | bytes 8288 | tf_op jit(solution)/shard_map/middle/pallas_call | solution.py:397
  171.4 3.1 convolution_convert_fusion
  174.8 15.0 %collective-permute-done.21.d1 = bf16[240,256]{1,0:T(8,128)(2,1)S(1)} collective-permute-done((bf16[240,256]{1,0:T(8,128)(2,1)}, bf16[240,256]{1,0:T(8,128)(2,1)S(1)}, u32[]{:S(2)}, u32[]{:S(2)}) %collective-permute-start.21) | collective-permute-done | bytes 122912 | tf_op jit(solution)/shard_map/ppermute | solution.py:67
  192.9 15.7 %attend_back.1 = (bf16[3,320,768]{2,1,0:T(8,128)(2,1)}, bf16[2,240,1024]{2,1,0:T(8,128)(2,1)}, bf16[2,240,1024]{2,1,0:T(8,128)(2,1)}, f32[8,1024]{1,0:T(8,128)}) custom-call(s32[4]{0:T(128)} %pad_add_fusion.2.meta, bf16[4,3,80,1024]{3,2,1,0:T(8,128)(2,1)} %bitcast.216, bf16[240,256]{1,0:T(8,128)(2,1)} %get-tuple-element.80.d0, bf16[240,256]{1,0:T(8,128)(2,1)} %copy-done.26, ...), custom_call_target="tpu_custom_call" | custom-call | flops 3010560 | bytes 8736 | tf_op jit(solution)/shard_map/attend_back/pallas_call | solution.py:235
  210.2 3.8 %bitcast_convert_fusion = bf16[1024,768]{1,0:T(8,128)(2,1)S(1)} fusion(bf16[3,320,1024]{2,1,0:T(8,128)(2,1)} %get-tuple-element.69, bf16[3,320,768]{2,1,0:T(8,128)(2,1)} %get-tuple-element.88), kind=kOutput, calls=%fused_computation.2 | convolution fusion | flops 1510735872 | bytes 5013504 | tf_op jit(solution)/shard_map/dot_general | solution.py:43
  224.5 18.7 %collective-permute-done.27 = bf16[240,1024]{1,0:T(8,128)(2,1)S(1)} collective-permute-done((bf16[240,1024]{1,0:T(8,128)(2,1)S(1)}, bf16[240,1024]{1,0:T(8,128)(2,1)S(1)}, u32[]{:S(2)}, u32[]{:S(2)}) %collective-permute-start.27) | collective-permute-done | bytes 491552 | tf_op jit(solution)/shard_map/ppermute | solution.py:67
  251.9 3.9 %collective-permute-done.35 = bf16[136,1024]{1,0:T(8,128)(2,1)S(1)} collective-permute-done((bf16[136,1024]{1,0:T(8,128)(2,1)S(1)}, bf16[136,1024]{1,0:T(8,128)(2,1)S(1)}, u32[]{:S(2)}, u32[]{:S(2)}) %collective-permute-start.35) | collective-permute-done | bytes 278560 | tf_op jit(solution)/shard_map/ppermute | solution.py:63
  257.6 3.7 %collective-permute-done.34 = bf16[136,1024]{1,0:T(8,128)(2,1)S(1)} collective-permute-done((bf16[136,1024]{1,0:T(8,128)(2,1)S(1)}, bf16[136,1024]{1,0:T(8,128)(2,1)S(1)}, u32[]{:S(2)}, u32[]{:S(2)}) %collective-permute-start.34) | collective-permute-done | bytes 278560 | tf_op jit(solution)/shard_map/ppermute | solution.py:63
  269.0 2.8 slice_convert_fusion
  274.2 13.4 %collective-permute-done.36 = bf16[136,1792]{1,0:T(8,128)(2,1)} collective-permute-done((bf16[136,1792]{1,0:T(8,128)(2,1)}, bf16[136,1792]{1,0:T(8,128)(2,1)}, u32[]{:S(2)}, u32[]{:S(2)}) %collective-permute-start.36) | collective-permute-done | bytes 487456 | tf_op jit(solution)/shard_map/ppermute | solution.py:67
  288.6 21.9 %collective-permute-done.47 = bf16[8,128,256]{2,1,0:T(8,128)(2,1)S(1)} collective-permute-done((bf16[8,128,256]{2,1,0:T(8,128)(2,1)S(1)}, bf16[8,128,256]{2,1,0:T(8,128)(2,1)S(1)}, u32[]{:S(2)}, u32[]{:S(2)}) %collective-permute-start.47) | collective-permute-done | bytes 524320 | tf_op jit(solution)/shard_map/ppermute | solution.py:67
  321.4 4.1 %finish.1 = bf16[240,1024]{1,0:T(8,128)(2,1)} custom-call(bf16[240,1024]{1,0:T(8,128)(2,1)} %bitcast.218, bf16[2,240,1024]{2,1,0:T(8,128)(2,1)} %get-tuple-element.90.mine, bf16[240,1024]{1,0:T(8,128)(2,1)} %copy-done.23, bf16[240,1024]{1,0:T(8,128)(2,1)} %copy-done.24, f32[240,1024]{1,0:T(8,128)} %get-tuple-element.107.hidden_grad, f32[6,1024]{1,0:T(8,128)} %bitcast.246), custom_call_target="tpu_custom_call" | custom-call | flops 4800 | bytes 2880 | tf_op jit(solution)/shard_map/finish/pallas_call | solution.py:426
  332.0 8.6 %collective-permute-done.45 = bf16[240,1024]{1,0:T(8,128)(2,1)} collective-permute-done((bf16[240,1024]{1,0:T(8,128)(2,1)}, bf16[240,1024]{1,0:T(8,128)(2,1)}, u32[]{:S(2)}, u32[]{:S(2)}) %collective-permute-start.45) | collective-permute-done | bytes 491552 | tf_op jit(solution)/shard_map/ppermute | solution.py:63
  (288 shorter events, 113.1 us)
Async XLA Ops:
  7.2 53.4 %all-gather.6.cloned.1.call-start = ((), (), s32[]{:S(2)}) async-start(), calls=%async_computation.3 | async-start | bytes 2457600 | tf_op jit(solution)/shard_map/all_gather | solution.py:471
  9.8 25.8 %collective-permute-start.1 = (bf16[240,1024]{1,0:T(8,128)(2,1)S(1)}, bf16[240,1024]{1,0:T(8,128)(2,1)S(1)}, u32[]{:S(2)}, u32[]{:S(2)}) collective-permute-start(bf16[240,1024]{1,0:T(8,128)(2,1)S(1)} %bitcast.219), channel_id=1, source_target_pairs={{0,16},{4,20},{8,24},{12,28},{16,0},{20,4},{24,8},{28,12},{1,17},{... | collective-permute-start | bytes 1474568 | tf_op jit(solution)/shard_map/ppermute | solution.py:63
  12.9 24.9 %collective-permute-start = (bf16[240,1024]{1,0:T(8,128)(2,1)S(1)}, bf16[240,1024]{1,0:T(8,128)(2,1)S(1)}, u32[]{:S(2)}, u32[]{:S(2)}) collective-permute-start(bf16[240,1024]{1,0:T(8,128)(2,1)S(1)} %bitcast.220), channel_id=1, source_target_pairs={{0,8},{4,12},{8,0},{12,4},{16,24},{20,28},{24,16},{28,20},{1,9},{5... | collective-permute-start | bytes 1474568 | tf_op jit(solution)/shard_map/ppermute | solution.py:63
  18.1 17.4 %collective-permute-start.7 = (bf16[136,768]{1,0:T(8,128)(2,1)}, bf16[136,768]{1,0:T(8,128)(2,1)S(1)}, u32[]{:S(2)}, u32[]{:S(2)}) collective-permute-start(bf16[136,768]{1,0:T(8,128)(2,1)} %get-tuple-element.207), channel_id=1, source_target_pairs={{0,24},{4,28},{8,16},{12,20},{16,8},{20,12},{24,0},{28,4},{1,25},{... | collective-permute-start | bytes 626696 | tf_op jit(solution)/shard_map/ppermute | solution.py:63
  22.6 37.9 %all-to-all-start = ((bf16[8,128,512]{2,1,0:T(8,128)(2,1)}), bf16[8,128,512]{2,1,0:T(8,128)(2,1)S(1)}, u32[]{:S(2)}, u32[]{:S(2)}) async-start(bf16[8,128,512]{2,1,0:T(8,128)(2,1)} %bitcast.209), calls=%async_computation | async-start | bytes 2097152 | tf_op jit(solution)/shard_map/all_to_all | solution.py:508
  26.2 59.9 %all-gather.4.cloned.1.call-start = ((), (), s32[]{:S(2)}) async-start(), calls=%async_computation.1 | async-start | bytes 2359296 | tf_op jit(solution)/shard_map/all_gather | solution.py:503
  26.9 236.9 %all-reduce.13.cloned.1.call-start = ((), (), s32[]{:S(2)}) async-start(), calls=%async_computation.2 | async-start | bytes 2162688 | tf_op jit(solution)/shard_map/psum | solution.py:557
  35.6 19.4 %collective-permute-start.8 = (bf16[4,136,768]{2,1,0:T(8,128)(2,1)S(1)}, bf16[4,136,768]{2,1,0:T(8,128)(2,1)S(1)}, u32[]{:S(2)}, u32[]{:S(2)}) collective-permute-start(bf16[4,136,768]{2,1,0:T(8,128)(2,1)S(1)} %pad_maximum_fusion.2), channel_id=1, source_target_pairs={{0,4},{4,0},{8,12},{12,8},{16,20},{20,16},{24,28},{28,24},{1,5},{5... | collective-permute-start | bytes 2506760 | tf_op jit(solution)/shard_map/ppermute | solution.py:63
  35.7 15.3 %collective-permute-start.3 = (bf16[240,512]{1,0:T(8,128)(2,1)S(1)}, bf16[240,512]{1,0:T(8,128)(2,1)S(1)}, u32[]{:S(2)}, u32[]{:S(2)}) collective-permute-start(bf16[240,512]{1,0:T(8,128)(2,1)S(1)} %slice.277), channel_id=1, source_target_pairs={{0,8},{4,12},{8,0},{12,4},{16,24},{20,28},{24,16},{28,20},{1,9},{5... | collective-permute-start | bytes 737288 | tf_op jit(solution)/shard_map/ppermute | solution.py:63
  134.4 19.4 %collective-permute-start.20 = (bf16[240,1024]{1,0:T(8,128)(2,1)}, bf16[240,1024]{1,0:T(8,128)(2,1)S(1)}, u32[]{:S(2)}, u32[]{:S(2)}) collective-permute-start(bf16[240,1024]{1,0:T(8,128)(2,1)} %get-tuple-element.154), channel_id=1, source_target_pairs={{0,24},{4,28},{8,16},{12,20},{16,8},{20,12},{24,0},{28,4},{1,25},{... | collective-permute-start | bytes 1474568 | tf_op jit(solution)/shard_map/ppermute | solution.py:63
  135.6 24.0 %collective-permute-start.19 = (bf16[240,1024]{1,0:T(8,128)(2,1)}, bf16[240,1024]{1,0:T(8,128)(2,1)S(1)}, u32[]{:S(2)}, u32[]{:S(2)}) collective-permute-start(bf16[240,1024]{1,0:T(8,128)(2,1)} %get-tuple-element.155), channel_id=1, source_target_pairs={{0,16},{4,20},{8,24},{12,28},{16,0},{20,4},{24,8},{28,12},{1,17},{... | collective-permute-start | bytes 1474568 | tf_op jit(solution)/shard_map/ppermute | solution.py:63
  135.7 23.8 %collective-permute-start.18 = (bf16[240,1024]{1,0:T(8,128)(2,1)}, bf16[240,1024]{1,0:T(8,128)(2,1)}, u32[]{:S(2)}, u32[]{:S(2)}) collective-permute-start(bf16[240,1024]{1,0:T(8,128)(2,1)} %get-tuple-element.156), channel_id=1, source_target_pairs={{0,8},{4,12},{8,0},{12,4},{16,24},{20,28},{24,16},{28,20},{1,9},{5... | collective-permute-start | bytes 1474568 | tf_op jit(solution)/shard_map/ppermute | solution.py:63
  152.2 40.1 %collective-permute-start.24 = (bf16[1024,256]{1,0:T(8,128)(2,1)S(1)}, bf16[1024,256]{1,0:T(8,128)(2,1)S(1)}, u32[]{:S(2)}, u32[]{:S(2)}) collective-permute-start(bf16[1024,256]{1,0:T(8,128)(2,1)S(1)} %get-tuple-element.174), channel_id=1, source_target_pairs={{0,1},{1,0},{2,3},{3,2},{4,5},{5,4},{6,7},{7,6},{8,9},{9,8},{10,11... | collective-permute-start | bytes 1572872 | tf_op jit(solution)/shard_map/ppermute | solution.py:67
  166.9 23.0 %collective-permute-start.21 = (bf16[240,256]{1,0:T(8,128)(2,1)}, bf16[240,256]{1,0:T(8,128)(2,1)S(1)}, u32[]{:S(2)}, u32[]{:S(2)}) collective-permute-start(bf16[240,256]{1,0:T(8,128)(2,1)} %get-tuple-element.81), channel_id=1, source_target_pairs={{0,1},{1,0},{2,3},{3,2},{4,5},{5,4},{6,7},{7,6},{8,9},{9,8},{10,11... | collective-permute-start | bytes 368648 | tf_op jit(solution)/shard_map/ppermute | solution.py:67
  168.5 21.4 %collective-permute-start.22 = (bf16[240,256]{1,0:T(8,128)(2,1)}, bf16[240,256]{1,0:T(8,128)(2,1)S(1)}, u32[]{:S(2)}, u32[]{:S(2)}) collective-permute-start(bf16[240,256]{1,0:T(8,128)(2,1)} %get-tuple-element.82), channel_id=1, source_target_pairs={{0,2},{1,3},{2,0},{3,1},{4,6},{5,7},{6,4},{7,5},{8,10},{9,11},{10,... | collective-permute-start | bytes 368648 | tf_op jit(solution)/shard_map/ppermute | solution.py:67
  170.1 22.3 %collective-permute-start.23 = (bf16[240,256]{1,0:T(8,128)(2,1)}, bf16[240,256]{1,0:T(8,128)(2,1)S(1)}, u32[]{:S(2)}, u32[]{:S(2)}) collective-permute-start(bf16[240,256]{1,0:T(8,128)(2,1)} %get-tuple-element.83), channel_id=1, source_target_pairs={{0,3},{1,2},{2,1},{3,0},{4,7},{5,6},{6,5},{7,4},{8,11},{9,10},{10,... | collective-permute-start | bytes 368648 | tf_op jit(solution)/shard_map/ppermute | solution.py:67
  218.2 25.9 %collective-permute-start.28 = (bf16[1024,256]{1,0:T(8,128)(2,1)S(1)}, bf16[1024,256]{1,0:T(8,128)(2,1)S(1)}, u32[]{:S(2)}, u32[]{:S(2)}) collective-permute-start(bf16[1024,256]{1,0:T(8,128)(2,1)S(1)} %add_convert_fusion.3), channel_id=1, source_target_pairs={{0,2},{1,3},{2,0},{3,1},{4,6},{5,7},{6,4},{7,5},{8,10},{9,11},{10,... | collective-permute-start | bytes 1572872 | tf_op jit(solution)/shard_map/ppermute | solution.py:67
  219.1 24.1 %collective-permute-start.27 = (bf16[240,1024]{1,0:T(8,128)(2,1)S(1)}, bf16[240,1024]{1,0:T(8,128)(2,1)S(1)}, u32[]{:S(2)}, u32[]{:S(2)}) collective-permute-start(bf16[240,1024]{1,0:T(8,128)(2,1)S(1)} %get-tuple-element.176), channel_id=1, source_target_pairs={{0,1},{1,0},{2,3},{3,2},{4,5},{5,4},{6,7},{7,6},{8,9},{9,8},{10,11... | collective-permute-start | bytes 1474568 | tf_op jit(solution)/shard_map/ppermute | solution.py:67
  221.6 92.9 %collective-permute-start.42 = (bf16[4,240,1024]{2,1,0:T(8,128)(2,1)}, bf16[4,240,1024]{2,1,0:T(8,128)(2,1)S(1)}, u32[]{:S(2)}, u32[]{:S(2)}) collective-permute-start(bf16[4,240,1024]{2,1,0:T(8,128)(2,1)} %get-tuple-element.104), channel_id=1, source_target_pairs={{0,4},{4,0},{8,12},{12,8},{16,20},{20,16},{24,28},{28,24},{1,5},{5... | collective-permute-start | bytes 5898248 | tf_op jit(solution)/shard_map/ppermute | solution.py:63
  221.9 22.6 %collective-permute-start.31 = (bf16[136,768]{1,0:T(8,128)(2,1)S(1)}, bf16[136,768]{1,0:T(8,128)(2,1)S(1)}, u32[]{:S(2)}, u32[]{:S(2)}) collective-permute-start(bf16[136,768]{1,0:T(8,128)(2,1)S(1)} %get-tuple-element.186), channel_id=1, source_target_pairs={{0,24},{4,28},{8,16},{12,20},{16,8},{20,12},{24,0},{28,4},{1,25},{... | collective-permute-start | bytes 626696 | tf_op jit(solution)/shard_map/ppermute | solution.py:63
  224.0 22.9 %collective-permute-start.30 = (bf16[136,768]{1,0:T(8,128)(2,1)S(1)}, bf16[136,768]{1,0:T(8,128)(2,1)S(1)}, u32[]{:S(2)}, u32[]{:S(2)}) collective-permute-start(bf16[136,768]{1,0:T(8,128)(2,1)S(1)} %get-tuple-element.187), channel_id=1, source_target_pairs={{0,16},{4,20},{8,24},{12,28},{16,0},{20,4},{24,8},{28,12},{1,17},{... | collective-permute-start | bytes 626696 | tf_op jit(solution)/shard_map/ppermute | solution.py:63
  246.9 14.4 %collective-permute-start.34 = (bf16[136,1024]{1,0:T(8,128)(2,1)S(1)}, bf16[136,1024]{1,0:T(8,128)(2,1)S(1)}, u32[]{:S(2)}, u32[]{:S(2)}) collective-permute-start(bf16[136,1024]{1,0:T(8,128)(2,1)S(1)} %get-tuple-element.169), channel_id=1, source_target_pairs={{0,16},{4,20},{8,24},{12,28},{16,0},{20,4},{24,8},{28,12},{1,17},{... | collective-permute-start | bytes 835592 | tf_op jit(solution)/shard_map/ppermute | solution.py:63
  249.0 13.9 %collective-permute-start.33 = (bf16[136,1024]{1,0:T(8,128)(2,1)S(1)}, bf16[136,1024]{1,0:T(8,128)(2,1)S(1)}, u32[]{:S(2)}, u32[]{:S(2)}) collective-permute-start(bf16[136,1024]{1,0:T(8,128)(2,1)S(1)} %get-tuple-element.170), channel_id=1, source_target_pairs={{0,8},{4,12},{8,0},{12,4},{16,24},{20,28},{24,16},{28,20},{1,9},{5... | collective-permute-start | bytes 835592 | tf_op jit(solution)/shard_map/ppermute | solution.py:63
  249.9 15.2 %collective-permute-start.39 = (bf16[2,128,256]{2,1,0:T(8,128)(2,1)}, bf16[2,128,256]{2,1,0:T(8,128)(2,1)}, u32[]{:S(2)}, u32[]{:S(2)}) collective-permute-start(bf16[2,128,256]{2,1,0:T(8,128)(2,1)} %get-tuple-element.199), channel_id=1, source_target_pairs={{0,8},{4,12},{8,0},{12,4},{16,24},{20,28},{24,16},{28,20},{1,9},{5... | collective-permute-start | bytes 393224 | tf_op jit(solution)/shard_map/ppermute | solution.py:63
  263.9 23.7 %collective-permute-start.36 = (bf16[136,1792]{1,0:T(8,128)(2,1)}, bf16[136,1792]{1,0:T(8,128)(2,1)}, u32[]{:S(2)}, u32[]{:S(2)}) collective-permute-start(bf16[136,1792]{1,0:T(8,128)(2,1)} %pad_maximum_fusion.7), channel_id=1, source_target_pairs={{0,2},{1,3},{2,0},{3,1},{4,6},{5,7},{6,4},{7,5},{8,10},{9,11},{10,... | collective-permute-start | bytes 1462280 | tf_op jit(solution)/shard_map/ppermute | solution.py:67
  265.2 54.6 %collective-permute-start.37 = (bf16[240,1024]{1,0:T(8,128)(2,1)}, bf16[240,1024]{1,0:T(8,128)(2,1)S(1)}, u32[]{:S(2)}, u32[]{:S(2)}) collective-permute-start(bf16[240,1024]{1,0:T(8,128)(2,1)} %get-tuple-element.175), channel_id=1, source_target_pairs={{0,1},{1,0},{2,3},{3,2},{4,5},{5,4},{6,7},{7,6},{8,9},{9,8},{10,11... | collective-permute-start | bytes 1474568 | tf_op jit(solution)/shard_map/ppermute | solution.py:67
  268.9 41.5 %collective-permute-start.47 = (bf16[8,128,256]{2,1,0:T(8,128)(2,1)S(1)}, bf16[8,128,256]{2,1,0:T(8,128)(2,1)S(1)}, u32[]{:S(2)}, u32[]{:S(2)}) collective-permute-start(bf16[8,128,256]{2,1,0:T(8,128)(2,1)S(1)} %bitcast.228), channel_id=1, source_target_pairs={{0,1},{1,0},{2,3},{3,2},{4,5},{5,4},{6,7},{7,6},{8,9},{9,8},{10,11... | collective-permute-start | bytes 1572872 | tf_op jit(solution)/shard_map/ppermute | solution.py:67
  271.8 48.0 %collective-permute-start.38 = (bf16[240,1024]{1,0:T(8,128)(2,1)S(1)}, bf16[240,1024]{1,0:T(8,128)(2,1)S(1)}, u32[]{:S(2)}, u32[]{:S(2)}) collective-permute-start(bf16[240,1024]{1,0:T(8,128)(2,1)S(1)} %copy-done.20), channel_id=1, source_target_pairs={{0,2},{1,3},{2,0},{3,1},{4,6},{5,7},{6,4},{7,5},{8,10},{9,11},{10,... | collective-permute-start | bytes 1474568 | tf_op jit(solution)/shard_map/ppermute | solution.py:67
  316.3 15.7 %collective-permute-start.43 = (bf16[240,1024]{1,0:T(8,128)(2,1)}, bf16[240,1024]{1,0:T(8,128)(2,1)}, u32[]{:S(2)}, u32[]{:S(2)}) collective-permute-start(bf16[240,1024]{1,0:T(8,128)(2,1)} %get-tuple-element.159), channel_id=1, source_target_pairs={{0,8},{4,12},{8,0},{12,4},{16,24},{20,28},{24,16},{28,20},{1,9},{5... | collective-permute-start | bytes 1474568 | tf_op jit(solution)/shard_map/ppermute | solution.py:63
  318.2 22.4 %collective-permute-start.45 = (bf16[240,1024]{1,0:T(8,128)(2,1)}, bf16[240,1024]{1,0:T(8,128)(2,1)}, u32[]{:S(2)}, u32[]{:S(2)}) collective-permute-start(bf16[240,1024]{1,0:T(8,128)(2,1)} %get-tuple-element.160), channel_id=1, source_target_pairs={{0,24},{4,28},{8,16},{12,20},{16,8},{20,12},{24,0},{28,4},{1,25},{... | collective-permute-start | bytes 1474568 | tf_op jit(solution)/shard_map/ppermute | solution.py:63
  319.6 22.4 %collective-permute-start.44 = (bf16[240,1024]{1,0:T(8,128)(2,1)}, bf16[240,1024]{1,0:T(8,128)(2,1)}, u32[]{:S(2)}, u32[]{:S(2)}) collective-permute-start(bf16[240,1024]{1,0:T(8,128)(2,1)} %get-tuple-element.161), channel_id=1, source_target_pairs={{0,16},{4,20},{8,24},{12,28},{16,0},{20,4},{24,8},{28,12},{1,17},{... | collective-permute-start | bytes 1474568 | tf_op jit(solution)/shard_map/ppermute | solution.py:63
  327.3 17.7 %collective-permute-start.46 = (bf16[136,2560]{1,0:T(8,128)(2,1)}, bf16[136,2560]{1,0:T(8,128)(2,1)}, u32[]{:S(2)}, u32[]{:S(2)}) collective-permute-start(bf16[136,2560]{1,0:T(8,128)(2,1)} %pad_maximum_fusion.5), channel_id=1, source_target_pairs={{0,1},{1,0},{2,3},{3,2},{4,5},{5,4},{6,7},{7,6},{8,9},{9,8},{10,11... | collective-permute-start | bytes 2088968 | tf_op jit(solution)/shard_map/ppermute | solution.py:67
  (61 other events, 485.7 us)
Sparse Core Ops, SparseCore 0:
  9.6 46.2 all-gather.5
  57.8 26.7 all-gather.3
  151.1 67.6 all-reduce.12
where the time goes:
time: 358 us; the launch traced here: 357 us
  waiting for transfers between devices  144 us (40%)
  Pallas kernels  68.6 us (19%)
  starting transfers between devices  54.8 us (15%)
  other arithmetic  35.8 us (10%)
  local copies, waits for them, and re-layouts  26.5 us (7%)
  between operations  14.7 us (4%)
  matrix products  12.1 us (3%)
    ppermute x14, waiting for transfers between devices, cross(): return lax.ppermute(value, 'seq', [(i, i ^ mask) for i in range(ZS)])  80.8 us
    ppermute x34, waiting for transfers between devices, swap(): return lax.ppermute(value, 'fsdp', [(i, i ^ mask) for i in range(size)])  62.1 us
    ppermute x34, starting transfers between devices, swap(): return lax.ppermute(value, 'fsdp', [(i, i ^ mask) for i in range(size)])  33.8 us
    ppermute x14, starting transfers between devices, cross(): return lax.ppermute(value, 'seq', [(i, i ^ mask) for i in range(ZS)])  17.3 us
    pallas_call x1, Pallas kernels, attend_back(): pl.pallas_call(attend_back_kernel, name='attend_back', grid_spec=pltpu.Pr...  15.7 us
    unnamed x106, local copies, waits for them, and re-layouts  14.8 us
    pallas_call x2, Pallas kernels, feed(): pl.pallas_call(feed_kernel, name='feed', grid=(count,), in_specs=[wide, t...  13.9 us
    pallas_call x1, Pallas kernels, feed_grads(): pl.pallas_call(feed_grads_kernel, name='feed_grads', grid=(4,), in_specs=...  13 us
  transfers between devices with their start and end apart: 52, of which 22 were waited for; matrix products, arithmetic and copies ran while one was open for 15% of the time, Pallas kernels for 16%

commit v1 on v0

--- a/solution.py
+++ b/solution.py
@@ -114,10 +114,14 @@
 
 
 def head_probs(queries, keys, valid):
-    scores = mm_rt(queries, keys) * HEAD ** (-0.5)
+    scores = mm_rt(keys, queries) * HEAD ** (-0.5)
     scores = jnp.where(valid, scores, MASKED)
-    exponent = jnp.exp(scores - jnp.max(scores, axis=-1, keepdims=True))
-    return exponent * (1.0 / jnp.sum(exponent, axis=-1, keepdims=True))
+    exponent = jnp.exp(scores - jnp.max(scores, axis=0, keepdims=True))
+    return exponent * (1.0 / jnp.sum(exponent, axis=0, keepdims=True))
+
+
+def both_heads(low, high):
+    return jnp.concatenate([low[:HEAD], high[HEAD:]], axis=0).T
 
 
 def attend_kernel(meta, rows_ref, wq, wk, wv, vecs, bias, qkv_ref, normed_ref, c0, c1, c2, c3):
@@ -135,16 +139,16 @@
         part = (mm(normed, w[...].reshape(model, width)) + bias[:, i * width : (i + 1) * width]).astype(BF16)
         qkv_ref[0, :, i * width : (i + 1) * width] = part
         parts.append(part)
-    valid = lax.broadcasted_iota(jnp.int32, (1, slots), 1) < length
+    valid = lax.broadcasted_iota(jnp.int32, (slots, slots), 0) < length
     first = lax.broadcasted_iota(jnp.int32, (1, 2 * HEAD), 1) < HEAD
     for pair in range(width // (2 * HEAD)):
         lanes = slice(pair * 2 * HEAD, (pair + 1) * 2 * HEAD)
         queries, keys, values = (part[:, lanes] for part in parts)
         outs = []
         for mine in (first, ~first):
-            probs = head_probs(jnp.where(mine, queries, jnp.zeros_like(queries)), keys, valid)
-            outs.append(mm(probs.astype(BF16), values))
-        context = jnp.where(first, outs[0], outs[1])
+            probs = head_probs(queries, jnp.where(mine, keys, jnp.zeros_like(keys)), valid)
+            outs.append(mm_lt(values, probs.astype(BF16)))
+        context = both_heads(*outs)
         pieces = [context[k * local : (k + 1) * local] for k in range(ZS)]
         for k, out in enumerate((c0, c1, c2, c3)):
             out[:, lanes] = chosen(pieces, z ^ k).astype(BF16)
@@ -191,7 +195,7 @@
     z = meta[meta.shape[0] - 1]
     given = [d[...] for d in (d0, d1, d2, d3)]
     upstream = jnp.concatenate([chosen(given, z ^ k) for k in range(ZS)], axis=0)
-    valid = lax.broadcasted_iota(jnp.int32, (1, slots), 1) < length
+    valid = lax.broadcasted_iota(jnp.int32, (slots, slots), 0) < length
     first = lax.broadcasted_iota(jnp.int32, (1, 2 * HEAD), 1) < HEAD
     for pair in range(width // (2 * HEAD)):
         spans = [slice(i * width + pair * 2 * HEAD, i * width + (pair + 1) * 2 * HEAD) for i in range(3)]
@@ -199,14 +203,15 @@
         above = upstream[:, spans[0]]
         grads = []
         for mine in (first, ~first):
-            probs = head_probs(jnp.where(mine, queries, jnp.zeros_like(queries)), keys, valid)
-            probs_grad = mm_rt(jnp.where(mine, above, jnp.zeros_like(above)), values)
-            inner = jnp.sum(probs * probs_grad, axis=-1, keepdims=True)
+            probs = head_probs(queries, jnp.where(mine, keys, jnp.zeros_like(keys)), valid)
+            probs_grad = mm_rt(jnp.where(mine, values, jnp.zeros_like(values)), above)
+            inner = jnp.sum(probs * probs_grad, axis=0, keepdims=True)
             scores_grad = (probs * (probs_grad - inner) * HEAD ** (-0.5)).astype(BF16)
             grads.append(
-                (mm(scores_grad, keys), mm_lt(scores_grad, queries), mm_lt(probs.astype(BF16), above))
+                (mm_lt(keys, scores_grad), mm(scores_grad, queries), mm(probs.astype(BF16), above))
             )
-        for span, low, high in zip(spans, *grads):
+        dqkv_ref[0, :, spans[0]] = both_heads(grads[0][0], grads[1][0]).astype(BF16)
+        for span, low, high in zip(spans[1:], grads[0][1:], grads[1][1:]):
             dqkv_ref[0, :, span] = jnp.where(first, low, high).astype(BF16)
     grad = dqkv_ref[0]
     total = mm_rt(grad[:, :width], wq[...].reshape(model, width))
@@ -283,26 +288,29 @@
 
 
 def feed_kernel(normed, above, up, bias, act_ref, grad_ref, back_ref):
-    value = mm(normed[0], up[...]) + bias[...]
+    count, rows, model = normed.shape
+    width = up.shape[1]
+    value = mm(normed[...].reshape(count * rows, model), up[...]) + bias[...]
     square = value * value
     root = math.sqrt(2.0 / math.pi)
     bend = jnp.tanh(root * value * (1.0 + 0.044715 * square))
-    act_ref[0] = (0.5 * value * (1.0 + bend)).astype(BF16)
-    slope = 0.5 * (1.0 + bend) + 0.5 * value * (1.0 - bend * bend) * root * (1.0 + 3 * 0.044715 * square)
-    grad = (above[0] * slope).astype(BF16)
-    grad_ref[0] = grad
-    back_ref[0] = mm_rt(grad, up[...]).astype(BF16)
+    half = 0.5 * (1.0 + bend)
+    act_ref[...] = (value * half).astype(BF16).reshape(count, rows, width)
+    slope = half + 0.5 * value * (1.0 - bend * bend) * (root + 3 * 0.044715 * root * square)
+    grad = (above[...].reshape(count * rows, width) * slope).astype(BF16)
+    grad_ref[...] = grad.reshape(count, rows, width)
+    back_ref[...] = mm_rt(grad, up[...]).astype(BF16).reshape(count, rows, model)
 
 
 def feed(normed, above, up, bias):
     count, rows, model = normed.shape
     width = up.shape[1]
-    wide = pl.BlockSpec((1, rows, model), lambda i: (i, 0, 0))
-    thin = pl.BlockSpec((1, rows, width), lambda i: (i, 0, 0))
+    wide = pl.BlockSpec((2, rows, model), lambda i: (i, 0, 0))
+    thin = pl.BlockSpec((2, rows, width), lambda i: (i, 0, 0))
     return pl.pallas_call(
         feed_kernel,
         name="feed",
-        grid=(count,),
+        grid=(count // 2,),
         in_specs=[wide, thin, block(model, width), block(1, width)],
         out_specs=[thin, thin, wide],
         out_shape=[shape_of((count, rows, width), BF16)] * 2 + [shape_of((count, rows, model), BF16)],
@@ -615,21 +623,23 @@
     far = cross(middle_sum, 2)
     up_sum = lax.optimization_barrier(joined(after(up_half, middle_sum), up_across))
     up_sum = up_sum.reshape(4, 2, own_rows, half_width)
-    qkv_mine = lax.optimization_barrier(over_team_chips(qkv_both, lambda m: chip ^ m, up_sum))
-    pair = jnp.stack([after(pick(up_sum, core, 1), qkv_mine), swap(pick(up_sum, 1 - core, 1), 1)], axis=1)
-    proj_mine = over_team_chips(proj_both, chip_at, pair)
-    lanes = qkv_mine.shape[1]
-    packed = jnp.concatenate([qkv_mine, proj_mine], axis=1)
-    packed_two = cross(packed, 2)
-    up_rel = [after(pick(pair, chip), packed)] + [swap(pick(pair, chip ^ m), 2 * m) for m in (1, 2, 3)]
-    up_rel = lax.optimization_barrier(jnp.stack(up_rel).reshape(TEAM, own_rows, half_width))
-    up_other = cross(up_rel, 1)
+    pair = jnp.stack([pick(up_sum, core, 1), swap(pick(up_sum, 1 - core, 1), 1)], axis=1)
+    up_moved = [swap(pick(pair, chip ^ m), 2 * m) for m in (1, 2, 3)]
     out_core = swap(after(out_odd, give), 1)
-    out_sums = [joined(after(out_even[m], up_rel), out_core[m]) for m in (1, 2, 3)]
+    out_sums = [joined(after(out_even[m], up_sum), out_core[m]) for m in (1, 2, 3)]
     out_moved = [swap(part, 2 * m) for m, part in zip((1, 2, 3), out_sums)]
     down_grad = after(down_total, qkv_both)[:down_rows].astype(F32)
-    input_grad = finish(own, mine, near[0], far, after(hidden_grad, *out_sums), vecs)
-    qkv_two = after(packed_two, input_grad)[:, :lanes]
+    input_grad = finish(own, mine, near[0], far, after(hidden_grad, pair, down_grad, *out_sums), vecs)
+    qkv_mine = lax.optimization_barrier(over_team_chips(qkv_both, lambda m: chip ^ m, up_sum))
+    proj_mine = over_team_chips(proj_both, chip_at, up_sum)
+    lanes = qkv_mine.shape[1]
+    packed = jnp.concatenate([after(qkv_mine, far), proj_mine], axis=1)
+    packed_two = cross(packed, 2)
+    up_rel = jnp.stack([after(pick(pair, chip), packed)] + up_moved)
+    up_rel = lax.optimization_barrier(up_rel.reshape(TEAM, own_rows, half_width))
+    up_other = cross(up_rel, 1)
+    packed_two = after(packed_two, up_rel)
+    qkv_two = packed_two[:, :lanes]
     proj_two = lax.optimization_barrier(joined(proj_mine, packed_two[:, lanes:]))
     packed_one = cross(jnp.concatenate([qkv_mine, qkv_two, proj_two], axis=1), 1)
     qkv_near = [packed_one[:, :lanes], packed_one[:, lanes : 2 * lanes]]

time: 358 us -> 328 us (0.916)
  waiting for transfers between devices: 144 us -> 121 us
    ppermute x14, waiting for transfers between devices: 80.8 us -> 66.5 us  [cross(): return lax.ppermute(value, 'seq', [(i, i ^ mask) for i in range(ZS)])]
    ppermute x34, waiting for transfers between devices: 62.1 us -> 52.7 us  [swap(): return lax.ppermute(value, 'fsdp', [(i, i ^ mask) for i in range(size)])]
    unnamed x106 -> x104, local copies, waits for them, and re-layouts: 14.8 us -> 11.9 us
  transfers between devices with their start and end apart: 52 -> 52, of which waited for: 22 -> 22; matrix products, arithmetic and copies ran while one was open for 15% -> 16% of each run, Pallas kernels for 16% -> 17%
where the time goes in v1:
time: 328 us; the launch traced here: 327 us
  waiting for transfers between devices  121 us (37%)
  Pallas kernels  66.1 us (20%)
  starting transfers between devices  54.9 us (17%)
  other arithmetic  35.4 us (11%)
  local copies, waits for them, and re-layouts  24.3 us (7%)
  between operations  14.7 us (4%)
  matrix products  10.6 us (3%)
    ppermute x14, waiting for transfers between devices, cross(): return lax.ppermute(value, 'seq', [(i, i ^ mask) for i in range(ZS)])  66.5 us
    ppermute x34, waiting for transfers between devices, swap(): return lax.ppermute(value, 'fsdp', [(i, i ^ mask) for i in range(size)])  52.7 us
    ppermute x34, starting transfers between devices, swap(): return lax.ppermute(value, 'fsdp', [(i, i ^ mask) for i in range(size)])  33.5 us
    ppermute x14, starting transfers between devices, cross(): return lax.ppermute(value, 'seq', [(i, i ^ mask) for i in range(ZS)])  17.7 us
    pallas_call x1, Pallas kernels, attend_back(): pl.pallas_call(attend_back_kernel, name='attend_back', grid_spec=pltpu.Pr...  14.5 us
    pallas_call x1, Pallas kernels, feed_grads(): pl.pallas_call(feed_grads_kernel, name='feed_grads', grid=(4,), in_specs=...  13 us
    pallas_call x2, Pallas kernels, feed(): pl.pallas_call(feed_kernel, name='feed', grid=(count // 2,), in_specs=[wi...  12.2 us
    pallas_call x1, Pallas kernels, attend(): pl.pallas_call(attend_kernel, name='attend', grid_spec=pltpu.PrefetchScal...  12 us
  transfers between devices with their start and end apart: 52, of which 22 were waited for; matrix products, arithmetic and copies ran while one was open for 16% of the time, Pallas kernels for 17%

profile of v1, /device:TPU:0, one launch (start us, length us, event | category | flops | bytes accessed | tf_op | source)
XLA Modules:
  0.0 326.6 jit_solution(1266805385866443777)
XLA Ops:
  9.8 3.0 collective-permute-start.1
  18.1 2.9 collective-permute-start.7
  22.6 3.6 %all-to-all-start = ((bf16[8,128,512]{2,1,0:T(8,128)(2,1)}), bf16[8,128,512]{2,1,0:T(8,128)(2,1)S(1)}, u32[]{:S(2)}, u32[]{:S(2)}) async-start(bf16[8,128,512]{2,1,0:T(8,128)(2,1)} %bitcast.206), calls=%async_computation | async-start | bytes 2097152 | tf_op jit(solution)/shard_map/all_to_all | solution.py:516
  31.5 4.0 %collective-permute-done.7 = bf16[136,768]{1,0:T(8,128)(2,1)S(1)} collective-permute-done((bf16[136,768]{1,0:T(8,128)(2,1)}, bf16[136,768]{1,0:T(8,128)(2,1)S(1)}, u32[]{:S(2)}, u32[]{:S(2)}) %collective-permute-start.7) | collective-permute-done | bytes 208928 | tf_op jit(solution)/shard_map/ppermute | solution.py:63
  39.4 11.7 %collective-permute-done.3 = bf16[240,512]{1,0:T(8,128)(2,1)S(1)} collective-permute-done((bf16[240,512]{1,0:T(8,128)(2,1)S(1)}, bf16[240,512]{1,0:T(8,128)(2,1)S(1)}, u32[]{:S(2)}, u32[]{:S(2)}) %collective-permute-start.3) | collective-permute-done | bytes 245792 | tf_op jit(solution)/shard_map/ppermute | solution.py:63
  60.4 12.0 %attend.1 = (bf16[3,320,768]{2,1,0:T(8,128)(2,1)}, bf16[3,320,1024]{2,1,0:T(8,128)(2,1)}, bf16[240,256]{1,0:T(8,128)(2,1)}, bf16[240,256]{1,0:T(8,128)(2,1)}, bf...) custom-call(s32[4]{0:T(128)} %pad_add_fusion.2.meta, bf16[4,3,80,1024]{3,2,1,0:T(8,128)(2,1)} %bitcast.212, ...), custom_call_target="tpu_custom_call" | custom-call | flops 2088960 | bytes 7296 | tf_op jit(solution)/shard_map/attend/pallas_call | solution.py:169
  74.1 2.6 collective-permute-start.10
  78.9 7.4 %collective-permute-done.10.c2 = bf16[240,256]{1,0:T(8,128)(2,1)S(1)} collective-permute-done((bf16[240,256]{1,0:T(8,128)(2,1)}, bf16[240,256]{1,0:T(8,128)(2,1)S(1)}, u32[]{:S(2)}, u32[]{:S(2)}) %collective-permute-start.10) | collective-permute-done | bytes 122912 | tf_op jit(solution)/shard_map/ppermute | solution.py:67
  87.1 4.3 %project.1 = (f32[240,1024]{1,0:T(8,128)}, bf16[240,1024]{1,0:T(8,128)(2,1)}) custom-call(s32[4]{0:T(128)} %pad_add_fusion.2.meta, bf16[240,256]{1,0:T(8,128)(2,1)} %get-tuple-element.64.c0, bf16[240,256]{1,0:T(8,128)(2,1)} %copy-done.29, bf16[240,256]{1,0:T(8,128)(2,1)} %copy-done.31, bf16[240,256]{1,0:T(8,128)(2,1)} %copy-done.33, ...), custom_call_target="tpu_custom_call" | custom-call | flops 491520 | bytes 4448 | tf_op jit(solution)/shard_map/project/pallas_call | solution.py:274
  93.4 9.1 %collective-permute-done.13 = bf16[240,1024]{1,0:T(8,128)(2,1)S(1)} collective-permute-done((bf16[240,1024]{1,0:T(8,128)(2,1)}, bf16[240,1024]{1,0:T(8,128)(2,1)S(1)}, u32[]{:S(2)}, u32[]{:S(2)}) %collective-permute-start.13) | collective-permute-done | bytes 491552 | tf_op jit(solution)/shard_map/ppermute | solution.py:63
  105.2 3.6 %collective-permute-done.15 = bf16[240,512]{1,0:T(8,128)(2,1)S(1)} collective-permute-done((bf16[240,512]{1,0:T(8,128)(2,1)S(1)}, bf16[240,512]{1,0:T(8,128)(2,1)S(1)}, u32[]{:S(2)}, u32[]{:S(2)}) %collective-permute-start.15) | collective-permute-done | bytes 245792 | tf_op jit(solution)/shard_map/ppermute | solution.py:63
  108.8 2.5 collective-permute-done.14
  112.9 2.8 collective-permute-done.16.normed.normed_o
  117.1 6.1 %feed.3 = (bf16[4,240,512]{2,1,0:T(8,128)(2,1)}, bf16[4,240,512]{2,1,0:T(8,128)(2,1)}, bf16[4,240,1024]{2,1,0:T(8,128)(2,1)}) custom-call(bf16[4,240,1024]{2,1,0:T(8,128)(2,1)} %copy-done.4, f32[4,240,512]{2,1,0:T(8,128)} %fusion.6.above, bf16[1024,512]{1,0:T(8,128)(2,1)} %bitcast.209, f32[1,512]{1,0:T(1,128)} %bitcast.252), custom_call_target="tpu_custom_call" | custom-call | flops 1966080 | bytes 8704 | tf_op jit(solution)/shard_map/feed/pallas_call | solution.py:310
  123.3 6.1 %feed.2 = (bf16[4,240,512]{2,1,0:T(8,128)(2,1)}, bf16[4,240,512]{2,1,0:T(8,128)(2,1)}, bf16[4,240,1024]{2,1,0:T(8,128)(2,1)}) custom-call(bf16[4,240,1024]{2,1,0:T(8,128)(2,1)} %copy-done.1, f32[4,240,512]{2,1,0:T(8,128)} %fusion.8.above, bf16[1024,512]{1,0:T(8,128)(2,1)} %bitcast.210, f32[1,512]{1,0:T(1,128)} %bitcast.253), custom_call_target="tpu_custom_call" | custom-call | flops 1966080 | bytes 8704 | tf_op jit(solution)/shard_map/feed/pallas_call | solution.py:310
  129.5 3.5 %fusion.18 = (bf16[240,1024]{1,0:T(8,128)(2,1)}, bf16[240,1024]{1,0:T(8,128)(2,1)}, bf16[240,1024]{1,0:T(8,128)(2,1)}) fusion(bf16[4,240,1024]{2,1,0:T(8,128)(2,1)S(1)} %collective-permute-done.17.g1, bf16[4,240,1024]{2,1,0:T(8,128)(2,1)} %get-tuple-element.71.g0), kind=kLoop, calls=%fused_computation.79 | loop fusion | flops 2949120 | bytes 4423680 | tf_op jit(solution)/shard_map/convert_element_type | solution.py:71
  136.5 13.0 %feed_grads.1 = (bf16[4,240,1024]{2,1,0:T(8,128)(2,1)}, bf16[4,240,1024]{2,1,0:T(8,128)(2,1)}, bf16[528,1024]{1,0:T(8,128)(2,1)}, bf16[1024,512]{1,0:T(8,128)(2,1)}) custom-call(bf16[4,240,512]{2,1,0:T(8,128)(2,1)} %get-tuple-element.74.act_e, bf16[4,240,512]{2,1,0:T(8,128)(2,1)} %get-tuple-element.75.act_o, bf16[4,240,512]{2,1,0:T(8,128)(2,1)} %get-tuple-element.76.grad_e, ...), custom_call_target="tpu_custom_call" | custom-call | flops 5898240 | bytes 18432 | tf_op jit(solution)/shard_map/feed_grads/pallas_call | solution.py:360
  153.1 5.0 %collective-permute-done.19.gy = bf16[240,1024]{1,0:T(8,128)(2,1)S(1)} collective-permute-done((bf16[240,1024]{1,0:T(8,128)(2,1)}, bf16[240,1024]{1,0:T(8,128)(2,1)S(1)}, u32[]{:S(2)}, u32[]{:S(2)}) %collective-permute-start.19) | collective-permute-done | bytes 491552 | tf_op jit(solution)/shard_map/ppermute | solution.py:63
  159.7 6.0 %middle.1 = (f32[240,1024]{1,0:T(8,128)}, bf16[240,1024]{1,0:T(8,128)(2,1)}, f32[4,1024]{1,0:T(4,128)}, bf16[240,256]{1,0:T(8,128)(2,1)}, bf16[240,256]{1,0:T(8,...) custom-call(s32[4]{0:T(128)} %pad_add_fusion.2.meta, bf16[4,240,1024]{2,1,0:T(8,128)(2,1)} %get-tuple-element.71.g0, ...), custom_call_target="tpu_custom_call" | custom-call | flops 491520 | bytes 8288 | tf_op jit(solution)/shard_map/middle/pallas_call | solution.py:405
  173.0 16.3 %collective-permute-done.21.d1 = bf16[240,256]{1,0:T(8,128)(2,1)S(1)} collective-permute-done((bf16[240,256]{1,0:T(8,128)(2,1)}, bf16[240,256]{1,0:T(8,128)(2,1)S(1)}, u32[]{:S(2)}, u32[]{:S(2)}) %collective-permute-start.21) | collective-permute-done | bytes 122912 | tf_op jit(solution)/shard_map/ppermute | solution.py:67
  189.3 3.1 collective-permute-done.23.d3
  193.7 14.5 %attend_back.1 = (bf16[3,320,768]{2,1,0:T(8,128)(2,1)}, bf16[2,240,1024]{2,1,0:T(8,128)(2,1)}, bf16[2,240,1024]{2,1,0:T(8,128)(2,1)}, f32[8,1024]{1,0:T(8,128)}) custom-call(s32[4]{0:T(128)} %pad_add_fusion.2.meta, bf16[4,3,80,1024]{3,2,1,0:T(8,128)(2,1)} %bitcast.213, bf16[240,256]{1,0:T(8,128)(2,1)} %get-tuple-element.80.d0, bf16[240,256]{1,0:T(8,128)(2,1)} %copy-done.25, ...), custom_call_target="tpu_custom_call" | custom-call | flops 3010560 | bytes 8736 | tf_op jit(solution)/shard_map/attend_back/pallas_call | solution.py:240
  209.7 3.8 %bitcast_convert_fusion = bf16[1024,768]{1,0:T(8,128)(2,1)S(1)} fusion(bf16[3,320,1024]{2,1,0:T(8,128)(2,1)} %get-tuple-element.69, bf16[3,320,768]{2,1,0:T(8,128)(2,1)} %get-tuple-element.88), kind=kOutput, calls=%fused_computation.2 | convolution fusion | flops 1510735872 | bytes 5013504 | tf_op jit(solution)/shard_map/dot_general | solution.py:43
  222.4 16.0 %collective-permute-done.27 = bf16[240,1024]{1,0:T(8,128)(2,1)S(1)} collective-permute-done((bf16[240,1024]{1,0:T(8,128)(2,1)S(1)}, bf16[240,1024]{1,0:T(8,128)(2,1)S(1)}, u32[]{:S(2)}, u32[]{:S(2)}) %collective-permute-start.27) | collective-permute-done | bytes 491552 | tf_op jit(solution)/shard_map/ppermute | solution.py:67
  243.8 2.5 collective-permute-start.32
  252.3 4.5 %collective-permute-done.35 = bf16[136,1024]{1,0:T(8,128)(2,1)S(1)} collective-permute-done((bf16[136,1024]{1,0:T(8,128)(2,1)S(1)}, bf16[136,1024]{1,0:T(8,128)(2,1)S(1)}, u32[]{:S(2)}, u32[]{:S(2)}) %collective-permute-start.35) | collective-permute-done | bytes 278560 | tf_op jit(solution)/shard_map/ppermute | solution.py:63
  258.4 3.6 %collective-permute-done.34 = bf16[136,1024]{1,0:T(8,128)(2,1)S(1)} collective-permute-done((bf16[136,1024]{1,0:T(8,128)(2,1)S(1)}, bf16[136,1024]{1,0:T(8,128)(2,1)S(1)}, u32[]{:S(2)}, u32[]{:S(2)}) %collective-permute-start.34) | collective-permute-done | bytes 278560 | tf_op jit(solution)/shard_map/ppermute | solution.py:63
  264.2 5.0 %collective-permute-done.32.far = bf16[240,1024]{1,0:T(8,128)(2,1)S(1)} collective-permute-done((bf16[240,1024]{1,0:T(8,128)(2,1)}, bf16[240,1024]{1,0:T(8,128)(2,1)S(1)}, u32[]{:S(2)}, u32[]{:S(2)}) %collective-permute-start.32) | collective-permute-done | bytes 491552 | tf_op jit(solution)/shard_map/ppermute | solution.py:67
  276.5 2.9 fusion.12
  282.9 4.1 %finish.1 = bf16[240,1024]{1,0:T(8,128)(2,1)} custom-call(bf16[240,1024]{1,0:T(8,128)(2,1)} %bitcast.215, bf16[2,240,1024]{2,1,0:T(8,128)(2,1)} %get-tuple-element.90.mine, bf16[240,1024]{1,0:T(8,128)(2,1)} %copy-done.22, bf16[240,1024]{1,0:T(8,128)(2,1)} %copy-done.18, f32[240,1024]{1,0:T(8,128)} %get-tuple-element.111.hidden_grad, f32[6,1024]{1,0:T(8,128)} %bitcast.242), custom_call_target="tpu_custom_call" | custom-call | flops 4800 | bytes 2880 | tf_op jit(solution)/shard_map/finish/pallas_call | solution.py:434
  287.0 8.2 %collective-permute-done.36 = bf16[136,1792]{1,0:T(8,128)(2,1)S(1)} collective-permute-done((bf16[136,1792]{1,0:T(8,128)(2,1)S(1)}, bf16[136,1792]{1,0:T(8,128)(2,1)S(1)}, u32[]{:S(2)}, u32[]{:S(2)}) %collective-permute-start.36) | collective-permute-done | bytes 487456 | tf_op jit(solution)/shard_map/ppermute | solution.py:67
  296.3 4.6 %collective-permute-done.47 = bf16[8,128,256]{2,1,0:T(8,128)(2,1)S(1)} collective-permute-done((bf16[8,128,256]{2,1,0:T(8,128)(2,1)S(1)}, bf16[8,128,256]{2,1,0:T(8,128)(2,1)S(1)}, u32[]{:S(2)}, u32[]{:S(2)}) %collective-permute-start.47) | collective-permute-done | bytes 524320 | tf_op jit(solution)/shard_map/ppermute | solution.py:67
  (286 shorter events, 113.4 us)
Async XLA Ops:
  7.2 53.2 %all-gather.6.cloned.1.call-start = ((), (), s32[]{:S(2)}) async-start(), calls=%async_computation.3 | async-start | bytes 2457600 | tf_op jit(solution)/shard_map/all_gather | solution.py:479
  9.8 25.8 %collective-permute-start.1 = (bf16[240,1024]{1,0:T(8,128)(2,1)S(1)}, bf16[240,1024]{1,0:T(8,128)(2,1)S(1)}, u32[]{:S(2)}, u32[]{:S(2)}) collective-permute-start(bf16[240,1024]{1,0:T(8,128)(2,1)S(1)} %bitcast.216), channel_id=1, source_target_pairs={{0,16},{4,20},{8,24},{12,28},{16,0},{20,4},{24,8},{28,12},{1,17},{... | collective-permute-start | bytes 1474568 | tf_op jit(solution)/shard_map/ppermute | solution.py:63
  12.9 24.9 %collective-permute-start = (bf16[240,1024]{1,0:T(8,128)(2,1)S(1)}, bf16[240,1024]{1,0:T(8,128)(2,1)S(1)}, u32[]{:S(2)}, u32[]{:S(2)}) collective-permute-start(bf16[240,1024]{1,0:T(8,128)(2,1)S(1)} %bitcast.217), channel_id=1, source_target_pairs={{0,8},{4,12},{8,0},{12,4},{16,24},{20,28},{24,16},{28,20},{1,9},{5... | collective-permute-start | bytes 1474568 | tf_op jit(solution)/shard_map/ppermute | solution.py:63
  18.0 13.5 %collective-permute-start.5 = (bf16[136,768]{1,0:T(8,128)(2,1)}, bf16[136,768]{1,0:T(8,128)(2,1)S(1)}, u32[]{:S(2)}, u32[]{:S(2)}) collective-permute-start(bf16[136,768]{1,0:T(8,128)(2,1)} %get-tuple-element.207), channel_id=1, source_target_pairs={{0,8},{4,12},{8,0},{12,4},{16,24},{20,28},{24,16},{28,20},{1,9},{5... | collective-permute-start | bytes 626696 | tf_op jit(solution)/shard_map/ppermute | solution.py:63
  18.1 17.4 %collective-permute-start.7 = (bf16[136,768]{1,0:T(8,128)(2,1)}, bf16[136,768]{1,0:T(8,128)(2,1)S(1)}, u32[]{:S(2)}, u32[]{:S(2)}) collective-permute-start(bf16[136,768]{1,0:T(8,128)(2,1)} %get-tuple-element.207), channel_id=1, source_target_pairs={{0,24},{4,28},{8,16},{12,20},{16,8},{20,12},{24,0},{28,4},{1,25},{... | collective-permute-start | bytes 626696 | tf_op jit(solution)/shard_map/ppermute | solution.py:63
  22.6 37.8 %all-to-all-start = ((bf16[8,128,512]{2,1,0:T(8,128)(2,1)}), bf16[8,128,512]{2,1,0:T(8,128)(2,1)S(1)}, u32[]{:S(2)}, u32[]{:S(2)}) async-start(bf16[8,128,512]{2,1,0:T(8,128)(2,1)} %bitcast.206), calls=%async_computation | async-start | bytes 2097152 | tf_op jit(solution)/shard_map/all_to_all | solution.py:516
  26.2 60.2 %all-gather.4.cloned.1.call-start = ((), (), s32[]{:S(2)}) async-start(), calls=%async_computation.1 | async-start | bytes 2359296 | tf_op jit(solution)/shard_map/all_gather | solution.py:511
  26.9 215.4 %all-reduce.13.cloned.1.call-start = ((), (), s32[]{:S(2)}) async-start(), calls=%async_computation.2 | async-start | bytes 2162688 | tf_op jit(solution)/shard_map/psum | solution.py:565
  35.6 19.3 %collective-permute-start.8 = (bf16[4,136,768]{2,1,0:T(8,128)(2,1)S(1)}, bf16[4,136,768]{2,1,0:T(8,128)(2,1)S(1)}, u32[]{:S(2)}, u32[]{:S(2)}) collective-permute-start(bf16[4,136,768]{2,1,0:T(8,128)(2,1)S(1)} %pad_maximum_fusion.2), channel_id=1, source_target_pairs={{0,4},{4,0},{8,12},{12,8},{16,20},{20,16},{24,28},{28,24},{1,5},{5... | collective-permute-start | bytes 2506760 | tf_op jit(solution)/shard_map/ppermute | solution.py:63
  35.7 15.3 %collective-permute-start.3 = (bf16[240,512]{1,0:T(8,128)(2,1)S(1)}, bf16[240,512]{1,0:T(8,128)(2,1)S(1)}, u32[]{:S(2)}, u32[]{:S(2)}) collective-permute-start(bf16[240,512]{1,0:T(8,128)(2,1)S(1)} %slice.277), channel_id=1, source_target_pairs={{0,8},{4,12},{8,0},{12,4},{16,24},{20,28},{24,16},{28,20},{1,9},{5... | collective-permute-start | bytes 737288 | tf_op jit(solution)/shard_map/ppermute | solution.py:63
  133.0 20.1 %collective-permute-start.20 = (bf16[240,1024]{1,0:T(8,128)(2,1)}, bf16[240,1024]{1,0:T(8,128)(2,1)S(1)}, u32[]{:S(2)}, u32[]{:S(2)}) collective-permute-start(bf16[240,1024]{1,0:T(8,128)(2,1)} %get-tuple-element.154), channel_id=1, source_target_pairs={{0,24},{4,28},{8,16},{12,20},{16,8},{20,12},{24,0},{28,4},{1,25},{... | collective-permute-start | bytes 1474568 | tf_op jit(solution)/shard_map/ppermute | solution.py:63
  134.2 24.0 %collective-permute-start.19 = (bf16[240,1024]{1,0:T(8,128)(2,1)}, bf16[240,1024]{1,0:T(8,128)(2,1)S(1)}, u32[]{:S(2)}, u32[]{:S(2)}) collective-permute-start(bf16[240,1024]{1,0:T(8,128)(2,1)} %get-tuple-element.155), channel_id=1, source_target_pairs={{0,16},{4,20},{8,24},{12,28},{16,0},{20,4},{24,8},{28,12},{1,17},{... | collective-permute-start | bytes 1474568 | tf_op jit(solution)/shard_map/ppermute | solution.py:63
  134.3 23.8 %collective-permute-start.18 = (bf16[240,1024]{1,0:T(8,128)(2,1)}, bf16[240,1024]{1,0:T(8,128)(2,1)S(1)}, u32[]{:S(2)}, u32[]{:S(2)}) collective-permute-start(bf16[240,1024]{1,0:T(8,128)(2,1)} %get-tuple-element.156), channel_id=1, source_target_pairs={{0,8},{4,12},{8,0},{12,4},{16,24},{20,28},{24,16},{28,20},{1,9},{5... | collective-permute-start | bytes 1474568 | tf_op jit(solution)/shard_map/ppermute | solution.py:63
  151.6 40.8 %collective-permute-start.24 = (bf16[1024,256]{1,0:T(8,128)(2,1)}, bf16[1024,256]{1,0:T(8,128)(2,1)}, u32[]{:S(2)}, u32[]{:S(2)}) collective-permute-start(bf16[1024,256]{1,0:T(8,128)(2,1)} %get-tuple-element.174), channel_id=1, source_target_pairs={{0,1},{1,0},{2,3},{3,2},{4,5},{5,4},{6,7},{7,6},{8,9},{9,8},{10,11... | collective-permute-start | bytes 1572872 | tf_op jit(solution)/shard_map/ppermute | solution.py:67
  166.4 22.9 %collective-permute-start.21 = (bf16[240,256]{1,0:T(8,128)(2,1)}, bf16[240,256]{1,0:T(8,128)(2,1)S(1)}, u32[]{:S(2)}, u32[]{:S(2)}) collective-permute-start(bf16[240,256]{1,0:T(8,128)(2,1)} %get-tuple-element.81), channel_id=1, source_target_pairs={{0,1},{1,0},{2,3},{3,2},{4,5},{5,4},{6,7},{7,6},{8,9},{9,8},{10,11... | collective-permute-start | bytes 368648 | tf_op jit(solution)/shard_map/ppermute | solution.py:67
  167.9 21.4 %collective-permute-start.22 = (bf16[240,256]{1,0:T(8,128)(2,1)}, bf16[240,256]{1,0:T(8,128)(2,1)S(1)}, u32[]{:S(2)}, u32[]{:S(2)}) collective-permute-start(bf16[240,256]{1,0:T(8,128)(2,1)} %get-tuple-element.82), channel_id=1, source_target_pairs={{0,2},{1,3},{2,0},{3,1},{4,6},{5,7},{6,4},{7,5},{8,10},{9,11},{10,... | collective-permute-start | bytes 368648 | tf_op jit(solution)/shard_map/ppermute | solution.py:67
  169.5 22.9 %collective-permute-start.23 = (bf16[240,256]{1,0:T(8,128)(2,1)}, bf16[240,256]{1,0:T(8,128)(2,1)S(1)}, u32[]{:S(2)}, u32[]{:S(2)}) collective-permute-start(bf16[240,256]{1,0:T(8,128)(2,1)} %get-tuple-element.83), channel_id=1, source_target_pairs={{0,3},{1,2},{2,1},{3,0},{4,7},{5,6},{6,5},{7,4},{8,11},{9,10},{10,... | collective-permute-start | bytes 368648 | tf_op jit(solution)/shard_map/ppermute | solution.py:67
  215.6 25.9 %collective-permute-start.28 = (bf16[1024,256]{1,0:T(8,128)(2,1)S(1)}, bf16[1024,256]{1,0:T(8,128)(2,1)S(1)}, u32[]{:S(2)}, u32[]{:S(2)}) collective-permute-start(bf16[1024,256]{1,0:T(8,128)(2,1)S(1)} %add_convert_fusion.3), channel_id=1, source_target_pairs={{0,2},{1,3},{2,0},{3,1},{4,6},{5,7},{6,4},{7,5},{8,10},{9,11},{10,... | collective-permute-start | bytes 1572872 | tf_op jit(solution)/shard_map/ppermute | solution.py:67
  216.6 21.8 %collective-permute-start.27 = (bf16[240,1024]{1,0:T(8,128)(2,1)S(1)}, bf16[240,1024]{1,0:T(8,128)(2,1)S(1)}, u32[]{:S(2)}, u32[]{:S(2)}) collective-permute-start(bf16[240,1024]{1,0:T(8,128)(2,1)S(1)} %get-tuple-element.176), channel_id=1, source_target_pairs={{0,1},{1,0},{2,3},{3,2},{4,5},{5,4},{6,7},{7,6},{8,9},{9,8},{10,11... | collective-permute-start | bytes 1474568 | tf_op jit(solution)/shard_map/ppermute | solution.py:67
  218.4 58.0 %collective-permute-start.41 = (bf16[4,240,1024]{2,1,0:T(8,128)(2,1)}, bf16[4,240,1024]{2,1,0:T(8,128)(2,1)}, u32[]{:S(2)}, u32[]{:S(2)}) collective-permute-start(bf16[4,240,1024]{2,1,0:T(8,128)(2,1)} %get-tuple-element.104), channel_id=1, source_target_pairs={{0,4},{4,0},{8,12},{12,8},{16,20},{20,16},{24,28},{28,24},{1,5},{5... | collective-permute-start | bytes 5898248 | tf_op jit(solution)/shard_map/ppermute | solution.py:63
  219.6 24.2 %collective-permute-start.31 = (bf16[136,768]{1,0:T(8,128)(2,1)}, bf16[136,768]{1,0:T(8,128)(2,1)}, u32[]{:S(2)}, u32[]{:S(2)}) collective-permute-start(bf16[136,768]{1,0:T(8,128)(2,1)} %get-tuple-element.186), channel_id=1, source_target_pairs={{0,24},{4,28},{8,16},{12,20},{16,8},{20,12},{24,0},{28,4},{1,25},{... | collective-permute-start | bytes 626696 | tf_op jit(solution)/shard_map/ppermute | solution.py:63
  221.6 24.7 %collective-permute-start.30 = (bf16[136,768]{1,0:T(8,128)(2,1)}, bf16[136,768]{1,0:T(8,128)(2,1)}, u32[]{:S(2)}, u32[]{:S(2)}) collective-permute-start(bf16[136,768]{1,0:T(8,128)(2,1)} %get-tuple-element.187), channel_id=1, source_target_pairs={{0,16},{4,20},{8,24},{12,28},{16,0},{20,4},{24,8},{28,12},{1,17},{... | collective-permute-start | bytes 626696 | tf_op jit(solution)/shard_map/ppermute | solution.py:63
  243.8 25.4 %collective-permute-start.32 = (bf16[240,1024]{1,0:T(8,128)(2,1)}, bf16[240,1024]{1,0:T(8,128)(2,1)S(1)}, u32[]{:S(2)}, u32[]{:S(2)}) collective-permute-start(bf16[240,1024]{1,0:T(8,128)(2,1)} %add_convert_fusion.4), channel_id=1, source_target_pairs={{0,2},{1,3},{2,0},{3,1},{4,6},{5,7},{6,4},{7,5},{8,10},{9,11},{10,... | collective-permute-start | bytes 1474568 | tf_op jit(solution)/shard_map/ppermute | solution.py:67
  247.8 14.2 %collective-permute-start.34 = (bf16[136,1024]{1,0:T(8,128)(2,1)S(1)}, bf16[136,1024]{1,0:T(8,128)(2,1)S(1)}, u32[]{:S(2)}, u32[]{:S(2)}) collective-permute-start(bf16[136,1024]{1,0:T(8,128)(2,1)S(1)} %get-tuple-element.169), channel_id=1, source_target_pairs={{0,16},{4,20},{8,24},{12,28},{16,0},{20,4},{24,8},{28,12},{1,17},{... | collective-permute-start | bytes 835592 | tf_op jit(solution)/shard_map/ppermute | solution.py:63
  248.6 14.2 %collective-permute-start.33 = (bf16[136,1024]{1,0:T(8,128)(2,1)S(1)}, bf16[136,1024]{1,0:T(8,128)(2,1)S(1)}, u32[]{:S(2)}, u32[]{:S(2)}) collective-permute-start(bf16[136,1024]{1,0:T(8,128)(2,1)S(1)} %get-tuple-element.170), channel_id=1, source_target_pairs={{0,8},{4,12},{8,0},{12,4},{16,24},{20,28},{24,16},{28,20},{1,9},{5... | collective-permute-start | bytes 835592 | tf_op jit(solution)/shard_map/ppermute | solution.py:63
  256.8 25.4 %collective-permute-start.45 = (bf16[240,1024]{1,0:T(8,128)(2,1)S(1)}, bf16[240,1024]{1,0:T(8,128)(2,1)S(1)}, u32[]{:S(2)}, u32[]{:S(2)}) collective-permute-start(bf16[240,1024]{1,0:T(8,128)(2,1)S(1)} %copy-done.24), channel_id=1, source_target_pairs={{0,1},{1,0},{2,3},{3,2},{4,5},{5,4},{6,7},{7,6},{8,9},{9,8},{10,11... | collective-permute-start | bytes 1474568 | tf_op jit(solution)/shard_map/ppermute | solution.py:67
  271.3 23.9 %collective-permute-start.36 = (bf16[136,1792]{1,0:T(8,128)(2,1)S(1)}, bf16[136,1792]{1,0:T(8,128)(2,1)S(1)}, u32[]{:S(2)}, u32[]{:S(2)}) collective-permute-start(bf16[136,1792]{1,0:T(8,128)(2,1)S(1)} %pad_maximum_fusion.7), channel_id=1, source_target_pairs={{0,2},{1,3},{2,0},{3,1},{4,6},{5,7},{6,4},{7,5},{8,10},{9,11},{10,... | collective-permute-start | bytes 1462280 | tf_op jit(solution)/shard_map/ppermute | solution.py:67
  275.3 25.7 %collective-permute-start.47 = (bf16[8,128,256]{2,1,0:T(8,128)(2,1)S(1)}, bf16[8,128,256]{2,1,0:T(8,128)(2,1)S(1)}, u32[]{:S(2)}, u32[]{:S(2)}) collective-permute-start(bf16[8,128,256]{2,1,0:T(8,128)(2,1)S(1)} %bitcast.225), channel_id=1, source_target_pairs={{0,1},{1,0},{2,3},{3,2},{4,5},{5,4},{6,7},{7,6},{8,9},{9,8},{10,11... | collective-permute-start | bytes 1572872 | tf_op jit(solution)/shard_map/ppermute | solution.py:67
  279.3 30.3 %collective-permute-start.42 = (bf16[240,1024]{1,0:T(8,128)(2,1)}, bf16[240,1024]{1,0:T(8,128)(2,1)}, u32[]{:S(2)}, u32[]{:S(2)}) collective-permute-start(bf16[240,1024]{1,0:T(8,128)(2,1)} %get-tuple-element.159), channel_id=1, source_target_pairs={{0,8},{4,12},{8,0},{12,4},{16,24},{20,28},{24,16},{28,20},{1,9},{5... | collective-permute-start | bytes 1474568 | tf_op jit(solution)/shard_map/ppermute | solution.py:63
  280.8 28.8 %collective-permute-start.44 = (bf16[240,1024]{1,0:T(8,128)(2,1)}, bf16[240,1024]{1,0:T(8,128)(2,1)}, u32[]{:S(2)}, u32[]{:S(2)}) collective-permute-start(bf16[240,1024]{1,0:T(8,128)(2,1)} %get-tuple-element.160), channel_id=1, source_target_pairs={{0,24},{4,28},{8,16},{12,20},{16,8},{20,12},{24,0},{28,4},{1,25},{... | collective-permute-start | bytes 1474568 | tf_op jit(solution)/shard_map/ppermute | solution.py:63
  282.2 27.5 %collective-permute-start.43 = (bf16[240,1024]{1,0:T(8,128)(2,1)}, bf16[240,1024]{1,0:T(8,128)(2,1)}, u32[]{:S(2)}, u32[]{:S(2)}) collective-permute-start(bf16[240,1024]{1,0:T(8,128)(2,1)} %get-tuple-element.161), channel_id=1, source_target_pairs={{0,16},{4,20},{8,24},{12,28},{16,0},{20,4},{24,8},{28,12},{1,17},{... | collective-permute-start | bytes 1474568 | tf_op jit(solution)/shard_map/ppermute | solution.py:63
  296.3 18.5 %collective-permute-start.46 = (bf16[136,2560]{1,0:T(8,128)(2,1)}, bf16[136,2560]{1,0:T(8,128)(2,1)}, u32[]{:S(2)}, u32[]{:S(2)}) collective-permute-start(bf16[136,2560]{1,0:T(8,128)(2,1)} %pad_maximum_fusion.5), channel_id=1, source_target_pairs={{0,1},{1,0},{2,3},{3,2},{4,5},{5,4},{6,7},{7,6},{8,9},{9,8},{10,11... | collective-permute-start | bytes 2088968 | tf_op jit(solution)/shard_map/ppermute | solution.py:67
  (60 other events, 451.1 us)
Sparse Core Ops, SparseCore 0:
  9.6 46.2 all-gather.5
  57.8 26.7 all-gather.3
  149.7 68.6 all-reduce.12

commit v2 on v1

--- a/solution.py
+++ b/solution.py
@@ -186,7 +186,7 @@
 
 
 def attend_back_kernel(meta, rows_ref, d0, d1, d2, d3, qkv_ref, wq, wk, wv, *refs):
-    dqkv_ref, keep_ref, give_ref, sums_ref = refs
+    dqkv_ref, sums_ref, *outs = refs
     local = rows_ref.shape[2]
     slots = ZS * local
     model = rows_ref.shape[3]
@@ -219,7 +219,7 @@
     total = total + mm_rt(grad[:, 2 * width :], wv[...].reshape(model, width))
     pieces = [total[k * local : (k + 1) * local] for k in range(ZS)]
     for k in range(ZS):
-        (keep_ref, give_ref)[k % 2][k // 2] = chosen(pieces, z ^ k).astype(BF16)
+        outs[k][...] = chosen(pieces, z ^ k).astype(BF16)
     unit, _ = normalize(rows_ref[:, 0].reshape(slots, model).astype(F32))
 
     @pl.when(pl.program_id(0) == 0)
@@ -235,7 +235,7 @@
     _, count, local, model = rows.shape
     slots, width = ZS * local, model // ZS
     packed = pl.BlockSpec((1, slots, 3 * width), lambda s, m: (s, 0, 0))
-    split = pl.BlockSpec((2, local, model), lambda s, m: (0, s, 0))
+    split = pl.BlockSpec((local, model), lambda s, m: (s, 0))
     flops = count * (2 * slots * model * 3 * width + 20 * slots * slots * width)
     return pl.pallas_call(
         attend_back_kernel,
@@ -247,11 +247,11 @@
             + [pl.BlockSpec((local, width), lambda s, m: (s, 0))] * ZS
             + [packed]
             + weight_specs(weights, model // weights.shape[0], width),
-            out_specs=[packed, split, split, block(8, model)],
+            out_specs=[packed, block(8, model)] + [split] * ZS,
         ),
         out_shape=[shape_of((count, slots, 3 * width), BF16)]
-        + [shape_of((2, count * local, model), BF16)] * 2
-        + [shape_of((8, model), F32)],
+        + [shape_of((8, model), F32)]
+        + [shape_of((count * local, model), BF16)] * ZS,
         compiler_params=params(),
         cost_estimate=cost(flops, 2 * count * slots * (2 * model + 7 * width) + 6 * model * width),
     )(meta, rows, *upstream, qkv, weights, weights, weights)
@@ -323,60 +323,78 @@
     )(normed, above, up, bias)
 
 
-def feed_grads_kernel(
-    act_e, act_o, grad_e, grad_o, normed_e, normed_o, cot_e, cot_o, down, out_e, out_o, down_ref, up_ref, down_sum, up_sum, bias_sum
-):
-    rows = act_e.shape[1]
-    width = down.shape[0]
-    act = jnp.concatenate([act_e[0], act_o[0]], axis=0)
-    grad = jnp.concatenate([grad_e[0], grad_o[0]], axis=0)
-    out = mm(act, down[...]).astype(BF16)
-    out_e[0] = out[:rows]
-    out_o[0] = out[rows:]
+def both(even, odd):
+    return jnp.concatenate([even[0], odd[0]], axis=0)
+
+
+def down_grad_kernel(act_e, act_o, grad_e, grad_o, cot_e, cot_o, down_ref, down_sum, bias_sum):
+    width = act_e.shape[2]
 
     @pl.when(pl.program_id(0) == 0)
     def _():
         down_sum[...] = jnp.zeros_like(down_sum)
-        up_sum[...] = jnp.zeros_like(up_sum)
         bias_sum[...] = jnp.zeros_like(bias_sum)
 
-    down_sum[...] += mm_lt(act, jnp.concatenate([cot_e[0], cot_o[0]], axis=0))
-    up_sum[...] += mm_lt(jnp.concatenate([normed_e[0], normed_o[0]], axis=0), grad)
-    bias_sum[0:1, :width] += jnp.sum(grad.astype(F32), axis=0, keepdims=True)
+    down_sum[...] += mm_lt(both(act_e, act_o), both(cot_e, cot_o))
+    bias_sum[0:1, :width] += jnp.sum(both(grad_e, grad_o).astype(F32), axis=0, keepdims=True)
 
     @pl.when(pl.program_id(0) == pl.num_programs(0) - 1)
     def _():
         down_ref[:width] = down_sum[...].astype(BF16)
         down_ref[width:] = bias_sum[...].astype(BF16)
+
+
+def down_gradient(act, grad, cot):
+    _, rows, width = act[0].shape
+    model = cot[0].shape[2]
+    thin = pl.BlockSpec((1, rows, width), lambda i: (i, 0, 0))
+    wide = pl.BlockSpec((1, rows, model), lambda i: (i, 0, 0))
+    return pl.pallas_call(
+        down_grad_kernel,
+        name="down_gradient",
+        grid=(4,),
+        in_specs=[thin] * 4 + [wide] * 2,
+        out_specs=block(width + 16, model),
+        scratch_shapes=[pltpu.VMEM((width, model), F32), pltpu.VMEM((16, model), F32)],
+        out_shape=shape_of((width + 16, model), BF16),
+        compiler_params=params(),
+        cost_estimate=cost(16 * rows * model * width, 16 * rows * (model + 2 * width)),
+    )(*act, *grad, *cot)
+
+
+def feed_grads_kernel(act_e, act_o, grad_e, grad_o, normed_e, normed_o, down, out_e, out_o, up_ref, up_sum):
+    rows = act_e.shape[1]
+    out = mm(both(act_e, act_o), down[...]).astype(BF16)
+    out_e[0] = out[:rows]
+    out_o[0] = out[rows:]
+
+    @pl.when(pl.program_id(0) == 0)
+    def _():
+        up_sum[...] = jnp.zeros_like(up_sum)
+
+    up_sum[...] += mm_lt(both(normed_e, normed_o), both(grad_e, grad_o))
+
+    @pl.when(pl.program_id(0) == pl.num_programs(0) - 1)
+    def _():
         up_ref[...] = up_sum[...].astype(BF16)
 
 
-def feed_grads(act, grad, normed, cot, down):
+def feed_grads(act, grad, normed, down):
     _, rows, width = act[0].shape
     model = down.shape[1]
     thin = pl.BlockSpec((1, rows, width), lambda i: (i, 0, 0))
     wide = pl.BlockSpec((1, rows, model), lambda i: (i, 0, 0))
-    total = 8 * rows
     return pl.pallas_call(
         feed_grads_kernel,
         name="feed_grads",
         grid=(4,),
-        in_specs=[thin] * 4 + [wide] * 4 + [block(width, model)],
-        out_specs=[wide, wide, block(width + 16, model), block(model, width)],
-        scratch_shapes=[
-            pltpu.VMEM((width, model), F32),
-            pltpu.VMEM((model, width), F32),
-            pltpu.VMEM((16, model), F32),
-        ],
-        out_shape=[
-            shape_of((4, rows, model), BF16),
-            shape_of((4, rows, model), BF16),
-            shape_of((width + 16, model), BF16),
-            shape_of((model, width), BF16),
-        ],
+        in_specs=[thin] * 4 + [wide] * 2 + [block(width, model)],
+        out_specs=[wide, wide, block(model, width)],
+        scratch_shapes=[pltpu.VMEM((model, width), F32)],
+        out_shape=[shape_of((4, rows, model), BF16)] * 2 + [shape_of((model, width), BF16)],
         compiler_params=params(),
-        cost_estimate=cost(6 * total * model * width, 2 * total * (3 * model + 2 * width) + 6 * model * width),
-    )(*act, *grad, *normed, *cot, down)
+        cost_estimate=cost(32 * rows * model * width, 16 * rows * (2 * model + 2 * width)),
+    )(*act, *grad, *normed, down)
 
 
 def middle_kernel(meta, g0, g1, gx, gy, gd, hidden, cot, weights, vecs, hidden_grad_ref, grad_ref, sums_ref, d0, d1, d2, d3):
@@ -422,7 +440,7 @@
 
 def finish_kernel(x, mine, near, far, hidden_grad, vecs, out):
     unit, inverse = normalize(x[...].astype(F32))
-    upstream = mine[0].astype(F32) + near[...].astype(F32) + far[...].astype(F32)
+    upstream = mine[...].astype(F32) + near[...].astype(F32) + far[...].astype(F32)
     out[...] = (hidden_grad[...] + norm_back(upstream, unit, inverse, vecs[0:1])).astype(BF16)
 
 
@@ -430,12 +448,11 @@
     rows, model = x.shape
     steps = 3 if rows % 48 == 0 else 1
     part = pl.BlockSpec((rows // steps, model), lambda i: (i, 0))
-    stack = pl.BlockSpec((1, rows // steps, model), lambda i: (0, i, 0))
     return pl.pallas_call(
         finish_kernel,
         name="finish",
         grid=(steps,),
-        in_specs=[part, stack, part, part, part, block(*vecs.shape)],
+        in_specs=[part] * 5 + [block(*vecs.shape)],
         out_specs=part,
         out_shape=shape_of((rows, model), BF16),
         compiler_params=params(),
@@ -537,11 +554,12 @@
         out = lax.dot_general(stack, down, (((2,), (1,)), ((), ())), preferred_element_type=F32)
         return out
 
-    above_even, above_odd = down_back(cot_even), down_back(cot_odd)
-
-    qkv, normed_attn, *context = attend(meta, after(rows, above_even, above_odd, up), weights, vecs, bias_quarter)
+
+    qkv, normed_attn, *context = attend(meta, after(rows, cot_odd, up), weights, vecs, bias_quarter)
     context = [context[0]] + [cross(context[k], k) for k in range(1, ZS)]
+    above_even, above_odd = (down_back(after(part, qkv)) for part in (cot_even, cot_odd))
     own = inputs.reshape(tokens, model)
+    context[0] = after(context[0], above_even, above_odd)
     hidden, normed = project(meta, context, own, proj, vecs)
 
     normed_even = over_chips(normed)
@@ -552,8 +570,9 @@
     sums = [joined(back_even[m], back_core[m]) for m in (1, 2, 3)]
     moved = [swap(part, 2 * m) for m, part in zip((1, 2, 3), sums)]
     act_even = after(act_even, *sums)
-    out_even, out_odd, down_part, up_part = feed_grads(
-        (act_even, act_odd), (grad_even, grad_odd), (normed_even, normed_odd), (cot_even, cot_odd), down
+    down_part = down_gradient((act_even, act_odd), (grad_even, grad_odd), (cot_even, cot_odd))
+    out_even, out_odd, up_part = feed_grads(
+        (act_even, after(act_odd, down_part)), (grad_even, grad_odd), (normed_even, normed_odd), down
     )
     if outer > 1:
         bias_part = rows_over_outer(down_part[feed_width, :feed_width].astype(F32), size)
@@ -601,7 +620,7 @@
     context_grad = [context_grad[0]] + [cross(context_grad[k], k) for k in range(1, ZS)]
     up_half = joined(after(up_keep, *context_grad), cross(up_give, 1))
     up_across = cross(up_half, 2)
-    qkv_grad, mine, give, attn_sums = attend_back(meta, rows, context_grad, after(qkv, up_half), weights)
+    qkv_grad, attn_sums, *parts = attend_back(meta, rows, context_grad, after(qkv, up_half), weights)
 
     qkv_part = mm_lt(normed_attn.reshape(-1, model), qkv_grad.reshape(-1, 3 * width)).astype(BF16)
 
@@ -616,20 +635,20 @@
     else:
         qkv_part = rows_over_outer(qkv_part, size).reshape(4, 2, own_rows, 3 * width)
 
-    near = [cross(give[k], 1) for k in range(2)]
+    near = [cross(parts[k], 1) for k in (1, 3)]
     qkv_both = over_core(qkv_part)
-    proj_both = over_core(proj_part, qkv_both)
-    middle_sum = joined(after(mine[1], proj_both), near[1])
+    down_grad = down_total[:down_rows].astype(F32)
+    proj_both = over_core(proj_part, qkv_both, down_grad)
+    middle_sum = joined(after(parts[2], proj_both), near[1])
     far = cross(middle_sum, 2)
     up_sum = lax.optimization_barrier(joined(after(up_half, middle_sum), up_across))
     up_sum = up_sum.reshape(4, 2, own_rows, half_width)
     pair = jnp.stack([pick(up_sum, core, 1), swap(pick(up_sum, 1 - core, 1), 1)], axis=1)
     up_moved = [swap(pick(pair, chip ^ m), 2 * m) for m in (1, 2, 3)]
-    out_core = swap(after(out_odd, give), 1)
+    out_core = swap(after(out_odd, qkv_grad), 1)
     out_sums = [joined(after(out_even[m], up_sum), out_core[m]) for m in (1, 2, 3)]
     out_moved = [swap(part, 2 * m) for m, part in zip((1, 2, 3), out_sums)]
-    down_grad = after(down_total, qkv_both)[:down_rows].astype(F32)
-    input_grad = finish(own, mine, near[0], far, after(hidden_grad, pair, down_grad, *out_sums), vecs)
+    input_grad = finish(own, parts[0], near[0], far, after(hidden_grad, pair, down_grad, *out_sums), vecs)
     qkv_mine = lax.optimization_barrier(over_team_chips(qkv_both, lambda m: chip ^ m, up_sum))
     proj_mine = over_team_chips(proj_both, chip_at, up_sum)
     lanes = qkv_mine.shape[1]

time: 328 us -> 326 us (level)
  waiting for transfers between devices: 121 us -> 115 us
  matrix products: 10.6 us -> 15.3 us
  local copies, waits for them, and re-layouts: 24.3 us -> 19.6 us
  Pallas kernels: 66.1 us -> 70.4 us
  starting transfers between devices: 54.9 us -> 50.8 us
    ppermute x14, waiting for transfers between devices: 66.5 us -> 52.8 us  [cross(): return lax.ppermute(value, 'seq', [(i, i ^ mask) for i in range(ZS)])]
    ppermute x34, waiting for transfers between devices: 52.7 us -> 60.1 us  [swap(): return lax.ppermute(value, 'fsdp', [(i, i ^ mask) for i in range(size)])]
    pallas_call x0 -> x1, Pallas kernels: none -> 6.79 us  [down_gradient(): pl.pallas_call(down_grad_kernel, name='down_gradient', grid=(4,), in_spec...]
    ppermute x14, starting transfers between devices: 17.7 us -> 11.7 us  [cross(): return lax.ppermute(value, 'seq', [(i, i ^ mask) for i in range(ZS)])]
    unnamed x104 -> x102, local copies, waits for them, and re-layouts: 11.9 us -> 9.18 us
  transfers between devices with their start and end apart: 52 -> 52, of which waited for: 22 -> 22; matrix products, arithmetic and copies ran while one was open for 16% -> 18% of each run, Pallas kernels for 17% -> 18%
where the time goes in v2:
time: 326 us; the launch traced here: 324 us
  waiting for transfers between devices  115 us (35%)
  Pallas kernels  70.4 us (22%)
  starting transfers between devices  50.8 us (16%)
  other arithmetic  38.6 us (12%)
  local copies, waits for them, and re-layouts  19.6 us (6%)
  matrix products  15.3 us (5%)
  between operations  14.9 us (5%)
    ppermute x34, waiting for transfers between devices, swap(): return lax.ppermute(value, 'fsdp', [(i, i ^ mask) for i in range(size)])  60.1 us
    ppermute x14, waiting for transfers between devices, cross(): return lax.ppermute(value, 'seq', [(i, i ^ mask) for i in range(ZS)])  52.8 us
    ppermute x34, starting transfers between devices, swap(): return lax.ppermute(value, 'fsdp', [(i, i ^ mask) for i in range(size)])  35.4 us
    pallas_call x1, Pallas kernels, attend_back(): pl.pallas_call(attend_back_kernel, name='attend_back', grid_spec=pltpu.Pr...  14.6 us
    convert_element_type x8, other arithmetic, joined(): return (first.astype(F32) + second.astype(F32)).astype(BF16)  12.2 us
    pallas_call x2, Pallas kernels, feed(): pl.pallas_call(feed_kernel, name='feed', grid=(count // 2,), in_specs=[wi...  12.2 us
    pallas_call x1, Pallas kernels, attend(): pl.pallas_call(attend_kernel, name='attend', grid_spec=pltpu.PrefetchScal...  12.1 us
    ppermute x14, starting transfers between devices, cross(): return lax.ppermute(value, 'seq', [(i, i ^ mask) for i in range(ZS)])  11.7 us
  transfers between devices with their start and end apart: 52, of which 22 were waited for; matrix products, arithmetic and copies ran while one was open for 18% of the time, Pallas kernels for 18%

profile of v2, /device:TPU:0, one launch (start us, length us, event | category | flops | bytes accessed | tf_op | source)
XLA Modules:
  0.0 324.4 jit_solution(18005141393559758038)
XLA Ops:
  10.0 3.0 collective-permute-start.1
  16.9 2.9 collective-permute-start.7
  21.5 3.6 %all-to-all-start = ((bf16[8,128,512]{2,1,0:T(8,128)(2,1)}), bf16[8,128,512]{2,1,0:T(8,128)(2,1)S(1)}, u32[]{:S(2)}, u32[]{:S(2)}) async-start(bf16[8,128,512]{2,1,0:T(8,128)(2,1)} %bitcast.201), calls=%async_computation | async-start | bytes 2097152 | tf_op jit(solution)/shard_map/all_to_all | solution.py:533
  31.6 4.0 %collective-permute-done.7 = bf16[136,768]{1,0:T(8,128)(2,1)S(1)} collective-permute-done((bf16[136,768]{1,0:T(8,128)(2,1)}, bf16[136,768]{1,0:T(8,128)(2,1)S(1)}, u32[]{:S(2)}, u32[]{:S(2)}) %collective-permute-start.7) | collective-permute-done | bytes 208928 | tf_op jit(solution)/shard_map/ppermute | solution.py:63
  35.8 15.3 %collective-permute-done.3 = bf16[240,512]{1,0:T(8,128)(2,1)S(1)} collective-permute-done((bf16[240,512]{1,0:T(8,128)(2,1)S(1)}, bf16[240,512]{1,0:T(8,128)(2,1)S(1)}, u32[]{:S(2)}, u32[]{:S(2)}) %collective-permute-start.3) | collective-permute-done | bytes 245792 | tf_op jit(solution)/shard_map/ppermute | solution.py:63
  57.1 12.1 %attend.1 = (bf16[3,320,768]{2,1,0:T(8,128)(2,1)}, bf16[3,320,1024]{2,1,0:T(8,128)(2,1)}, bf16[240,256]{1,0:T(8,128)(2,1)}, bf16[240,256]{1,0:T(8,128)(2,1)}, bf...) custom-call(s32[4]{0:T(128)} %pad_add_fusion.2.meta, bf16[4,3,80,1024]{3,2,1,0:T(8,128)(2,1)} %bitcast.207, ...), custom_call_target="tpu_custom_call" | custom-call | flops 2088960 | bytes 7296 | tf_op jit(solution)/shard_map/attend/pallas_call | solution.py:169
  73.7 4.1 %fusion.8.above = f32[4,240,512]{2,1,0:T(8,128)} fusion(bf16[4,240,1024]{2,1,0:T(8,128)(2,1)} %pad_maximum_fusion.cot_e, bf16[512,1024]{1,0:T(8,128)(2,1)S(1)} %copy-done.11), kind=kOutput, calls=%fused_computation.36 | convolution fusion | flops 1006632960 | bytes 4980736 | tf_op jit(solution)/shard_map/dot_general | solution.py:554
  77.8 4.0 %fusion.6.above = f32[4,240,512]{2,1,0:T(8,128)} fusion(bf16[4,240,1024]{2,1,0:T(8,128)(2,1)} %collective-permute-done.4.cot_o, bf16[512,1024]{1,0:T(8,128)(2,1)S(1)} %copy-done.11), kind=kOutput, calls=%fused_computation.34 | convolution fusion | flops 1006632960 | bytes 4980736 | tf_op jit(solution)/shard_map/dot_general | solution.py:554
  84.6 4.3 %project.1 = (f32[240,1024]{1,0:T(8,128)}, bf16[240,1024]{1,0:T(8,128)(2,1)}) custom-call(s32[4]{0:T(128)} %pad_add_fusion.2.meta, bf16[240,256]{1,0:T(8,128)(2,1)} %get-tuple-element.72.c0, bf16[240,256]{1,0:T(8,128)(2,1)} %collective-permute-done.9.c1, bf16[240,256]{1,0:T(8,128)(2,1)} %copy-done.23, bf16[240,256]{1,0:T(8,128)(2,1)} %copy-done.24, ...), custom_call_target="tpu_custom_call" | custom-call | flops 491520 | bytes 4448 | tf_op jit(solution)/shard_map/project/pallas_call | solution.py:274
  91.0 11.6 %collective-permute-done.13 = bf16[240,1024]{1,0:T(8,128)(2,1)S(1)} collective-permute-done((bf16[240,1024]{1,0:T(8,128)(2,1)}, bf16[240,1024]{1,0:T(8,128)(2,1)S(1)}, u32[]{:S(2)}, u32[]{:S(2)}) %collective-permute-start.13) | collective-permute-done | bytes 491552 | tf_op jit(solution)/shard_map/ppermute | solution.py:63
  104.7 5.2 %collective-permute-done.15 = bf16[240,512]{1,0:T(8,128)(2,1)S(1)} collective-permute-done((bf16[240,512]{1,0:T(8,128)(2,1)S(1)}, bf16[240,512]{1,0:T(8,128)(2,1)S(1)}, u32[]{:S(2)}, u32[]{:S(2)}) %collective-permute-start.15) | collective-permute-done | bytes 245792 | tf_op jit(solution)/shard_map/ppermute | solution.py:63
  112.8 2.8 collective-permute-done.16.normed.normed_o
  116.9 6.1 %feed.3 = (bf16[4,240,512]{2,1,0:T(8,128)(2,1)}, bf16[4,240,512]{2,1,0:T(8,128)(2,1)}, bf16[4,240,1024]{2,1,0:T(8,128)(2,1)}) custom-call(bf16[4,240,1024]{2,1,0:T(8,128)(2,1)} %copy-done.3, f32[4,240,512]{2,1,0:T(8,128)} %fusion.6.above, bf16[1024,512]{1,0:T(8,128)(2,1)} %bitcast.204, f32[1,512]{1,0:T(1,128)} %bitcast.245), custom_call_target="tpu_custom_call" | custom-call | flops 1966080 | bytes 8704 | tf_op jit(solution)/shard_map/feed/pallas_call | solution.py:310
  123.1 6.1 %feed.2 = (bf16[4,240,512]{2,1,0:T(8,128)(2,1)}, bf16[4,240,512]{2,1,0:T(8,128)(2,1)}, bf16[4,240,1024]{2,1,0:T(8,128)(2,1)}) custom-call(bf16[4,240,1024]{2,1,0:T(8,128)(2,1)} %copy-done.1, f32[4,240,512]{2,1,0:T(8,128)} %fusion.8.above, bf16[1024,512]{1,0:T(8,128)(2,1)} %bitcast.205, f32[1,512]{1,0:T(1,128)} %bitcast.246), custom_call_target="tpu_custom_call" | custom-call | flops 1966080 | bytes 8704 | tf_op jit(solution)/shard_map/feed/pallas_call | solution.py:310
  129.2 3.6 %fusion.18 = (bf16[240,1024]{1,0:T(8,128)(2,1)}, bf16[240,1024]{1,0:T(8,128)(2,1)}, bf16[240,1024]{1,0:T(8,128)(2,1)S(1)}) fusion(bf16[4,240,1024]{2,1,0:T(8,128)(2,1)S(1)} %collective-permute-done.17.g1, bf16[4,240,1024]{2,1,0:T(8,128)(2,1)} %get-tuple-element.79.g0), kind=kLoop, calls=%fused_computation.79 | loop fusion | flops 2949120 | bytes 4423680 | tf_op jit(solution)/shard_map/convert_element_type | solution.py:71
  136.4 6.8 %down_gradient.1 = bf16[528,1024]{1,0:T(8,128)(2,1)} custom-call(bf16[4,240,512]{2,1,0:T(8,128)(2,1)} %get-tuple-element.82.act_e, bf16[4,240,512]{2,1,0:T(8,128)(2,1)} %get-tuple-element.86.act_o, bf16[4,240,512]{2,1,0:T(8,128)(2,1)} %get-tuple-element.84.grad_e, bf16[4,240,512]{2,1,0:T(8,128)(2,1)} %get-tuple-element.85.grad_o, ...), custom_call_target="tpu_custom_call" | custom-call | flops 1966080 | bytes 7680 | tf_op jit(solution)/shard_map/down_gradient/pallas_call | solution.py:352
  143.2 10.4 %feed_grads.1 = (bf16[4,240,1024]{2,1,0:T(8,128)(2,1)}, bf16[4,240,1024]{2,1,0:T(8,128)(2,1)}, bf16[1024,512]{1,0:T(8,128)(2,1)}) custom-call(bf16[4,240,512]{2,1,0:T(8,128)(2,1)} %get-tuple-element.82.act_e, bf16[4,240,512]{2,1,0:T(8,128)(2,1)} %get-tuple-element.86.act_o, bf16[4,240,512]{2,1,0:T(8,128)(2,1)} %get-tuple-element.84.grad_e, ...), custom_call_target="tpu_custom_call" | custom-call | flops 3932160 | bytes 11520 | tf_op jit(solution)/shard_map/feed_grads/pallas_call | solution.py:387
  159.5 5.9 %middle.1 = (f32[240,1024]{1,0:T(8,128)}, bf16[240,1024]{1,0:T(8,128)(2,1)}, f32[4,1024]{1,0:T(4,128)}, bf16[240,256]{1,0:T(8,128)(2,1)}, bf16[240,256]{1,0:T(8,...) custom-call(s32[4]{0:T(128)} %pad_add_fusion.2.meta, bf16[4,240,1024]{2,1,0:T(8,128)(2,1)} %get-tuple-element.79.g0, ...), custom_call_target="tpu_custom_call" | custom-call | flops 491520 | bytes 8288 | tf_op jit(solution)/shard_map/middle/pallas_call | solution.py:423
  170.6 3.3 %convolution_convert_fusion = bf16[1024,1024]{1,0:T(8,128)(2,1)} fusion(bf16[240,1024]{1,0:T(8,128)(2,1)} %get-tuple-element.99, bf16[240,256]{1,0:T(8,128)(2,1)} %copy-done.24, bf16[240,256]{1,0:T(8,128)(2,1)} %copy-done.23, bf16[240,256]{1,0:T(8,128)(2,1)} %collective-permute-done.9.c1, bf16[240,256]{1,0:T(8,128)(2,1)} %get-tuple-element.72.c0), kind=kOutput, calls=%fused_computation.26 | convolution fusion | flops 506331136 | bytes 3080192 | tf_op jit(solution)/shard_map/dot_general | solution.py:43
  174.3 10.2 %collective-permute-done.21.d1 = bf16[240,256]{1,0:T(8,128)(2,1)S(1)} collective-permute-done((bf16[240,256]{1,0:T(8,128)(2,1)}, bf16[240,256]{1,0:T(8,128)(2,1)S(1)}, u32[]{:S(2)}, u32[]{:S(2)}) %collective-permute-start.21) | collective-permute-done | bytes 122912 | tf_op jit(solution)/shard_map/ppermute | solution.py:67
  184.5 4.5 %collective-permute-done.23.d3 = bf16[240,256]{1,0:T(8,128)(2,1)S(1)} collective-permute-done((bf16[240,256]{1,0:T(8,128)(2,1)}, bf16[240,256]{1,0:T(8,128)(2,1)S(1)}, u32[]{:S(2)}, u32[]{:S(2)}) %collective-permute-start.23) | collective-permute-done | bytes 122912 | tf_op jit(solution)/shard_map/ppermute | solution.py:67
  189.6 14.6 %attend_back.1 = (bf16[3,320,768]{2,1,0:T(8,128)(2,1)}, f32[8,1024]{1,0:T(8,128)}, bf16[240,1024]{1,0:T(8,128)(2,1)}, bf16[240,1024]{1,0:T(8,128)(2,1)}, bf16[24...) custom-call(s32[4]{0:T(128)} %pad_add_fusion.2.meta, bf16[4,3,80,1024]{3,2,1,0:T(8,128)(2,1)} %bitcast.208, ...), custom_call_target="tpu_custom_call" | custom-call | flops 3010560 | bytes 8736 | tf_op jit(solution)/shard_map/attend_back/pallas_call | solution.py:240
  205.7 3.8 %bitcast_convert_fusion = bf16[1024,768]{1,0:T(8,128)(2,1)S(1)} fusion(bf16[3,320,1024]{2,1,0:T(8,128)(2,1)} %get-tuple-element.77, bf16[3,320,768]{2,1,0:T(8,128)(2,1)} %get-tuple-element.96), kind=kOutput, calls=%fused_computation.2 | convolution fusion | flops 1510735872 | bytes 5013504 | tf_op jit(solution)/shard_map/dot_general | solution.py:43
  223.2 15.1 %collective-permute-done.27 = bf16[240,1024]{1,0:T(8,128)(2,1)} collective-permute-done((bf16[240,1024]{1,0:T(8,128)(2,1)}, bf16[240,1024]{1,0:T(8,128)(2,1)}, u32[]{:S(2)}, u32[]{:S(2)}) %collective-permute-start.27) | collective-permute-done | bytes 491552 | tf_op jit(solution)/shard_map/ppermute | solution.py:67
  248.3 5.3 %collective-permute-done.35 = bf16[136,1024]{1,0:T(8,128)(2,1)S(1)} collective-permute-done((bf16[136,1024]{1,0:T(8,128)(2,1)S(1)}, bf16[136,1024]{1,0:T(8,128)(2,1)S(1)}, u32[]{:S(2)}, u32[]{:S(2)}) %collective-permute-start.35) | collective-permute-done | bytes 278560 | tf_op jit(solution)/shard_map/ppermute | solution.py:63
  253.7 5.1 %collective-permute-done.34 = bf16[136,1024]{1,0:T(8,128)(2,1)S(1)} collective-permute-done((bf16[136,1024]{1,0:T(8,128)(2,1)S(1)}, bf16[136,1024]{1,0:T(8,128)(2,1)S(1)}, u32[]{:S(2)}, u32[]{:S(2)}) %collective-permute-start.34) | collective-permute-done | bytes 278560 | tf_op jit(solution)/shard_map/ppermute | solution.py:63
  261.1 6.5 %collective-permute-done.32.far = bf16[240,1024]{1,0:T(8,128)(2,1)S(1)} collective-permute-done((bf16[240,1024]{1,0:T(8,128)(2,1)S(1)}, bf16[240,1024]{1,0:T(8,128)(2,1)S(1)}, u32[]{:S(2)}, u32[]{:S(2)}) %collective-permute-start.32) | collective-permute-done | bytes 491552 | tf_op jit(solution)/shard_map/ppermute | solution.py:67
  270.4 3.4 %collective-permute-done.40 = bf16[2,128,256]{2,1,0:T(8,128)(2,1)S(1)} collective-permute-done((bf16[2,128,256]{2,1,0:T(8,128)(2,1)S(1)}, bf16[2,128,256]{2,1,0:T(8,128)(2,1)S(1)}, u32[]{:S(2)}, u32[]{:S(2)}) %collective-permute-start.40) | collective-permute-done | bytes 131104 | tf_op jit(solution)/shard_map/ppermute | solution.py:63
  274.0 2.9 fusion.12
  280.6 4.1 %finish.1 = bf16[240,1024]{1,0:T(8,128)(2,1)} custom-call(bf16[240,1024]{1,0:T(8,128)(2,1)} %bitcast.210, bf16[240,1024]{1,0:T(8,128)(2,1)} %get-tuple-element.116.mine, bf16[240,1024]{1,0:T(8,128)(2,1)} %copy-done.15, bf16[240,1024]{1,0:T(8,128)(2,1)} %copy-done.13, f32[240,1024]{1,0:T(8,128)} %get-tuple-element.119.hidden_grad, f32[6,1024]{1,0:T(8,128)} %bitcast.234), custom_call_target="tpu_custom_call" | custom-call | flops 4800 | bytes 2880 | tf_op jit(solution)/shard_map/finish/pallas_call | solution.py:451
  284.7 6.2 %collective-permute-done.36 = bf16[136,1792]{1,0:T(8,128)(2,1)S(1)} collective-permute-done((bf16[136,1792]{1,0:T(8,128)(2,1)S(1)}, bf16[136,1792]{1,0:T(8,128)(2,1)S(1)}, u32[]{:S(2)}, u32[]{:S(2)}) %collective-permute-start.36) | collective-permute-done | bytes 487456 | tf_op jit(solution)/shard_map/ppermute | solution.py:67
  291.9 7.3 %collective-permute-done.47 = bf16[8,128,256]{2,1,0:T(8,128)(2,1)S(1)} collective-permute-done((bf16[8,128,256]{2,1,0:T(8,128)(2,1)S(1)}, bf16[8,128,256]{2,1,0:T(8,128)(2,1)S(1)}, u32[]{:S(2)}, u32[]{:S(2)}) %collective-permute-start.47) | collective-permute-done | bytes 524320 | tf_op jit(solution)/shard_map/ppermute | solution.py:67
  (283 shorter events, 105.4 us)
Async XLA Ops:
  7.3 49.8 %all-gather.6.cloned.1.call-start = ((), (), s32[]{:S(2)}) async-start(), calls=%async_computation.3 | async-start | bytes 2457600 | tf_op jit(solution)/shard_map/all_gather | solution.py:496
  8.0 76.6 %all-gather.4.cloned.1.call-start = ((), (), s32[]{:S(2)}) async-start(), calls=%async_computation.1 | async-start | bytes 2359296 | tf_op jit(solution)/shard_map/all_gather | solution.py:528
  10.0 17.2 %collective-permute-start.1 = (bf16[240,1024]{1,0:T(8,128)(2,1)S(1)}, bf16[240,1024]{1,0:T(8,128)(2,1)S(1)}, u32[]{:S(2)}, u32[]{:S(2)}) collective-permute-start(bf16[240,1024]{1,0:T(8,128)(2,1)S(1)} %bitcast.211), channel_id=1, source_target_pairs={{0,16},{4,20},{8,24},{12,28},{16,0},{20,4},{24,8},{28,12},{1,17},{... | collective-permute-start | bytes 1474568 | tf_op jit(solution)/shard_map/ppermute | solution.py:63
  13.0 16.1 %collective-permute-start = (bf16[240,1024]{1,0:T(8,128)(2,1)S(1)}, bf16[240,1024]{1,0:T(8,128)(2,1)S(1)}, u32[]{:S(2)}, u32[]{:S(2)}) collective-permute-start(bf16[240,1024]{1,0:T(8,128)(2,1)S(1)} %bitcast.212), channel_id=1, source_target_pairs={{0,8},{4,12},{8,0},{12,4},{16,24},{20,28},{24,16},{28,20},{1,9},{5... | collective-permute-start | bytes 1474568 | tf_op jit(solution)/shard_map/ppermute | solution.py:63
  16.3 14.3 %collective-permute-start.6 = (bf16[136,768]{1,0:T(8,128)(2,1)}, bf16[136,768]{1,0:T(8,128)(2,1)S(1)}, u32[]{:S(2)}, u32[]{:S(2)}) collective-permute-start(bf16[136,768]{1,0:T(8,128)(2,1)} %get-tuple-element.213), channel_id=1, source_target_pairs={{0,16},{4,20},{8,24},{12,28},{16,0},{20,4},{24,8},{28,12},{1,17},{... | collective-permute-start | bytes 626696 | tf_op jit(solution)/shard_map/ppermute | solution.py:63
  16.8 14.8 %collective-permute-start.5 = (bf16[136,768]{1,0:T(8,128)(2,1)}, bf16[136,768]{1,0:T(8,128)(2,1)S(1)}, u32[]{:S(2)}, u32[]{:S(2)}) collective-permute-start(bf16[136,768]{1,0:T(8,128)(2,1)} %get-tuple-element.213), channel_id=1, source_target_pairs={{0,8},{4,12},{8,0},{12,4},{16,24},{20,28},{24,16},{28,20},{1,9},{5... | collective-permute-start | bytes 626696 | tf_op jit(solution)/shard_map/ppermute | solution.py:63
  16.9 18.7 %collective-permute-start.7 = (bf16[136,768]{1,0:T(8,128)(2,1)}, bf16[136,768]{1,0:T(8,128)(2,1)S(1)}, u32[]{:S(2)}, u32[]{:S(2)}) collective-permute-start(bf16[136,768]{1,0:T(8,128)(2,1)} %get-tuple-element.213), channel_id=1, source_target_pairs={{0,24},{4,28},{8,16},{12,20},{16,8},{20,12},{24,0},{28,4},{1,25},{... | collective-permute-start | bytes 626696 | tf_op jit(solution)/shard_map/ppermute | solution.py:63
  21.5 33.1 %all-to-all-start = ((bf16[8,128,512]{2,1,0:T(8,128)(2,1)}), bf16[8,128,512]{2,1,0:T(8,128)(2,1)S(1)}, u32[]{:S(2)}, u32[]{:S(2)}) async-start(bf16[8,128,512]{2,1,0:T(8,128)(2,1)} %bitcast.201), calls=%async_computation | async-start | bytes 2097152 | tf_op jit(solution)/shard_map/all_to_all | solution.py:533
  25.0 189.4 %all-reduce.13.cloned.1.call-start = ((), (), s32[]{:S(2)}) async-start(), calls=%async_computation.2 | async-start | bytes 2162688 | tf_op jit(solution)/shard_map/psum | solution.py:584
  27.2 24.0 %collective-permute-start.3 = (bf16[240,512]{1,0:T(8,128)(2,1)S(1)}, bf16[240,512]{1,0:T(8,128)(2,1)S(1)}, u32[]{:S(2)}, u32[]{:S(2)}) collective-permute-start(bf16[240,512]{1,0:T(8,128)(2,1)S(1)} %slice.265), channel_id=1, source_target_pairs={{0,8},{4,12},{8,0},{12,4},{16,24},{20,28},{24,16},{28,20},{1,9},{5... | collective-permute-start | bytes 737288 | tf_op jit(solution)/shard_map/ppermute | solution.py:63
  29.1 22.1 %collective-permute-start.2 = (bf16[240,512]{1,0:T(8,128)(2,1)S(1)}, bf16[240,512]{1,0:T(8,128)(2,1)S(1)}, u32[]{:S(2)}, u32[]{:S(2)}) collective-permute-start(bf16[240,512]{1,0:T(8,128)(2,1)S(1)} %slice.264), channel_id=1, source_target_pairs={{0,16},{4,20},{8,24},{12,28},{16,0},{20,4},{24,8},{28,12},{1,17},{... | collective-permute-start | bytes 737288 | tf_op jit(solution)/shard_map/ppermute | solution.py:63
  35.7 17.1 %collective-permute-start.8 = (bf16[4,136,768]{2,1,0:T(8,128)(2,1)S(1)}, bf16[4,136,768]{2,1,0:T(8,128)(2,1)S(1)}, u32[]{:S(2)}, u32[]{:S(2)}) collective-permute-start(bf16[4,136,768]{2,1,0:T(8,128)(2,1)S(1)} %pad_maximum_fusion.2), channel_id=1, source_target_pairs={{0,4},{4,0},{8,12},{12,8},{16,20},{20,16},{24,28},{28,24},{1,5},{5... | collective-permute-start | bytes 2506760 | tf_op jit(solution)/shard_map/ppermute | solution.py:63
  132.8 23.2 %collective-permute-start.20 = (bf16[240,1024]{1,0:T(8,128)(2,1)}, bf16[240,1024]{1,0:T(8,128)(2,1)S(1)}, u32[]{:S(2)}, u32[]{:S(2)}) collective-permute-start(bf16[240,1024]{1,0:T(8,128)(2,1)} %get-tuple-element.162), channel_id=1, source_target_pairs={{0,24},{4,28},{8,16},{12,20},{16,8},{20,12},{24,0},{28,4},{1,25},{... | collective-permute-start | bytes 1474568 | tf_op jit(solution)/shard_map/ppermute | solution.py:63
  134.2 23.8 %collective-permute-start.19 = (bf16[240,1024]{1,0:T(8,128)(2,1)}, bf16[240,1024]{1,0:T(8,128)(2,1)S(1)}, u32[]{:S(2)}, u32[]{:S(2)}) collective-permute-start(bf16[240,1024]{1,0:T(8,128)(2,1)} %get-tuple-element.163), channel_id=1, source_target_pairs={{0,16},{4,20},{8,24},{12,28},{16,0},{20,4},{24,8},{28,12},{1,17},{... | collective-permute-start | bytes 1474568 | tf_op jit(solution)/shard_map/ppermute | solution.py:63
  134.9 23.1 %collective-permute-start.18 = (bf16[240,1024]{1,0:T(8,128)(2,1)S(1)}, bf16[240,1024]{1,0:T(8,128)(2,1)S(1)}, u32[]{:S(2)}, u32[]{:S(2)}) collective-permute-start(bf16[240,1024]{1,0:T(8,128)(2,1)S(1)} %get-tuple-element.164), channel_id=1, source_target_pairs={{0,8},{4,12},{8,0},{12,4},{16,24},{20,28},{24,16},{28,20},{1,9},{5... | collective-permute-start | bytes 1474568 | tf_op jit(solution)/shard_map/ppermute | solution.py:63
  154.8 34.1 %collective-permute-start.24 = (bf16[1024,256]{1,0:T(8,128)(2,1)S(1)}, bf16[1024,256]{1,0:T(8,128)(2,1)S(1)}, u32[]{:S(2)}, u32[]{:S(2)}) collective-permute-start(bf16[1024,256]{1,0:T(8,128)(2,1)S(1)} %get-tuple-element.182), channel_id=1, source_target_pairs={{0,1},{1,0},{2,3},{3,2},{4,5},{5,4},{6,7},{7,6},{8,9},{9,8},{10,11... | collective-permute-start | bytes 1572872 | tf_op jit(solution)/shard_map/ppermute | solution.py:67
  166.1 18.3 %collective-permute-start.21 = (bf16[240,256]{1,0:T(8,128)(2,1)}, bf16[240,256]{1,0:T(8,128)(2,1)S(1)}, u32[]{:S(2)}, u32[]{:S(2)}) collective-permute-start(bf16[240,256]{1,0:T(8,128)(2,1)} %get-tuple-element.90), channel_id=1, source_target_pairs={{0,1},{1,0},{2,3},{3,2},{4,5},{5,4},{6,7},{7,6},{8,9},{9,8},{10,11... | collective-permute-start | bytes 368648 | tf_op jit(solution)/shard_map/ppermute | solution.py:67
  167.5 16.9 %collective-permute-start.22 = (bf16[240,256]{1,0:T(8,128)(2,1)}, bf16[240,256]{1,0:T(8,128)(2,1)S(1)}, u32[]{:S(2)}, u32[]{:S(2)}) collective-permute-start(bf16[240,256]{1,0:T(8,128)(2,1)} %get-tuple-element.91), channel_id=1, source_target_pairs={{0,2},{1,3},{2,0},{3,1},{4,6},{5,7},{6,4},{7,5},{8,10},{9,11},{10,... | collective-permute-start | bytes 368648 | tf_op jit(solution)/shard_map/ppermute | solution.py:67
  170.1 18.8 %collective-permute-start.23 = (bf16[240,256]{1,0:T(8,128)(2,1)}, bf16[240,256]{1,0:T(8,128)(2,1)S(1)}, u32[]{:S(2)}, u32[]{:S(2)}) collective-permute-start(bf16[240,256]{1,0:T(8,128)(2,1)} %get-tuple-element.92), channel_id=1, source_target_pairs={{0,3},{1,2},{2,1},{3,0},{4,7},{5,6},{6,5},{7,4},{8,11},{9,10},{10,... | collective-permute-start | bytes 368648 | tf_op jit(solution)/shard_map/ppermute | solution.py:67
  213.2 27.9 %collective-permute-start.28 = (bf16[1024,256]{1,0:T(8,128)(2,1)S(1)}, bf16[1024,256]{1,0:T(8,128)(2,1)}, u32[]{:S(2)}, u32[]{:S(2)}) collective-permute-start(bf16[1024,256]{1,0:T(8,128)(2,1)S(1)} %add_convert_fusion.3), channel_id=1, source_target_pairs={{0,2},{1,3},{2,0},{3,1},{4,6},{5,7},{6,4},{7,5},{8,10},{9,11},{10,... | collective-permute-start | bytes 1572872 | tf_op jit(solution)/shard_map/ppermute | solution.py:67
  213.2 25.2 %collective-permute-start.27 = (bf16[240,1024]{1,0:T(8,128)(2,1)}, bf16[240,1024]{1,0:T(8,128)(2,1)}, u32[]{:S(2)}, u32[]{:S(2)}) collective-permute-start(bf16[240,1024]{1,0:T(8,128)(2,1)} %get-tuple-element.103), channel_id=1, source_target_pairs={{0,1},{1,0},{2,3},{3,2},{4,5},{5,4},{6,7},{7,6},{8,9},{9,8},{10,11... | collective-permute-start | bytes 1474568 | tf_op jit(solution)/shard_map/ppermute | solution.py:67
  214.4 59.6 %collective-permute-start.41 = (bf16[4,240,1024]{2,1,0:T(8,128)(2,1)}, bf16[4,240,1024]{2,1,0:T(8,128)(2,1)}, u32[]{:S(2)}, u32[]{:S(2)}) collective-permute-start(bf16[4,240,1024]{2,1,0:T(8,128)(2,1)} %get-tuple-element.112), channel_id=1, source_target_pairs={{0,4},{4,0},{8,12},{12,8},{16,20},{20,16},{24,28},{28,24},{1,5},{5... | collective-permute-start | bytes 5898248 | tf_op jit(solution)/shard_map/ppermute | solution.py:63
  218.6 24.3 %collective-permute-start.31 = (bf16[136,768]{1,0:T(8,128)(2,1)S(1)}, bf16[136,768]{1,0:T(8,128)(2,1)S(1)}, u32[]{:S(2)}, u32[]{:S(2)}) collective-permute-start(bf16[136,768]{1,0:T(8,128)(2,1)S(1)} %get-tuple-element.192), channel_id=1, source_target_pairs={{0,24},{4,28},{8,16},{12,20},{16,8},{20,12},{24,0},{28,4},{1,25},{... | collective-permute-start | bytes 626696 | tf_op jit(solution)/shard_map/ppermute | solution.py:63
  221.0 22.1 %collective-permute-start.30 = (bf16[136,768]{1,0:T(8,128)(2,1)S(1)}, bf16[136,768]{1,0:T(8,128)(2,1)S(1)}, u32[]{:S(2)}, u32[]{:S(2)}) collective-permute-start(bf16[136,768]{1,0:T(8,128)(2,1)S(1)} %get-tuple-element.193), channel_id=1, source_target_pairs={{0,16},{4,20},{8,24},{12,28},{16,0},{20,4},{24,8},{28,12},{1,17},{... | collective-permute-start | bytes 626696 | tf_op jit(solution)/shard_map/ppermute | solution.py:63
  243.0 24.6 %collective-permute-start.32 = (bf16[240,1024]{1,0:T(8,128)(2,1)S(1)}, bf16[240,1024]{1,0:T(8,128)(2,1)S(1)}, u32[]{:S(2)}, u32[]{:S(2)}) collective-permute-start(bf16[240,1024]{1,0:T(8,128)(2,1)S(1)} %add_convert_fusion.4), channel_id=1, source_target_pairs={{0,2},{1,3},{2,0},{3,1},{4,6},{5,7},{6,4},{7,5},{8,10},{9,11},{10,... | collective-permute-start | bytes 1474568 | tf_op jit(solution)/shard_map/ppermute | solution.py:67
  253.6 26.2 %collective-permute-start.45 = (bf16[240,1024]{1,0:T(8,128)(2,1)S(1)}, bf16[240,1024]{1,0:T(8,128)(2,1)S(1)}, u32[]{:S(2)}, u32[]{:S(2)}) collective-permute-start(bf16[240,1024]{1,0:T(8,128)(2,1)S(1)} %copy-done.38), channel_id=1, source_target_pairs={{0,1},{1,0},{2,3},{3,2},{4,5},{5,4},{6,7},{7,6},{8,9},{9,8},{10,11... | collective-permute-start | bytes 1474568 | tf_op jit(solution)/shard_map/ppermute | solution.py:67
  269.0 21.8 %collective-permute-start.36 = (bf16[136,1792]{1,0:T(8,128)(2,1)S(1)}, bf16[136,1792]{1,0:T(8,128)(2,1)S(1)}, u32[]{:S(2)}, u32[]{:S(2)}) collective-permute-start(bf16[136,1792]{1,0:T(8,128)(2,1)S(1)} %pad_maximum_fusion.7), channel_id=1, source_target_pairs={{0,2},{1,3},{2,0},{3,1},{4,6},{5,7},{6,4},{7,5},{8,10},{9,11},{10,... | collective-permute-start | bytes 1462280 | tf_op jit(solution)/shard_map/ppermute | solution.py:67
  273.9 25.3 %collective-permute-start.47 = (bf16[8,128,256]{2,1,0:T(8,128)(2,1)S(1)}, bf16[8,128,256]{2,1,0:T(8,128)(2,1)S(1)}, u32[]{:S(2)}, u32[]{:S(2)}) collective-permute-start(bf16[8,128,256]{2,1,0:T(8,128)(2,1)S(1)} %bitcast.219), channel_id=1, source_target_pairs={{0,1},{1,0},{2,3},{3,2},{4,5},{5,4},{6,7},{7,6},{8,9},{9,8},{10,11... | collective-permute-start | bytes 1572872 | tf_op jit(solution)/shard_map/ppermute | solution.py:67
  276.9 31.0 %collective-permute-start.42 = (bf16[240,1024]{1,0:T(8,128)(2,1)}, bf16[240,1024]{1,0:T(8,128)(2,1)}, u32[]{:S(2)}, u32[]{:S(2)}) collective-permute-start(bf16[240,1024]{1,0:T(8,128)(2,1)} %get-tuple-element.167), channel_id=1, source_target_pairs={{0,8},{4,12},{8,0},{12,4},{16,24},{20,28},{24,16},{28,20},{1,9},{5... | collective-permute-start | bytes 1474568 | tf_op jit(solution)/shard_map/ppermute | solution.py:63
  277.4 30.5 %collective-permute-start.44 = (bf16[240,1024]{1,0:T(8,128)(2,1)}, bf16[240,1024]{1,0:T(8,128)(2,1)}, u32[]{:S(2)}, u32[]{:S(2)}) collective-permute-start(bf16[240,1024]{1,0:T(8,128)(2,1)} %get-tuple-element.168), channel_id=1, source_target_pairs={{0,24},{4,28},{8,16},{12,20},{16,8},{20,12},{24,0},{28,4},{1,25},{... | collective-permute-start | bytes 1474568 | tf_op jit(solution)/shard_map/ppermute | solution.py:63
  279.8 28.1 %collective-permute-start.43 = (bf16[240,1024]{1,0:T(8,128)(2,1)}, bf16[240,1024]{1,0:T(8,128)(2,1)}, u32[]{:S(2)}, u32[]{:S(2)}) collective-permute-start(bf16[240,1024]{1,0:T(8,128)(2,1)} %get-tuple-element.169), channel_id=1, source_target_pairs={{0,16},{4,20},{8,24},{12,28},{16,0},{20,4},{24,8},{28,12},{1,17},{... | collective-permute-start | bytes 1474568 | tf_op jit(solution)/shard_map/ppermute | solution.py:63
  291.9 20.8 %collective-permute-start.46 = (bf16[136,2560]{1,0:T(8,128)(2,1)}, bf16[136,2560]{1,0:T(8,128)(2,1)}, u32[]{:S(2)}, u32[]{:S(2)}) collective-permute-start(bf16[136,2560]{1,0:T(8,128)(2,1)} %pad_maximum_fusion.5), channel_id=1, source_target_pairs={{0,1},{1,0},{2,3},{3,2},{4,5},{5,4},{6,7},{7,6},{8,9},{9,8},{10,11... | collective-permute-start | bytes 2088968 | tf_op jit(solution)/shard_map/ppermute | solution.py:67
  (59 other events, 443.2 us)
Sparse Core Ops, SparseCore 0:
  9.7 46.2 all-gather.5
  57.8 26.7 all-gather.3
  143.3 64.5 all-reduce.12

commit v3 on v2

--- a/solution.py
+++ b/solution.py
@@ -460,6 +460,32 @@
     )(x, mine, near, far, hidden_grad, vecs)
 
 
+def place_up_kernel(seat, mine, other, out):
+    width = mine.shape[2]
+    side, team = seat[0] & 1, seat[1]
+    for j in range(TEAM):
+        own, got = mine[j ^ team].astype(F32), other[j ^ team].astype(F32)
+        out[:, 2 * j * width : (2 * j + 1) * width] = jnp.where(side == 0, own, got)
+        out[:, (2 * j + 1) * width : (2 * j + 2) * width] = jnp.where(side == 0, got, own)
+
+
+def place_up(seat, mine, other):
+    _, rows, width = mine.shape
+    return pl.pallas_call(
+        place_up_kernel,
+        name="place_up",
+        grid_spec=pltpu.PrefetchScalarGridSpec(
+            num_scalar_prefetch=1,
+            grid=(1,),
+            in_specs=[block(*mine.shape)] * 2,
+            out_specs=block(rows, 2 * TEAM * width),
+        ),
+        out_shape=shape_of((rows, 2 * TEAM * width), F32),
+        compiler_params=params(),
+        cost_estimate=cost(1, 12 * rows * TEAM * width),
+    )(seat, mine, other)
+
+
 def per_device(
     inputs,
     lengths,
@@ -657,7 +683,7 @@
     up_rel = jnp.stack([after(pick(pair, chip), packed)] + up_moved)
     up_rel = lax.optimization_barrier(up_rel.reshape(TEAM, own_rows, half_width))
     up_other = cross(up_rel, 1)
-    packed_two = after(packed_two, up_rel)
+    packed_two = after(packed_two, up_rel, input_grad)
     qkv_two = packed_two[:, :lanes]
     proj_two = lax.optimization_barrier(joined(proj_mine, packed_two[:, lanes:]))
     packed_one = cross(jnp.concatenate([qkv_mine, qkv_two, proj_two], axis=1), 1)
@@ -671,12 +697,16 @@
     output = jnp.where(row_valid, output.reshape(inputs.shape), 0.0).astype(BF16)
 
     up_bias_grad = down_total[down_rows, : up_bias.shape[0]].astype(F32)
-    up_first = jnp.where(side == 0, up_rel, up_other)
-    up_second = jnp.where(side == 0, up_other, up_rel)
-    up_rel = jnp.concatenate([up_first, up_second], axis=2)
-    up_grad = jnp.stack([pick(up_rel, j ^ team) for j in range(TEAM)], axis=1).astype(F32)
-    up_grad = up_grad.reshape(own_rows, TEAM, outer, feed_width // outer).transpose(0, 2, 1, 3)
-    up_grad = up_grad.reshape(own_rows, hidden_units)
+    seats = jnp.stack([seat, team]).astype(jnp.int32)
+    if outer == 1:
+        up_grad = place_up(seats, up_rel, up_other)
+    else:
+        up_first = jnp.where(side == 0, up_rel, up_other)
+        up_second = jnp.where(side == 0, up_other, up_rel)
+        up_rel = jnp.concatenate([up_first, up_second], axis=2)
+        up_grad = jnp.stack([pick(up_rel, j ^ team) for j in range(TEAM)], axis=1).astype(F32)
+        up_grad = up_grad.reshape(own_rows, TEAM, outer, feed_width // outer).transpose(0, 2, 1, 3)
+        up_grad = up_grad.reshape(own_rows, hidden_units)
     proj_grad = proj_total[:own_rows]
     qkv_parts = jnp.stack([qkv_mine, qkv_near[0], qkv_two, qkv_near[1]])
     ordered = [pick(qkv_parts, seat ^ j).astype(F32) for j in range(ZS)]

time: 326 us -> 324 us (level)
  other arithmetic: 38.6 us -> 32 us
  Pallas kernels: 70.4 us -> 73.7 us
    unnamed x8 -> x1, other arithmetic: 5.37 us -> 0.02 us
    ppermute x14, waiting for transfers between devices: 52.8 us -> 57.8 us  [cross(): return lax.ppermute(value, 'seq', [(i, i ^ mask) for i in range(ZS)])]
    pallas_call x0 -> x1, Pallas kernels: none -> 3.36 us  [place_up(): pl.pallas_call(place_up_kernel, name='place_up', grid_spec=pltpu.Prefetch...]
    unnamed x102 -> x121, local copies, waits for them, and re-layouts: 9.18 us -> 10.8 us
  transfers between devices with their start and end apart: 52 -> 52, of which waited for: 22 -> 23; matrix products, arithmetic and copies ran while one was open for 18% -> 16% of each run, Pallas kernels for 18% -> 20%
where the time goes in v3:
time: 324 us; the launch traced here: 323 us
  waiting for transfers between devices  117 us (36%)
  Pallas kernels  73.7 us (23%)
  starting transfers between devices  50.9 us (16%)
  other arithmetic  32 us (10%)
  local copies, waits for them, and re-layouts  18.7 us (6%)
  matrix products  15.1 us (5%)
  between operations  14.9 us (5%)
    ppermute x34, waiting for transfers between devices, swap(): return lax.ppermute(value, 'fsdp', [(i, i ^ mask) for i in range(size)])  57.8 us
    ppermute x14, waiting for transfers between devices, cross(): return lax.ppermute(value, 'seq', [(i, i ^ mask) for i in range(ZS)])  57.8 us
    ppermute x34, starting transfers between devices, swap(): return lax.ppermute(value, 'fsdp', [(i, i ^ mask) for i in range(size)])  35.4 us
    pallas_call x1, Pallas kernels, attend_back(): pl.pallas_call(attend_back_kernel, name='attend_back', grid_spec=pltpu.Pr...  14.6 us
    pallas_call x2, Pallas kernels, feed(): pl.pallas_call(feed_kernel, name='feed', grid=(count // 2,), in_specs=[wi...  12.2 us
    pallas_call x1, Pallas kernels, attend(): pl.pallas_call(attend_kernel, name='attend', grid_spec=pltpu.PrefetchScal...  12.1 us
    convert_element_type x8, other arithmetic, joined(): return (first.astype(F32) + second.astype(F32)).astype(BF16)  11.9 us
    ppermute x14, starting transfers between devices, cross(): return lax.ppermute(value, 'seq', [(i, i ^ mask) for i in range(ZS)])  11.8 us
  transfers between devices with their start and end apart: 52, of which 23 were waited for; matrix products, arithmetic and copies ran while one was open for 16% of the time, Pallas kernels for 20%

profile of v3, /device:TPU:0, one launch (start us, length us, event | category | flops | bytes accessed | tf_op | source)
XLA Modules:
  0.0 322.8 jit_solution(9168772852074059777)
XLA Ops:
  9.9 3.0 collective-permute-start.1
  17.0 2.9 collective-permute-start.7
  21.7 3.7 %all-to-all-start = ((bf16[8,128,512]{2,1,0:T(8,128)(2,1)}), bf16[8,128,512]{2,1,0:T(8,128)(2,1)S(1)}, u32[]{:S(2)}, u32[]{:S(2)}) async-start(bf16[8,128,512]{2,1,0:T(8,128)(2,1)} %bitcast.186), calls=%async_computation | async-start | bytes 2097152 | tf_op jit(solution)/shard_map/all_to_all | solution.py:559
  31.7 4.0 %collective-permute-done.7 = bf16[136,768]{1,0:T(8,128)(2,1)} collective-permute-done((bf16[136,768]{1,0:T(8,128)(2,1)}, bf16[136,768]{1,0:T(8,128)(2,1)}, u32[]{:S(2)}, u32[]{:S(2)}) %collective-permute-start.7) | collective-permute-done | bytes 208928 | tf_op jit(solution)/shard_map/ppermute | solution.py:63
  38.0 13.2 %collective-permute-done.3 = bf16[240,512]{1,0:T(8,128)(2,1)S(1)} collective-permute-done((bf16[240,512]{1,0:T(8,128)(2,1)S(1)}, bf16[240,512]{1,0:T(8,128)(2,1)S(1)}, u32[]{:S(2)}, u32[]{:S(2)}) %collective-permute-start.3) | collective-permute-done | bytes 245792 | tf_op jit(solution)/shard_map/ppermute | solution.py:63
  57.1 12.1 %attend.1 = (bf16[3,320,768]{2,1,0:T(8,128)(2,1)}, bf16[3,320,1024]{2,1,0:T(8,128)(2,1)}, bf16[240,256]{1,0:T(8,128)(2,1)}, bf16[240,256]{1,0:T(8,128)(2,1)}, bf...) custom-call(s32[4]{0:T(128)} %pad_add_fusion.2.meta, bf16[4,3,80,1024]{3,2,1,0:T(8,128)(2,1)} %bitcast.191, ...), custom_call_target="tpu_custom_call" | custom-call | flops 2088960 | bytes 7296 | tf_op jit(solution)/shard_map/attend/pallas_call | solution.py:169
  73.7 4.1 %fusion.8.above = f32[4,240,512]{2,1,0:T(8,128)} fusion(bf16[4,240,1024]{2,1,0:T(8,128)(2,1)} %pad_maximum_fusion.cot_e, bf16[512,1024]{1,0:T(8,128)(2,1)S(1)} %copy-done.10), kind=kOutput, calls=%fused_computation.20 | convolution fusion | flops 1006632960 | bytes 4980736 | tf_op jit(solution)/shard_map/dot_general | solution.py:580
  77.8 4.0 %fusion.6.above = f32[4,240,512]{2,1,0:T(8,128)} fusion(bf16[4,240,1024]{2,1,0:T(8,128)(2,1)} %collective-permute-done.4.cot_o, bf16[512,1024]{1,0:T(8,128)(2,1)S(1)} %copy-done.10), kind=kOutput, calls=%fused_computation.18 | convolution fusion | flops 1006632960 | bytes 4980736 | tf_op jit(solution)/shard_map/dot_general | solution.py:580
  84.6 4.3 %project.1 = (f32[240,1024]{1,0:T(8,128)}, bf16[240,1024]{1,0:T(8,128)(2,1)}) custom-call(s32[4]{0:T(128)} %pad_add_fusion.2.meta, bf16[240,256]{1,0:T(8,128)(2,1)} %get-tuple-element.72.c0, bf16[240,256]{1,0:T(8,128)(2,1)} %copy-done.31, bf16[240,256]{1,0:T(8,128)(2,1)} %copy-done.33, bf16[240,256]{1,0:T(8,128)(2,1)} %copy-done.35, ...), custom_call_target="tpu_custom_call" | custom-call | flops 491520 | bytes 4448 | tf_op jit(solution)/shard_map/project/pallas_call | solution.py:274
  91.0 11.6 %collective-permute-done.13 = bf16[240,1024]{1,0:T(8,128)(2,1)S(1)} collective-permute-done((bf16[240,1024]{1,0:T(8,128)(2,1)}, bf16[240,1024]{1,0:T(8,128)(2,1)S(1)}, u32[]{:S(2)}, u32[]{:S(2)}) %collective-permute-start.13) | collective-permute-done | bytes 491552 | tf_op jit(solution)/shard_map/ppermute | solution.py:63
  104.7 5.2 %collective-permute-done.15 = bf16[240,512]{1,0:T(8,128)(2,1)S(1)} collective-permute-done((bf16[240,512]{1,0:T(8,128)(2,1)S(1)}, bf16[240,512]{1,0:T(8,128)(2,1)S(1)}, u32[]{:S(2)}, u32[]{:S(2)}) %collective-permute-start.15) | collective-permute-done | bytes 245792 | tf_op jit(solution)/shard_map/ppermute | solution.py:63
  116.9 6.1 %feed.3 = (bf16[4,240,512]{2,1,0:T(8,128)(2,1)}, bf16[4,240,512]{2,1,0:T(8,128)(2,1)}, bf16[4,240,1024]{2,1,0:T(8,128)(2,1)}) custom-call(bf16[4,240,1024]{2,1,0:T(8,128)(2,1)} %copy-done.3, f32[4,240,512]{2,1,0:T(8,128)} %fusion.6.above, bf16[1024,512]{1,0:T(8,128)(2,1)} %bitcast.189, f32[1,512]{1,0:T(1,128)} %bitcast.226), custom_call_target="tpu_custom_call" | custom-call | flops 1966080 | bytes 8704 | tf_op jit(solution)/shard_map/feed/pallas_call | solution.py:310
  123.1 6.1 %feed.2 = (bf16[4,240,512]{2,1,0:T(8,128)(2,1)}, bf16[4,240,512]{2,1,0:T(8,128)(2,1)}, bf16[4,240,1024]{2,1,0:T(8,128)(2,1)}) custom-call(bf16[4,240,1024]{2,1,0:T(8,128)(2,1)} %copy-done.1, f32[4,240,512]{2,1,0:T(8,128)} %fusion.8.above, bf16[1024,512]{1,0:T(8,128)(2,1)} %bitcast.190, f32[1,512]{1,0:T(1,128)} %bitcast.227), custom_call_target="tpu_custom_call" | custom-call | flops 1966080 | bytes 8704 | tf_op jit(solution)/shard_map/feed/pallas_call | solution.py:310
  129.2 3.5 %fusion.18 = (bf16[240,1024]{1,0:T(8,128)(2,1)}, bf16[240,1024]{1,0:T(8,128)(2,1)}, bf16[240,1024]{1,0:T(8,128)(2,1)}) fusion(bf16[4,240,1024]{2,1,0:T(8,128)(2,1)S(1)} %collective-permute-done.17.g1, bf16[4,240,1024]{2,1,0:T(8,128)(2,1)} %get-tuple-element.79.g0), kind=kLoop, calls=%fused_computation.61 | loop fusion | flops 2949120 | bytes 4423680 | tf_op jit(solution)/shard_map/convert_element_type | solution.py:71
  136.3 6.8 %down_gradient.1 = bf16[528,1024]{1,0:T(8,128)(2,1)} custom-call(bf16[4,240,512]{2,1,0:T(8,128)(2,1)} %get-tuple-element.82.act_e, bf16[4,240,512]{2,1,0:T(8,128)(2,1)} %get-tuple-element.86.act_o, bf16[4,240,512]{2,1,0:T(8,128)(2,1)} %get-tuple-element.84.grad_e, bf16[4,240,512]{2,1,0:T(8,128)(2,1)} %get-tuple-element.85.grad_o, ...), custom_call_target="tpu_custom_call" | custom-call | flops 1966080 | bytes 7680 | tf_op jit(solution)/shard_map/down_gradient/pallas_call | solution.py:352
  143.1 10.4 %feed_grads.1 = (bf16[4,240,1024]{2,1,0:T(8,128)(2,1)}, bf16[4,240,1024]{2,1,0:T(8,128)(2,1)}, bf16[1024,512]{1,0:T(8,128)(2,1)}) custom-call(bf16[4,240,512]{2,1,0:T(8,128)(2,1)} %get-tuple-element.82.act_e, bf16[4,240,512]{2,1,0:T(8,128)(2,1)} %get-tuple-element.86.act_o, bf16[4,240,512]{2,1,0:T(8,128)(2,1)} %get-tuple-element.84.grad_e, ...), custom_call_target="tpu_custom_call" | custom-call | flops 3932160 | bytes 11520 | tf_op jit(solution)/shard_map/feed_grads/pallas_call | solution.py:387
  159.5 5.9 %middle.1 = (f32[240,1024]{1,0:T(8,128)}, bf16[240,1024]{1,0:T(8,128)(2,1)}, f32[4,1024]{1,0:T(4,128)}, bf16[240,256]{1,0:T(8,128)(2,1)}, bf16[240,256]{1,0:T(8,...) custom-call(s32[4]{0:T(128)} %pad_add_fusion.2.meta, bf16[4,240,1024]{2,1,0:T(8,128)(2,1)} %get-tuple-element.79.g0, ...), custom_call_target="tpu_custom_call" | custom-call | flops 491520 | bytes 8288 | tf_op jit(solution)/shard_map/middle/pallas_call | solution.py:423
  170.5 3.1 convolution_convert_fusion
  174.0 10.4 %collective-permute-done.21.d1 = bf16[240,256]{1,0:T(8,128)(2,1)S(1)} collective-permute-done((bf16[240,256]{1,0:T(8,128)(2,1)}, bf16[240,256]{1,0:T(8,128)(2,1)S(1)}, u32[]{:S(2)}, u32[]{:S(2)}) %collective-permute-start.21) | collective-permute-done | bytes 122912 | tf_op jit(solution)/shard_map/ppermute | solution.py:67
  184.4 4.5 %collective-permute-done.23.d3 = bf16[240,256]{1,0:T(8,128)(2,1)S(1)} collective-permute-done((bf16[240,256]{1,0:T(8,128)(2,1)}, bf16[240,256]{1,0:T(8,128)(2,1)S(1)}, u32[]{:S(2)}, u32[]{:S(2)}) %collective-permute-start.23) | collective-permute-done | bytes 122912 | tf_op jit(solution)/shard_map/ppermute | solution.py:67
  189.5 14.6 %attend_back.1 = (bf16[3,320,768]{2,1,0:T(8,128)(2,1)}, f32[8,1024]{1,0:T(8,128)}, bf16[240,1024]{1,0:T(8,128)(2,1)}, bf16[240,1024]{1,0:T(8,128)(2,1)}, bf16[24...) custom-call(s32[4]{0:T(128)} %pad_add_fusion.2.meta, bf16[4,3,80,1024]{3,2,1,0:T(8,128)(2,1)} %bitcast.192, ...), custom_call_target="tpu_custom_call" | custom-call | flops 3010560 | bytes 8736 | tf_op jit(solution)/shard_map/attend_back/pallas_call | solution.py:240
  205.6 3.8 %bitcast_convert_fusion = bf16[1024,768]{1,0:T(8,128)(2,1)S(1)} fusion(bf16[3,320,1024]{2,1,0:T(8,128)(2,1)} %get-tuple-element.77, bf16[3,320,768]{2,1,0:T(8,128)(2,1)} %get-tuple-element.96), kind=kOutput, calls=%fused_computation.2 | convolution fusion | flops 1510735872 | bytes 5013504 | tf_op jit(solution)/shard_map/dot_general | solution.py:43
  223.0 15.1 %collective-permute-done.27 = bf16[240,1024]{1,0:T(8,128)(2,1)} collective-permute-done((bf16[240,1024]{1,0:T(8,128)(2,1)}, bf16[240,1024]{1,0:T(8,128)(2,1)}, u32[]{:S(2)}, u32[]{:S(2)}) %collective-permute-start.27) | collective-permute-done | bytes 491552 | tf_op jit(solution)/shard_map/ppermute | solution.py:67
  248.1 5.4 %collective-permute-done.35 = bf16[136,1024]{1,0:T(8,128)(2,1)S(1)} collective-permute-done((bf16[136,1024]{1,0:T(8,128)(2,1)S(1)}, bf16[136,1024]{1,0:T(8,128)(2,1)S(1)}, u32[]{:S(2)}, u32[]{:S(2)}) %collective-permute-start.35) | collective-permute-done | bytes 278560 | tf_op jit(solution)/shard_map/ppermute | solution.py:63
  253.6 5.4 %collective-permute-done.34 = bf16[136,1024]{1,0:T(8,128)(2,1)S(1)} collective-permute-done((bf16[136,1024]{1,0:T(8,128)(2,1)S(1)}, bf16[136,1024]{1,0:T(8,128)(2,1)S(1)}, u32[]{:S(2)}, u32[]{:S(2)}) %collective-permute-start.34) | collective-permute-done | bytes 278560 | tf_op jit(solution)/shard_map/ppermute | solution.py:63
  261.2 6.5 %collective-permute-done.32.far = bf16[240,1024]{1,0:T(8,128)(2,1)S(1)} collective-permute-done((bf16[240,1024]{1,0:T(8,128)(2,1)S(1)}, bf16[240,1024]{1,0:T(8,128)(2,1)S(1)}, u32[]{:S(2)}, u32[]{:S(2)}) %collective-permute-start.32) | collective-permute-done | bytes 491552 | tf_op jit(solution)/shard_map/ppermute | solution.py:67
  270.1 3.9 %collective-permute-done.40 = bf16[2,128,256]{2,1,0:T(8,128)(2,1)S(1)} collective-permute-done((bf16[2,128,256]{2,1,0:T(8,128)(2,1)S(1)}, bf16[2,128,256]{2,1,0:T(8,128)(2,1)S(1)}, u32[]{:S(2)}, u32[]{:S(2)}) %collective-permute-start.40) | collective-permute-done | bytes 131104 | tf_op jit(solution)/shard_map/ppermute | solution.py:63
  280.7 4.1 %finish.1 = bf16[240,1024]{1,0:T(8,128)(2,1)} custom-call(bf16[240,1024]{1,0:T(8,128)(2,1)} %bitcast.194, bf16[240,1024]{1,0:T(8,128)(2,1)} %get-tuple-element.109.mine, bf16[240,1024]{1,0:T(8,128)(2,1)} %copy-done.22, bf16[240,1024]{1,0:T(8,128)(2,1)} %copy-done.20, f32[240,1024]{1,0:T(8,128)} %get-tuple-element.117.hidden_grad, f32[6,1024]{1,0:T(8,128)} %bitcast.215), custom_call_target="tpu_custom_call" | custom-call | flops 4800 | bytes 2880 | tf_op jit(solution)/shard_map/finish/pallas_call | solution.py:451
  284.8 7.3 %collective-permute-done.36 = bf16[136,1792]{1,0:T(8,128)(2,1)S(1)} collective-permute-done((bf16[136,1792]{1,0:T(8,128)(2,1)}, bf16[136,1792]{1,0:T(8,128)(2,1)S(1)}, u32[]{:S(2)}, u32[]{:S(2)}) %collective-permute-start.36) | collective-permute-done | bytes 487456 | tf_op jit(solution)/shard_map/ppermute | solution.py:67
  293.7 5.7 %collective-permute-done.47.other = bf16[8,128,256]{2,1,0:T(8,128)(2,1)S(1)} collective-permute-done((bf16[8,128,256]{2,1,0:T(8,128)(2,1)S(1)}, bf16[8,128,256]{2,1,0:T(8,128)(2,1)S(1)}, u32[]{:S(2)}, u32[]{:S(2)}) %collective-permute-start.47) | collective-permute-done | bytes 524320 | tf_op jit(solution)/shard_map/ppermute | solution.py:67
  300.2 3.4 %place_up.1 = f32[128,4096]{1,0:T(8,128)} custom-call(s32[2]{0:T(128)} %add_convert_fusion.12.seat, bf16[8,128,256]{2,1,0:T(8,128)(2,1)} %bitcast.204, bf16[8,128,256]{2,1,0:T(8,128)(2,1)} %copy-done.19), custom_call_target="tpu_custom_call" | custom-call | bytes 3072 | tf_op jit(solution)/shard_map/place_up/pallas_call | solution.py:474
  306.2 6.8 %collective-permute-done.46 = bf16[136,2560]{1,0:T(8,128)(2,1)S(1)} collective-permute-done((bf16[136,2560]{1,0:T(8,128)(2,1)S(1)}, bf16[136,2560]{1,0:T(8,128)(2,1)S(1)}, u32[]{:S(2)}, u32[]{:S(2)}) %collective-permute-start.46) | collective-permute-done | bytes 696352 | tf_op jit(solution)/shard_map/ppermute | solution.py:67
  (294 shorter events, 101.1 us)
Async XLA Ops:
  7.3 49.8 %all-gather.6.cloned.1.call-start = ((), (), s32[]{:S(2)}) async-start(), calls=%async_computation.3 | async-start | bytes 2457600 | tf_op jit(solution)/shard_map/all_gather | solution.py:522
  8.0 76.6 %all-gather.4.cloned.1.call-start = ((), (), s32[]{:S(2)}) async-start(), calls=%async_computation.1 | async-start | bytes 2359296 | tf_op jit(solution)/shard_map/all_gather | solution.py:554
  9.9 16.2 %collective-permute-start.1 = (bf16[240,1024]{1,0:T(8,128)(2,1)S(1)}, bf16[240,1024]{1,0:T(8,128)(2,1)S(1)}, u32[]{:S(2)}, u32[]{:S(2)}) collective-permute-start(bf16[240,1024]{1,0:T(8,128)(2,1)S(1)} %bitcast.195), channel_id=1, source_target_pairs={{0,16},{4,20},{8,24},{12,28},{16,0},{20,4},{24,8},{28,12},{1,17},{... | collective-permute-start | bytes 1474568 | tf_op jit(solution)/shard_map/ppermute | solution.py:63
  13.0 15.1 %collective-permute-start = (bf16[240,1024]{1,0:T(8,128)(2,1)S(1)}, bf16[240,1024]{1,0:T(8,128)(2,1)S(1)}, u32[]{:S(2)}, u32[]{:S(2)}) collective-permute-start(bf16[240,1024]{1,0:T(8,128)(2,1)S(1)} %bitcast.196), channel_id=1, source_target_pairs={{0,8},{4,12},{8,0},{12,4},{16,24},{20,28},{24,16},{28,20},{1,9},{5... | collective-permute-start | bytes 1474568 | tf_op jit(solution)/shard_map/ppermute | solution.py:63
  16.9 14.8 %collective-permute-start.5 = (bf16[136,768]{1,0:T(8,128)(2,1)}, bf16[136,768]{1,0:T(8,128)(2,1)}, u32[]{:S(2)}, u32[]{:S(2)}) collective-permute-start(bf16[136,768]{1,0:T(8,128)(2,1)} %get-tuple-element.169), channel_id=1, source_target_pairs={{0,8},{4,12},{8,0},{12,4},{16,24},{20,28},{24,16},{28,20},{1,9},{5... | collective-permute-start | bytes 626696 | tf_op jit(solution)/shard_map/ppermute | solution.py:63
  17.0 18.7 %collective-permute-start.7 = (bf16[136,768]{1,0:T(8,128)(2,1)}, bf16[136,768]{1,0:T(8,128)(2,1)}, u32[]{:S(2)}, u32[]{:S(2)}) collective-permute-start(bf16[136,768]{1,0:T(8,128)(2,1)} %get-tuple-element.169), channel_id=1, source_target_pairs={{0,24},{4,28},{8,16},{12,20},{16,8},{20,12},{24,0},{28,4},{1,25},{... | collective-permute-start | bytes 626696 | tf_op jit(solution)/shard_map/ppermute | solution.py:63
  21.7 34.8 %all-to-all-start = ((bf16[8,128,512]{2,1,0:T(8,128)(2,1)}), bf16[8,128,512]{2,1,0:T(8,128)(2,1)S(1)}, u32[]{:S(2)}, u32[]{:S(2)}) async-start(bf16[8,128,512]{2,1,0:T(8,128)(2,1)} %bitcast.186), calls=%async_computation | async-start | bytes 2097152 | tf_op jit(solution)/shard_map/all_to_all | solution.py:559
  25.4 188.9 %all-reduce.13.cloned.1.call-start = ((), (), s32[]{:S(2)}) async-start(), calls=%async_computation.2 | async-start | bytes 2162688 | tf_op jit(solution)/shard_map/psum | solution.py:610
  26.1 25.0 %collective-permute-start.3 = (bf16[240,512]{1,0:T(8,128)(2,1)S(1)}, bf16[240,512]{1,0:T(8,128)(2,1)S(1)}, u32[]{:S(2)}, u32[]{:S(2)}) collective-permute-start(bf16[240,512]{1,0:T(8,128)(2,1)S(1)} %slice.265), channel_id=1, source_target_pairs={{0,8},{4,12},{8,0},{12,4},{16,24},{20,28},{24,16},{28,20},{1,9},{5... | collective-permute-start | bytes 737288 | tf_op jit(solution)/shard_map/ppermute | solution.py:63
  28.1 23.1 %collective-permute-start.2 = (bf16[240,512]{1,0:T(8,128)(2,1)S(1)}, bf16[240,512]{1,0:T(8,128)(2,1)S(1)}, u32[]{:S(2)}, u32[]{:S(2)}) collective-permute-start(bf16[240,512]{1,0:T(8,128)(2,1)S(1)} %slice.264), channel_id=1, source_target_pairs={{0,16},{4,20},{8,24},{12,28},{16,0},{20,4},{24,8},{28,12},{1,17},{... | collective-permute-start | bytes 737288 | tf_op jit(solution)/shard_map/ppermute | solution.py:63
  36.9 17.7 %collective-permute-start.8 = (bf16[4,136,768]{2,1,0:T(8,128)(2,1)S(1)}, bf16[4,136,768]{2,1,0:T(8,128)(2,1)S(1)}, u32[]{:S(2)}, u32[]{:S(2)}) collective-permute-start(bf16[4,136,768]{2,1,0:T(8,128)(2,1)S(1)} %pad_maximum_fusion.2), channel_id=1, source_target_pairs={{0,4},{4,0},{8,12},{12,8},{16,20},{20,16},{24,28},{28,24},{1,5},{5... | collective-permute-start | bytes 2506760 | tf_op jit(solution)/shard_map/ppermute | solution.py:63
  132.8 23.3 %collective-permute-start.20 = (bf16[240,1024]{1,0:T(8,128)(2,1)}, bf16[240,1024]{1,0:T(8,128)(2,1)S(1)}, u32[]{:S(2)}, u32[]{:S(2)}) collective-permute-start(bf16[240,1024]{1,0:T(8,128)(2,1)} %get-tuple-element.120), channel_id=1, source_target_pairs={{0,24},{4,28},{8,16},{12,20},{16,8},{20,12},{24,0},{28,4},{1,25},{... | collective-permute-start | bytes 1474568 | tf_op jit(solution)/shard_map/ppermute | solution.py:63
  134.1 23.8 %collective-permute-start.19 = (bf16[240,1024]{1,0:T(8,128)(2,1)}, bf16[240,1024]{1,0:T(8,128)(2,1)S(1)}, u32[]{:S(2)}, u32[]{:S(2)}) collective-permute-start(bf16[240,1024]{1,0:T(8,128)(2,1)} %get-tuple-element.121), channel_id=1, source_target_pairs={{0,16},{4,20},{8,24},{12,28},{16,0},{20,4},{24,8},{28,12},{1,17},{... | collective-permute-start | bytes 1474568 | tf_op jit(solution)/shard_map/ppermute | solution.py:63
  134.8 23.1 %collective-permute-start.18 = (bf16[240,1024]{1,0:T(8,128)(2,1)}, bf16[240,1024]{1,0:T(8,128)(2,1)S(1)}, u32[]{:S(2)}, u32[]{:S(2)}) collective-permute-start(bf16[240,1024]{1,0:T(8,128)(2,1)} %get-tuple-element.122), channel_id=1, source_target_pairs={{0,8},{4,12},{8,0},{12,4},{16,24},{20,28},{24,16},{28,20},{1,9},{5... | collective-permute-start | bytes 1474568 | tf_op jit(solution)/shard_map/ppermute | solution.py:63
  154.8 34.1 %collective-permute-start.24 = (bf16[1024,256]{1,0:T(8,128)(2,1)S(1)}, bf16[1024,256]{1,0:T(8,128)(2,1)S(1)}, u32[]{:S(2)}, u32[]{:S(2)}) collective-permute-start(bf16[1024,256]{1,0:T(8,128)(2,1)S(1)} %get-tuple-element.138), channel_id=1, source_target_pairs={{0,1},{1,0},{2,3},{3,2},{4,5},{5,4},{6,7},{7,6},{8,9},{9,8},{10,11... | collective-permute-start | bytes 1572872 | tf_op jit(solution)/shard_map/ppermute | solution.py:67
  166.1 18.3 %collective-permute-start.21 = (bf16[240,256]{1,0:T(8,128)(2,1)}, bf16[240,256]{1,0:T(8,128)(2,1)S(1)}, u32[]{:S(2)}, u32[]{:S(2)}) collective-permute-start(bf16[240,256]{1,0:T(8,128)(2,1)} %get-tuple-element.90), channel_id=1, source_target_pairs={{0,1},{1,0},{2,3},{3,2},{4,5},{5,4},{6,7},{7,6},{8,9},{9,8},{10,11... | collective-permute-start | bytes 368648 | tf_op jit(solution)/shard_map/ppermute | solution.py:67
  167.5 16.9 %collective-permute-start.22 = (bf16[240,256]{1,0:T(8,128)(2,1)}, bf16[240,256]{1,0:T(8,128)(2,1)S(1)}, u32[]{:S(2)}, u32[]{:S(2)}) collective-permute-start(bf16[240,256]{1,0:T(8,128)(2,1)} %get-tuple-element.91), channel_id=1, source_target_pairs={{0,2},{1,3},{2,0},{3,1},{4,6},{5,7},{6,4},{7,5},{8,10},{9,11},{10,... | collective-permute-start | bytes 368648 | tf_op jit(solution)/shard_map/ppermute | solution.py:67
  170.0 18.8 %collective-permute-start.23 = (bf16[240,256]{1,0:T(8,128)(2,1)}, bf16[240,256]{1,0:T(8,128)(2,1)S(1)}, u32[]{:S(2)}, u32[]{:S(2)}) collective-permute-start(bf16[240,256]{1,0:T(8,128)(2,1)} %get-tuple-element.92), channel_id=1, source_target_pairs={{0,3},{1,2},{2,1},{3,0},{4,7},{5,6},{6,5},{7,4},{8,11},{9,10},{10,... | collective-permute-start | bytes 368648 | tf_op jit(solution)/shard_map/ppermute | solution.py:67
  213.0 27.9 %collective-permute-start.28 = (bf16[1024,256]{1,0:T(8,128)(2,1)S(1)}, bf16[1024,256]{1,0:T(8,128)(2,1)}, u32[]{:S(2)}, u32[]{:S(2)}) collective-permute-start(bf16[1024,256]{1,0:T(8,128)(2,1)S(1)} %add_convert_fusion.3), channel_id=1, source_target_pairs={{0,2},{1,3},{2,0},{3,1},{4,6},{5,7},{6,4},{7,5},{8,10},{9,11},{10,... | collective-permute-start | bytes 1572872 | tf_op jit(solution)/shard_map/ppermute | solution.py:67
  213.0 25.2 %collective-permute-start.27 = (bf16[240,1024]{1,0:T(8,128)(2,1)}, bf16[240,1024]{1,0:T(8,128)(2,1)}, u32[]{:S(2)}, u32[]{:S(2)}) collective-permute-start(bf16[240,1024]{1,0:T(8,128)(2,1)} %get-tuple-element.103), channel_id=1, source_target_pairs={{0,1},{1,0},{2,3},{3,2},{4,5},{5,4},{6,7},{7,6},{8,9},{9,8},{10,11... | collective-permute-start | bytes 1474568 | tf_op jit(solution)/shard_map/ppermute | solution.py:67
  214.2 59.9 %collective-permute-start.42 = (bf16[4,240,1024]{2,1,0:T(8,128)(2,1)}, bf16[4,240,1024]{2,1,0:T(8,128)(2,1)}, u32[]{:S(2)}, u32[]{:S(2)}) collective-permute-start(bf16[4,240,1024]{2,1,0:T(8,128)(2,1)} %get-tuple-element.114), channel_id=1, source_target_pairs={{0,4},{4,0},{8,12},{12,8},{16,20},{20,16},{24,28},{28,24},{1,5},{5... | collective-permute-start | bytes 5898248 | tf_op jit(solution)/shard_map/ppermute | solution.py:63
  218.5 24.5 %collective-permute-start.31 = (bf16[136,768]{1,0:T(8,128)(2,1)S(1)}, bf16[136,768]{1,0:T(8,128)(2,1)S(1)}, u32[]{:S(2)}, u32[]{:S(2)}) collective-permute-start(bf16[136,768]{1,0:T(8,128)(2,1)S(1)} %get-tuple-element.148), channel_id=1, source_target_pairs={{0,24},{4,28},{8,16},{12,20},{16,8},{20,12},{24,0},{28,4},{1,25},{... | collective-permute-start | bytes 626696 | tf_op jit(solution)/shard_map/ppermute | solution.py:63
  220.8 22.2 %collective-permute-start.30 = (bf16[136,768]{1,0:T(8,128)(2,1)S(1)}, bf16[136,768]{1,0:T(8,128)(2,1)S(1)}, u32[]{:S(2)}, u32[]{:S(2)}) collective-permute-start(bf16[136,768]{1,0:T(8,128)(2,1)S(1)} %get-tuple-element.149), channel_id=1, source_target_pairs={{0,16},{4,20},{8,24},{12,28},{16,0},{20,4},{24,8},{28,12},{1,17},{... | collective-permute-start | bytes 626696 | tf_op jit(solution)/shard_map/ppermute | solution.py:63
  242.9 24.8 %collective-permute-start.32 = (bf16[240,1024]{1,0:T(8,128)(2,1)S(1)}, bf16[240,1024]{1,0:T(8,128)(2,1)S(1)}, u32[]{:S(2)}, u32[]{:S(2)}) collective-permute-start(bf16[240,1024]{1,0:T(8,128)(2,1)S(1)} %add_convert_fusion.4), channel_id=1, source_target_pairs={{0,2},{1,3},{2,0},{3,1},{4,6},{5,7},{6,4},{7,5},{8,10},{9,11},{10,... | collective-permute-start | bytes 1474568 | tf_op jit(solution)/shard_map/ppermute | solution.py:67
  244.9 14.1 %collective-permute-start.34 = (bf16[136,1024]{1,0:T(8,128)(2,1)S(1)}, bf16[136,1024]{1,0:T(8,128)(2,1)S(1)}, u32[]{:S(2)}, u32[]{:S(2)}) collective-permute-start(bf16[136,1024]{1,0:T(8,128)(2,1)S(1)} %get-tuple-element.135), channel_id=1, source_target_pairs={{0,16},{4,20},{8,24},{12,28},{16,0},{20,4},{24,8},{28,12},{1,17},{... | collective-permute-start | bytes 835592 | tf_op jit(solution)/shard_map/ppermute | solution.py:63
  253.5 26.4 %collective-permute-start.41 = (bf16[240,1024]{1,0:T(8,128)(2,1)S(1)}, bf16[240,1024]{1,0:T(8,128)(2,1)S(1)}, u32[]{:S(2)}, u32[]{:S(2)}) collective-permute-start(bf16[240,1024]{1,0:T(8,128)(2,1)S(1)} %copy-done.47), channel_id=1, source_target_pairs={{0,1},{1,0},{2,3},{3,2},{4,5},{5,4},{6,7},{7,6},{8,9},{9,8},{10,11... | collective-permute-start | bytes 1474568 | tf_op jit(solution)/shard_map/ppermute | solution.py:67
  270.0 22.1 %collective-permute-start.36 = (bf16[136,1792]{1,0:T(8,128)(2,1)}, bf16[136,1792]{1,0:T(8,128)(2,1)S(1)}, u32[]{:S(2)}, u32[]{:S(2)}) collective-permute-start(bf16[136,1792]{1,0:T(8,128)(2,1)} %pad_maximum_fusion.7), channel_id=1, source_target_pairs={{0,2},{1,3},{2,0},{3,1},{4,6},{5,7},{6,4},{7,5},{8,10},{9,11},{10,... | collective-permute-start | bytes 1462280 | tf_op jit(solution)/shard_map/ppermute | solution.py:67
  274.1 25.3 %collective-permute-start.47 = (bf16[8,128,256]{2,1,0:T(8,128)(2,1)S(1)}, bf16[8,128,256]{2,1,0:T(8,128)(2,1)S(1)}, u32[]{:S(2)}, u32[]{:S(2)}) collective-permute-start(bf16[8,128,256]{2,1,0:T(8,128)(2,1)S(1)} %bitcast.203), channel_id=1, source_target_pairs={{0,1},{1,0},{2,3},{3,2},{4,5},{5,4},{6,7},{7,6},{8,9},{9,8},{10,11... | collective-permute-start | bytes 1572872 | tf_op jit(solution)/shard_map/ppermute | solution.py:67
  277.0 26.5 %collective-permute-start.43 = (bf16[240,1024]{1,0:T(8,128)(2,1)}, bf16[240,1024]{1,0:T(8,128)(2,1)S(1)}, u32[]{:S(2)}, u32[]{:S(2)}) collective-permute-start(bf16[240,1024]{1,0:T(8,128)(2,1)} %get-tuple-element.125), channel_id=1, source_target_pairs={{0,8},{4,12},{8,0},{12,4},{16,24},{20,28},{24,16},{28,20},{1,9},{5... | collective-permute-start | bytes 1474568 | tf_op jit(solution)/shard_map/ppermute | solution.py:63
  277.6 26.0 %collective-permute-start.45 = (bf16[240,1024]{1,0:T(8,128)(2,1)S(1)}, bf16[240,1024]{1,0:T(8,128)(2,1)S(1)}, u32[]{:S(2)}, u32[]{:S(2)}) collective-permute-start(bf16[240,1024]{1,0:T(8,128)(2,1)S(1)} %get-tuple-element.126), channel_id=1, source_target_pairs={{0,24},{4,28},{8,16},{12,20},{16,8},{20,12},{24,0},{28,4},{1,25},{... | collective-permute-start | bytes 1474568 | tf_op jit(solution)/shard_map/ppermute | solution.py:63
  279.9 23.6 %collective-permute-start.44 = (bf16[240,1024]{1,0:T(8,128)(2,1)S(1)}, bf16[240,1024]{1,0:T(8,128)(2,1)}, u32[]{:S(2)}, u32[]{:S(2)}) collective-permute-start(bf16[240,1024]{1,0:T(8,128)(2,1)S(1)} %get-tuple-element.127), channel_id=1, source_target_pairs={{0,16},{4,20},{8,24},{12,28},{16,0},{20,4},{24,8},{28,12},{1,17},{... | collective-permute-start | bytes 1474568 | tf_op jit(solution)/shard_map/ppermute | solution.py:63
  292.3 20.7 %collective-permute-start.46 = (bf16[136,2560]{1,0:T(8,128)(2,1)S(1)}, bf16[136,2560]{1,0:T(8,128)(2,1)S(1)}, u32[]{:S(2)}, u32[]{:S(2)}) collective-permute-start(bf16[136,2560]{1,0:T(8,128)(2,1)S(1)} %pad_maximum_fusion.5), channel_id=1, source_target_pairs={{0,1},{1,0},{2,3},{3,2},{4,5},{5,4},{6,7},{7,6},{8,9},{9,8},{10,11... | collective-permute-start | bytes 2088968 | tf_op jit(solution)/shard_map/ppermute | solution.py:67
  (69 other events, 578.3 us)
Sparse Core Ops, SparseCore 0:
  9.7 46.2 all-gather.5
  57.8 26.7 all-gather.3
  143.2 64.4 all-reduce.12
